TPU v7x, 32 devices: a whole 2x2x4 slice. The times are simulated.
32 devices in a mesh: dom: 16 (over z, y, x), rep: 2 (over core).
Axes of the slice: x: 2, y: 2, z: 4, core: 2. Of those that a mesh axis runs over, the one named last changes fastest.
Arguments:
- features: float32 [4, 32768, 100], P('rep', 'dom'), may hold values from -6 to 6
- neighbors: int32 [4, 32768, 16], P('rep', 'dom'), may hold values from 0 to 2175, as said below
- nbr_mask: int32 [4, 32768, 16], P('rep', 'dom'), may hold values 0 or 1
- send_rows: int32 [4, 256, 8], P('rep', 'dom'), may hold values from 0 to 2047
- halo_count: int32 [4, 256], P('rep', 'dom'), may hold values from 1 to 8, as said below
- pos_edges: int32 [4, 4096, 2], P('rep', 'dom'), may hold values from 0 to 2175, as said below
- neg_edges: int32 [4, 4096, 2], P('rep', 'dom'), may hold values from 0 to 2175, as said below
- w_one: float32 [100, 2048], P(None, ('dom', 'rep')), may hold values from -0.625 to 0.625
- b_one: float32 [2048], P(('dom', 'rep')), may hold values from -3 to 3
- w_two: float32 [2048, 47], P(('dom', 'rep')), may hold values from -0.125 to 0.125
- b_two: float32 [47], replicated, may hold values from -2 to 2
- w_one_row: float32 [100], replicated, may hold values from 2.1362305e-06 to 8.544922e-06
- w_one_col: float32 [2048], P(('dom', 'rep')), may hold values from 1.0375977e-07 to 4.1503907e-07
- w_two_row: float32 [2048], P(('dom', 'rep')), may hold values from 1.2207031e-05 to 4.8828126e-05
- w_two_col: float32 [47], replicated, may hold values from 0.0005493164 to 0.0021972656
- b_one_second: float32 [2048], P(('dom', 'rep')), may hold values from 3.051758e-08 to 1.2207032e-07
- b_two_second: float32 [47], replicated, may hold values from 1.0986328e-06 to 4.394531e-06
Outputs:
- loss: float32 [], replicated
- w_one_grad: float32 [100, 2048], P(None, ('dom', 'rep'))
- w_one_new: float32 [100, 2048], P(None, ('dom', 'rep'))
- w_one_row_new: float32 [100], replicated
- w_one_col_new: float32 [2048], P(('dom', 'rep'))
- w_two_grad: float32 [2048, 47], P(('dom', 'rep'))
- w_two_new: float32 [2048, 47], P(('dom', 'rep'))
- w_two_row_new: float32 [2048], P(('dom', 'rep'))
- w_two_col_new: float32 [47], replicated
- b_one_grad: float32 [2048], P(('dom', 'rep'))
- b_one_new: float32 [2048], P(('dom', 'rep'))
- b_one_second_new: float32 [2048], P(('dom', 'rep'))
- b_two_grad: float32 [47], replicated
- b_two_new: float32 [47], replicated
- b_two_second_new: float32 [47], replicated
Inputs may be any that keep to these rules, and one draw needn't show every extreme that they name: `halo_count`: A halo slot index 2048 + s * 8 + j is only used where j is below the count of partition s to this partition; in every micro-batch one reader gets 8 rows from every partition. `neighbors`: indices below 2048 are local nodes, others halo slots. `pos_edges`: the first entry is a local node; the second as in neighbors. `neg_edges`: as pos_edges.
All inputs are finite; a program needn't handle non-finite values. No bound on the sum of `nbr_mask` on one device may be relied on, other than what follows from the above.
Results may differ from a plain program's by a relative error of at most 0.00085.
Values sent between devices are 32-bit elements; how exact they have to be, the bound alone decides.
No kernel may reach another device: no remote copies, remote signals or barrier semaphores. Data moves between devices by JAX's collectives and lax.ppermute only.
A program may use at most 128 MiB of HBM per device.

v0:
```python
import jax
import jax.numpy as jnp
from jax import lax
from jax.sharding import PartitionSpec as P

F = 100
H = 2048
C = 47
HCAP = 8
STEP = 20


tiny_eps = 1e-30
scale_eps = 0.001
clip_limit = 1.0
step_rate = 0.3
highest = lax.Precision.HIGHEST


def contract_rows(left, right):
    return lax.dot_general(left, right, (((0,), (0,)), ((), ())), precision=highest)


def pack_rows(values, sender, valid):
    return values[sender] * valid[..., None]


def slot_valid(counts):
    return (jnp.arange(HCAP)[None, :] < counts[:, None]).astype(jnp.float32)


def local(
    features,
    neighbors,
    nbr_mask,
    send_rows,
    halo_count,
    pos_edges,
    neg_edges,
    w_one,
    b_one,
    w_two,
    b_two,
    w_one_row,
    w_one_col,
    w_two_row,
    w_two_col,
    b_one_second,
    b_two_second,
):
    peers = lax.axis_size("dom")
    micro_count = features.shape[0]
    node_rows = features.shape[1]
    classes = w_two.shape[1]
    total_edges = pos_edges.shape[1] * peers * micro_count * lax.axis_size("rep")
    grad_one = jnp.zeros((F, H), jnp.float32)
    grad_bias = jnp.zeros((H,), jnp.float32)
    grad_two = jnp.zeros((H, classes), jnp.float32)
    grad_head = jnp.zeros((classes,), jnp.float32)
    local_loss = jnp.float32(0.0)
    for micro in range(micro_count):
        whole = (
            lax.all_gather(w_one, ("dom", "rep"), axis=1, tiled=True),
            lax.all_gather(b_one, ("dom", "rep"), axis=0, tiled=True),
            lax.all_gather(w_two, ("dom", "rep"), axis=0, tiled=True),
        )
        full_one, full_bias, full_two = whole
        sender = send_rows[micro]
        valid = slot_valid(halo_count[micro])
        inputs = features[micro]
        arrived = lax.all_to_all(
            pack_rows(inputs, sender, valid), "dom", split_axis=0, concat_axis=0, tiled=True
        )
        buffer_x = jnp.concatenate([inputs, arrived.reshape(-1, inputs.shape[1])], axis=0)
        weight_mask = nbr_mask[micro].astype(jnp.float32)
        summed = jnp.sum(buffer_x[neighbors[micro]] * weight_mask[..., None], axis=1)
        degree = 1.0 + jnp.sum(weight_mask, axis=1)
        agg = (inputs + summed) / degree[:, None]
        pre = jnp.dot(agg, full_one, precision=highest) + full_bias
        hidden = jnp.maximum(pre, 0.0)
        outputs = jnp.dot(hidden, full_two, precision=highest) + b_two
        arrived_z = lax.all_to_all(
            pack_rows(outputs, sender, valid), "dom", split_axis=0, concat_axis=0, tiled=True
        )
        buffer_z = jnp.concatenate([outputs, arrived_z.reshape(-1, classes)], axis=0)
        grad_buffer = jnp.zeros(buffer_z.shape, jnp.float32)
        grad_out = jnp.zeros(outputs.shape, jnp.float32)
        for edges, sign in ((pos_edges[micro], -1.0), (neg_edges[micro], 1.0)):
            start_rows = outputs[edges[:, 0]]
            end_rows = buffer_z[edges[:, 1]]
            score = jnp.sum(start_rows * end_rows, axis=-1)
            local_loss = local_loss + jnp.sum(jax.nn.softplus(sign * score))
            slope = sign * jax.nn.sigmoid(sign * score) / (2.0 * total_edges)
            grad_out = grad_out.at[edges[:, 0]].add(slope[:, None] * end_rows)
            grad_buffer = grad_buffer.at[edges[:, 1]].add(slope[:, None] * start_rows)
        returned = lax.all_to_all(
            grad_buffer[node_rows:].reshape(peers, HCAP, classes),
            "dom",
            split_axis=0,
            concat_axis=0,
            tiled=True,
        )
        grad_out = grad_out + grad_buffer[:node_rows]
        grad_out = grad_out.at[sender.reshape(-1)].add(
            (returned * valid[..., None]).reshape(-1, classes)
        )
        grad_two = grad_two + contract_rows(hidden, grad_out)
        grad_head = grad_head + jnp.sum(grad_out, axis=0)
        grad_pre = lax.dot_general(
            grad_out, full_two, (((1,), (1,)), ((), ())), precision=highest
        ) * (pre > 0.0).astype(jnp.float32)
        grad_one = grad_one + contract_rows(agg, grad_pre)
        grad_bias = grad_bias + jnp.sum(grad_pre, axis=0)
    g_one, gb_one, g_two = (
        lax.psum_scatter(grad_one, ("dom", "rep"), scatter_dimension=1, tiled=True),
        lax.psum_scatter(grad_bias, ("dom", "rep"), scatter_dimension=0, tiled=True),
        lax.psum_scatter(grad_two, ("dom", "rep"), scatter_dimension=0, tiled=True),
    )
    decay = 1.0 - jnp.float32(STEP) ** (-0.8)
    row_part = jnp.sum(g_one * g_one + tiny_eps, axis=1)
    col_one = decay * w_one_col + (1.0 - decay) * jnp.sum(g_one * g_one + tiny_eps, axis=0)
    row_two = decay * w_two_row + (1.0 - decay) * jnp.sum(g_two * g_two + tiny_eps, axis=1)
    col_part = jnp.sum(g_two * g_two + tiny_eps, axis=0)
    second_one = decay * b_one_second + (1.0 - decay) * (gb_one * gb_one + tiny_eps)
    square_one = jnp.sum(w_one * w_one)
    square_two = jnp.sum(w_two * w_two)
    square_bias = jnp.sum(b_one * b_one)
    loss_total = lax.psum(local_loss, ("dom", "rep"))
    sums = lax.psum(
        (row_part, col_part, jnp.sum(row_two), grad_head, square_one, square_two, square_bias),
        ("dom", "rep"),
    )
    row_sum, col_sum, row_two_total, gb_two, total_one, total_two, total_bias = sums[:7]
    loss = loss_total / (2.0 * total_edges)
    row_one = decay * w_one_row + (1.0 - decay) * row_sum
    col_two = decay * w_two_col + (1.0 - decay) * col_sum
    second_two = decay * b_two_second + (1.0 - decay) * (gb_two * gb_two + tiny_eps)
    step_one = g_one * lax.rsqrt(jnp.outer(row_one, col_one) / jnp.sum(row_one))
    step_two = g_two * lax.rsqrt(jnp.outer(row_two, col_two) / row_two_total)
    step_bias = gb_one * lax.rsqrt(second_one)
    step_head = gb_two * lax.rsqrt(second_two)
    rms_one, rms_two, rms_bias = lax.psum(
        (
            jnp.sum(step_one * step_one),
            jnp.sum(step_two * step_two),
            jnp.sum(step_bias * step_bias),
        ),
        ("dom", "rep"),
    )
    step_one = step_one / jnp.maximum(1.0, jnp.sqrt(rms_one / (F * H)) / clip_limit)
    step_two = step_two / jnp.maximum(1.0, jnp.sqrt(rms_two / (H * C)) / clip_limit)
    step_bias = step_bias / jnp.maximum(1.0, jnp.sqrt(rms_bias / H) / clip_limit)
    step_head = step_head / jnp.maximum(1.0, jnp.sqrt(jnp.mean(step_head * step_head)) / clip_limit)
    w_one_new = w_one - step_rate * jnp.maximum(scale_eps, jnp.sqrt(total_one / (F * H))) * step_one
    w_two_new = w_two - step_rate * jnp.maximum(scale_eps, jnp.sqrt(total_two / (H * C))) * step_two
    b_one_new = b_one - step_rate * jnp.maximum(scale_eps, jnp.sqrt(total_bias / H)) * step_bias
    b_two_new = (
        b_two - step_rate * jnp.maximum(scale_eps, jnp.sqrt(jnp.mean(b_two * b_two))) * step_head
    )
    return (
        loss,
        g_one,
        w_one_new,
        row_one,
        col_one,
        g_two,
        w_two_new,
        row_two,
        col_two,
        gb_one,
        b_one_new,
        second_one,
        gb_two,
        b_two_new,
        second_two,
    )


def solution(mesh):
    return jax.shard_map(
        local,
        mesh=mesh,
        in_specs=(
            P("rep", "dom", None),
            P("rep", "dom", None),
            P("rep", "dom", None),
            P("rep", "dom", None),
            P("rep", "dom"),
            P("rep", "dom", None),
            P("rep", "dom", None),
            P(None, ("dom", "rep")),
            P(("dom", "rep")),
            P(("dom", "rep"), None),
            P(),
            P(),
            P(("dom", "rep")),
            P(("dom", "rep")),
            P(),
            P(("dom", "rep")),
            P(),
        ),
        out_specs=(
            P(),
            P(None, ("dom", "rep")),
            P(None, ("dom", "rep")),
            P(),
            P(("dom", "rep")),
            P(("dom", "rep"), None),
            P(("dom", "rep"), None),
            P(("dom", "rep")),
            P(),
            P(("dom", "rep")),
            P(("dom", "rep")),
            P(("dom", "rep")),
            P(),
            P(),
            P(),
        ),
        check_vma=False,
    )
```

profile of v0, /device:TPU:0, one launch (start us, length us, event | category | flops | bytes accessed | tf_op | source)
XLA Modules:
  0.0 1086.3 jit_solution(14681531400470478647)
XLA Ops:
  8.9 3.7 fusion.84
  15.2 8.3 all-to-all-start
  33.5 40.6 %all-reduce = f32[2048]{0:T(1024)S(1)} all-reduce(f32[2048]{0:T(1024)S(1)} %dynamic-update-slice), channel_id=1, replica_groups=mesh['dom'=16,'rep'=2] {'dom','rep'}, use_global_device_ids=true, to_apply=%add | all-reduce | flops 2048 | bytes 16384
  76.2 1.6 compare_select_fusion.2
  77.9 42.8 %all-gather = f32[32,64,47]{1,2,0:T(8,128)S(1)} all-gather(f32[1,64,47]{1,2,0:T(8,128)} %bitcast.102), channel_id=1, replica_groups=mesh['dom'=16,'rep'=2] {'dom','rep'}, dimensions={0}, use_global_device_ids=true | all-gather | bytes 397056 | tf_op jit(solution)/shard_map/all_gather | solution.py:65
  122.0 1.3 copy.89
  124.0 42.4 %all_gather.12 = f32[100,2048]{0,1:T(8,128)} all-gather(f32[100,64]{0,1:T(8,128)} %param.24), channel_id=1, replica_groups=mesh['dom'=16,'rep'=2] {'dom','rep'}, dimensions={1}, use_global_device_ids=true | all-gather | bytes 844800 | tf_op jit(solution)/shard_map/all_gather | solution.py:63
  173.1 3.5 all-to-all-start.2
  177.6 6.6 all-to-all-done.2
  184.8 1.3 pad_maximum_fusion.1
  186.1 108.2 %gather_fusion.1 = f32[32768,100]{1,0:T(8,128)} fusion(f32[2176,100]{1,0:T(8,128)S(1)} %pad_maximum_fusion, s32[32768]{0:T(1024)S(1)} %broadcast_clamp_fusion.1), kind=kCustom, calls=%fused_computation.1 | custom fusion | bytes 26345472 | tf_op jit(solution)/shard_map/gather | solution.py:76
  294.3 13.2 %multiply_reduce_fusion.1 = f32[2048,100]{1,0:T(8,128)S(1)} fusion(f32[2048,16]{1,0:T(8,128)} %copy.78, f32[32768,100]{1,0:T(8,128)} %gather_fusion.1), kind=kLoop, calls=%fused_computation.25 | loop fusion | flops 6348800 | bytes 14057472 | tf_op jit(solution)/shard_map/reduce_sum | solution.py:76
  307.6 14.6 %fusion.80 = f32[2048,2048]{1,0:T(8,128)S(1)} fusion(f32[100,2048]{0,1:T(8,128)S(1)} %copy-done.10, f32[2048,100]{1,0:T(8,128)S(1)} %multiply_reduce_fusion.1, f32[2048]{0:T(1024)S(1)} %copy-done.19, f32[1,2048,100]{2,1,0:T(8,128)S(1)} %copy.100), kind=kOutput, calls=%fused_computation.191 | convolution fusion | flops 5033574400 | bytes 19243008 | tf_op jit(solution)/shard_map/dot_general | solution.py:79
  322.2 5.7 copy-done
  327.9 17.9 %fusion.23 = f32[2048,47]{0,1:T(8,128)} fusion(f32[2048,47]{0,1:T(8,128)S(1)} %copy-done.8, f32[2048,2048]{1,0:T(8,128)S(1)} %fusion.80, f32[2048]{0:T(1024)S(1)} %all-reduce, f32[47]{0:T(128)S(1)} %copy-done.30), kind=kOutput, calls=%fused_computation.50 | convolution fusion | flops 2374072320 | bytes 17555644 | tf_op jit(solution)/shard_map/dot_general | solution.py:81
  345.8 1.3 copy.80
  348.6 4.1 all-to-all-start.1
  352.8 108.2 %gather_fusion.8 = f32[32768,100]{1,0:T(8,128)} fusion(f32[2176,100]{1,0:T(8,128)S(1)} %pad_maximum_fusion.1, s32[32768]{0:T(1024)S(1)} %broadcast_clamp_fusion), kind=kCustom, calls=%fused_computation.8 | custom fusion | bytes 26345472 | tf_op jit(solution)/shard_map/gather | solution.py:76
  461.0 13.0 %multiply_reduce_fusion = f32[2048,100]{1,0:T(8,128)S(1)} fusion(f32[2048,16]{1,0:T(8,128)} %copy.89, f32[32768,100]{1,0:T(8,128)} %gather_fusion.8), kind=kLoop, calls=%fused_computation.24 | loop fusion | flops 6348800 | bytes 14057472 | tf_op jit(solution)/shard_map/reduce_sum | solution.py:76
  475.0 14.6 %fusion.81 = f32[2048,2048]{1,0:T(8,128)S(1)} fusion(f32[100,2048]{0,1:T(8,128)S(1)} %copy-done.11, f32[2048,100]{1,0:T(8,128)S(1)} %multiply_reduce_fusion, f32[2048]{0:T(1024)S(1)} %broadcast_add_fusion, f32[1,2048,100]{2,1,0:T(8,128)S(1)} %copy-done.3), kind=kOutput, calls=%fused_computation.192 | convolution fusion | flops 5033574400 | bytes 19243008 | tf_op jit(solution)/shard_map/dot_general | solution.py:79
  489.7 5.7 copy-done.1
  495.4 17.9 %fusion.26 = f32[2048,47]{0,1:T(8,128)} fusion(f32[2048,47]{0,1:T(8,128)S(1)} %copy-done.9, f32[2048,2048]{1,0:T(8,128)S(1)} %fusion.81, f32[2048]{0:T(1024)S(1)} %all-reduce, f32[47]{0:T(128)S(1)} %copy-done.30), kind=kOutput, calls=%fused_computation.51 | convolution fusion | flops 2374072320 | bytes 17555644 | tf_op jit(solution)/shard_map/dot_general | solution.py:81
  513.3 2.3 copy.90
  515.6 1.9 gather_fusion.10
  518.4 1.5 gather_fusion.2
  520.6 2.1 gather_fusion.12
  522.7 2.7 gather_fusion.9
  525.4 6.8 all-to-all-start.3
  532.7 1.4 reduce.2
  534.3 1.8 pad_maximum_fusion.2
  536.2 1.4 copy.83
  537.6 1.5 gather_fusion.6
  539.0 1.5 gather_fusion.4
  544.4 2.9 scatter_custom_fusion
  548.2 1.8 pad_maximum_fusion.3
  550.0 1.4 copy.93
  551.4 1.5 gather_fusion.13
  552.9 1.5 gather_fusion.11
  557.7 2.2 scatter_custom_fusion.5
  559.9 2.6 scatter_custom_fusion.6
  563.4 6.9 all-to-all-start.5
  570.3 4.2 scatter_custom_fusion.1
  575.4 2.3 slice.148
  579.0 4.4 scatter_custom_fusion.2
  583.4 4.6 scatter_custom_fusion.3
  588.7 2.8 scatter_custom_fusion.7
  591.5 2.8 scatter_custom_fusion.8
  594.3 6.9 all-to-all-start.4
  602.1 1.9 scatter_custom_fusion.9
  604.0 19.1 %fusion.87 = (f32[2048]{0:T(1024)S(1)}, f32[2048,2048]{1,0:T(8,128)}) fusion(f32[2048,47]{1,0:T(8,128)S(1)} %scatter_custom_fusion.9, f32[2048,47]{0,1:T(8,128)} %reshape.535, f32[2048,2048]{1,0:T(8,128)} %copy-done.1, f32[2048]{0:T(1024)S(1)} %all-reduce), kind=kOutput, calls=%fused_computation.198 | convolution fusion | flops 2382362624 | bytes 34340864 | tf_op jit(solution)/shard_map/dot_general | solution.py:109
  623.1 15.9 %fusion = f32[2048,47]{0,1:T(8,128)} fusion(f32[2048,47]{1,0:T(8,128)S(1)} %scatter_custom_fusion.9, f32[2048,2048]{1,0:T(8,128)} %copy-done.1, f32[2048]{0:T(1024)S(1)} %all-reduce), kind=kOutput, calls=%fused_computation.28 | convolution fusion | flops 2373976064 | bytes 17555456 | tf_op jit(solution)/shard_map/dot_general | solution.py:21
  639.9 3.5 scatter_custom_fusion.4
  643.4 18.7 %fusion.86 = (f32[2048]{0:T(1024)S(1)}, f32[2048,2048]{1,0:T(8,128)S(1)}) fusion(f32[2048,47]{1,0:T(8,128)} %scatter_custom_fusion.4, f32[2048,47]{0,1:T(8,128)} %reshape.535, f32[2048,2048]{1,0:T(8,128)} %copy-done, f32[2048]{0:T(1024)S(1)} %all-reduce), kind=kOutput, calls=%fused_computation.197 | convolution fusion | flops 2382362624 | bytes 34340864 | tf_op jit(solution)/shard_map/dot_general | solution.py:109
  662.1 16.1 %fusion.20 = f32[2048,47]{0,1:T(8,128)} fusion(f32[2048,47]{0,1:T(8,128)S(1)} %copy-done.13, f32[2048,47]{1,0:T(8,128)} %scatter_custom_fusion.4, f32[2048,2048]{1,0:T(8,128)} %copy-done, f32[2048]{0:T(1024)S(1)} %all-reduce), kind=kOutput, calls=%fused_computation.49 | convolution fusion | flops 2374072320 | bytes 17940480 | tf_op jit(solution)/shard_map/dot_general | solution.py:21
  678.2 28.8 %fusion.79 = f32[100,2048]{0,1:T(8,128)} fusion(f32[2048,2048]{1,0:T(8,128)S(1)} %get-tuple-element.75, f32[2048,100]{1,0:T(8,128)S(1)} %copy-done.6, f32[2048]{0:T(1024)S(1)} %copy-done.20, f32[1,2048,100]{2,1,0:T(8,128)S(1)} %copy.100), kind=kOutput, calls=%fused_computation.190 | convolution fusion | flops 5033574400 | bytes 19243008 | tf_op jit(solution)/shard_map/dot_general | solution.py:21
  707.2 2.4 copy.98
  709.7 31.3 %convolution_add_fusion = f32[100,2048]{0,1:T(8,128)} fusion(f32[100,2048]{0,1:T(8,128)} %fusion.79, f32[2048,2048]{1,0:T(8,128)} %get-tuple-element.77, f32[2048,100]{1,0:T(8,128)} %copy-done.7, f32[2048]{0:T(1024)S(1)} %broadcast_add_fusion, f32[1,2048,100]{2,1,0:T(8,128)S(1)} %copy-done.3), kind=kOutput, calls=%fused_computation.48 | convolution fusion | flops 5033779200 | bytes 20062208 | tf_op jit(solution)/shard_map/dot_general | solution.py:21
  747.3 100.3 %reduce-scatter.7.cloned.1.call-done = f32[64,47]{1,0:T(8,128)} async-done(((f32[2048,47]{1,0:T(8,128)}), f32[64,47]{1,0:T(8,128)}) %reduce-scatter.7.cloned.1.call-update) | async-done | bytes 12048
  849.2 133.6 %reduce-scatter.5.cloned.1.call-done = f32[100,64]{0,1:T(8,128)} async-done(((f32[100,2048]{0,1:T(8,128)}), f32[100,64]{0,1:T(8,128)}) %reduce-scatter.5.cloned.1.call-update) | async-done | bytes 25616 | tf_op jit(solution)/shard_map/reduce_scatter | solution.py:115
  983.8 37.0 %all-reduce.3 = (f32[100]{0:T(128)S(1)}, f32[]{:T(128)}, f32[47]{0:T(128)S(1)}, f32[2048]{0:T(1024)S(1)}) all-reduce(f32[100]{0:T(128)S(1)} %get-tuple-element.18, f32[]{:T(128)} %get-tuple-element.40, f32[47]{0:T(128)S(1)} %get-tuple-element.19, f32[2048]{0:T(1024)S(1)} %add.347), channel_id=1, replica_groups=mesh['dom'=16,'rep'=2] {'dom','rep'}, use_global_device_ids=true, to_apply=%region_27.28 | all-reduce | flops 2196 | bytes 17568 | tf_op jit(solution)/shard_map/psum | solution.py:129
  1023.5 2.1 multiply_reduce_fusion.6
  1025.7 41.8 %all-reduce.2 = (f32[]{:T(128)}, f32[]{:T(128)}, f32[]{:T(128)}, f32[]{:T(128)}, f32[]{:T(128)}, /*index=5*/f32[]{:T(128)}, f32[]{:T(128)}, f32[47]{0:T(128)S(1)}) all-reduce(f32[]{:T(128)S(6)} %add.332, f32[]{:T(128)} %multiply_reduce_fusion.6, f32[]{:T(128)} %multiply_reduce_fusion.7, ...), channel_id=1, replica_groups=mesh['dom'=16,'rep'=2] {'dom','rep'}, use_global_device_ids=true, to_apply=%region_12.13 | all-reduce | flops 54 | bytes 432 | tf_op jit(solution)/shard_map/psum | solution.py:128
  1073.5 1.3 multiply_subtract_fusion.1
  1075.9 2.1 multiply_subtract_fusion
  (221 shorter events, 54.7 us)
Async XLA Ops:
  8.0 115.3 %copy-start.21 = (f32[16,8]{1,0:T(8,128)}, f32[16,8]{1,0:T(8,128)S(1)}, u32[]{:S(2)}) copy-start(f32[16,8]{1,0:T(8,128)S(1)} %fusion.67) | copy-start | bytes 1540
  8.9 114.4 %copy-start.26 = (s32[1024]{0:T(1024)}, s32[1024]{0:T(1024)S(1)}, u32[]{:S(2)}) copy-start(s32[1024]{0:T(1024)S(1)} %pad_clamp_fusion.9) | copy-start | bytes 12292
  15.2 157.9 %all-to-all-start = ((f32[16,8,100]{2,1,0:T(8,128)}), f32[16,8,100]{2,1,0:T(8,128)S(1)}, u32[]{:S(2)}, u32[]{:S(2)}) async-start(f32[16,8,100]{2,1,0:T(8,128)} %bitcast_multiply_fusion.3), calls=%async_computation | async-start | bytes 131072 | tf_op jit(solution)/shard_map/all_to_all | solution.py:71
  27.0 3.1 copy-start.41
  27.0 3.1 copy-start.43
  27.0 5.5 copy-start.37
  27.0 5.5 copy-start.38
  30.7 92.6 %copy-start.39 = (s32[256,1]{0,1:T(1,128)}, s32[256,1]{0,1:T(1,128)S(1)}, u32[]{:S(2)}) copy-start(s32[256,1]{0,1:T(1,128)S(1)} %get-tuple-element.57) | copy-start | bytes 3076
  30.7 92.6 %copy-start.40 = (s32[256,1]{0,1:T(1,128)}, s32[256,1]{0,1:T(1,128)S(1)}, u32[]{:S(2)}) copy-start(s32[256,1]{0,1:T(1,128)S(1)} %get-tuple-element.80) | copy-start | bytes 3076
  30.7 92.6 %copy-start.42 = (s32[256,1]{0,1:T(1,128)}, s32[256,1]{0,1:T(1,128)S(1)}, u32[]{:S(2)}) copy-start(s32[256,1]{0,1:T(1,128)S(1)} %get-tuple-element.56) | copy-start | bytes 3076
  32.6 144.1 %copy-start.24 = (f32[16,8]{1,0:T(8,128)}, f32[16,8]{1,0:T(8,128)S(1)}, u32[]{:S(2)}) copy-start(f32[16,8]{1,0:T(8,128)S(1)} %fusion.68) | copy-start | bytes 1540
  75.6 101.1 %copy-start.28 = (s32[1024]{0:T(1024)}, s32[1024]{0:T(1024)S(1)}, u32[]{:S(2)}) copy-start(s32[1024]{0:T(1024)S(1)} %pad_clamp_fusion.4) | copy-start | bytes 12292
  170.5 13.6 %copy-start.2 = (f32[1,2048,100]{2,1,0:T(8,128)}, f32[1,2048,100]{2,1,0:T(8,128)S(1)}, u32[]{:S(2)}) copy-start(f32[1,2048,100]{2,1,0:T(8,128)S(1)} %copy.101) | copy-start | bytes 2457604
  173.1 3.5 copy-start.16
  173.1 11.0 %all-to-all-start.2 = ((f32[16,8,100]{2,1,0:T(8,128)}), f32[16,8,100]{2,1,0:T(8,128)S(1)}, u32[]{:S(2)}, u32[]{:S(2)}) async-start(f32[16,8,100]{2,1,0:T(8,128)} %bitcast_multiply_fusion.1), calls=%async_computation.2 | async-start | bytes 131072 | tf_op jit(solution)/shard_map/all_to_all | solution.py:71
  294.3 13.2 %copy-start.10 = (f32[100,2048]{0,1:T(8,128)S(1)}, f32[100,2048]{0,1:T(8,128)}, u32[]{:S(2)}) copy-start(f32[100,2048]{0,1:T(8,128)} %all_gather.12) | copy-start | bytes 2457604
  294.3 13.2 %copy-start.19 = (f32[2048]{0:T(1024)S(1)}, f32[2048]{0:T(1024)}, u32[]{:S(2)}) copy-start(f32[2048]{0:T(1024)} %broadcast_add_fusion.1) | copy-start | bytes 24580
  294.3 33.6 %copy-start.8 = (f32[2048,47]{0,1:T(8,128)S(1)}, f32[2048,47]{0,1:T(8,128)}, u32[]{:S(2)}) copy-start(f32[2048,47]{0,1:T(8,128)} %reshape.535) | copy-start | bytes 1155076
  294.3 33.6 %copy-start.30 = (f32[47]{0:T(128)S(1)}, f32[47]{0:T(128)}, u32[]{:S(2)}) copy-start(f32[47]{0:T(128)} %param.27) | copy-start | bytes 568
  307.6 14.6 %copy-start.5 = (f32[2048,100]{1,0:T(8,128)}, f32[2048,100]{1,0:T(8,128)S(1)}, u32[]{:S(2)}) copy-start(f32[2048,100]{1,0:T(8,128)S(1)} %multiply_reduce_fusion.1) | copy-start | bytes 2457604
  322.2 5.7 copy-start
  327.9 19.3 %copy-start.27 = (s32[1024]{0:T(1024)S(1)}, s32[1024]{0:T(1024)}, u32[]{:S(2)}) copy-start(s32[1024]{0:T(1024)} %copy-done.26) | copy-start | bytes 12292
  327.9 19.9 %copy-start.22 = (f32[16,8]{1,0:T(8,128)S(1)}, f32[16,8]{1,0:T(8,128)}, u32[]{:S(2)}) copy-start(f32[16,8]{1,0:T(8,128)} %copy-done.21) | copy-start | bytes 1540
  348.6 176.7 %all-to-all-start.1 = ((f32[16,1,376]{2,1,0:T(1,128)}), f32[16,1,376]{2,1,0:T(1,128)}, u32[]{:S(2)}, u32[]{:S(2)}) async-start(f32[16,1,376]{2,1,0:T(1,128)} %reshape.558), calls=%async_computation.1 | async-start | bytes 49152 | tf_op jit(solution)/shard_map/all_to_all | solution.py:82
  461.0 14.0 %copy-start.3 = (f32[1,2048,100]{2,1,0:T(8,128)S(1)}, f32[1,2048,100]{2,1,0:T(8,128)}, u32[]{:S(2)}) copy-start(f32[1,2048,100]{2,1,0:T(8,128)} %copy-done.2) | copy-start | bytes 2457604
  461.0 14.0 %copy-start.11 = (f32[100,2048]{0,1:T(8,128)S(1)}, f32[100,2048]{0,1:T(8,128)}, u32[]{:S(2)}) copy-start(f32[100,2048]{0,1:T(8,128)} %all_gather.12) | copy-start | bytes 2457604
  461.0 34.4 %copy-start.9 = (f32[2048,47]{0,1:T(8,128)S(1)}, f32[2048,47]{0,1:T(8,128)}, u32[]{:S(2)}) copy-start(f32[2048,47]{0,1:T(8,128)} %reshape.535) | copy-start | bytes 1155076
  474.0 1.0 copy-start.7
  489.7 5.7 copy-start.1
  495.4 20.2 %copy-start.29 = (s32[1024]{0:T(1024)S(1)}, s32[1024]{0:T(1024)}, u32[]{:S(2)}) copy-start(s32[1024]{0:T(1024)} %copy-done.28) | copy-start | bytes 12292
  495.4 22.1 %copy-start.25 = (f32[16,8]{1,0:T(8,128)S(1)}, f32[16,8]{1,0:T(8,128)}, u32[]{:S(2)}) copy-start(f32[16,8]{1,0:T(8,128)} %copy-done.24) | copy-start | bytes 1540
  525.4 21.9 %all-to-all-start.3 = ((f32[16,1,376]{2,1,0:T(1,128)}), f32[16,1,376]{2,1,0:T(1,128)S(1)}, u32[]{:S(2)}, u32[]{:S(2)}) async-start(f32[16,1,376]{2,1,0:T(1,128)} %reshape.560), calls=%async_computation.3 | async-start | bytes 49152 | tf_op jit(solution)/shard_map/all_to_all | solution.py:82
  542.2 5.1 copy-start.32
  556.1 3.8 copy-start.33
  557.7 2.2 copy-start.34
  562.5 12.9 %copy-start.12 = (f32[2176,47]{1,0:T(8,128)}, f32[2176,47]{1,0:T(8,128)S(1)}, u32[]{:S(2)}) copy-start(f32[2176,47]{1,0:T(8,128)S(1)} %scatter_custom_fusion.6) | copy-start | bytes 1227268
  563.4 30.9 %all-to-all-start.5 = ((f32[16,1,376]{2,1,0:T(1,128)}), f32[16,1,376]{2,1,0:T(1,128)S(1)}, u32[]{:S(2)}, u32[]{:S(2)}) async-start(f32[16,1,376]{2,1,0:T(1,128)} %reshape.564), calls=%async_computation.5 | async-start | bytes 49152 | tf_op jit(solution)/shard_map/all_to_all | solution.py:96
  594.3 44.7 %all-to-all-start.4 = ((f32[16,1,376]{2,1,0:T(1,128)}), f32[16,1,376]{2,1,0:T(1,128)S(1)}, u32[]{:S(2)}, u32[]{:S(2)}) async-start(f32[16,1,376]{2,1,0:T(1,128)} %reshape.562), calls=%async_computation.4 | async-start | bytes 49152 | tf_op jit(solution)/shard_map/all_to_all | solution.py:96
  601.2 246.4 %reduce-scatter.7.cloned.1.call-start = ((), (), s32[]{:S(2)}) async-start(), calls=%async_computation.9 | async-start | bytes 1081344
  623.1 16.7 %copy-start.23 = (f32[16,8]{1,0:T(8,128)S(1)}, f32[16,8]{1,0:T(8,128)}, u32[]{:S(2)}) copy-start(f32[16,8]{1,0:T(8,128)} %copy-done.21) | copy-start | bytes 1540
  643.4 18.7 %copy-start.13 = (f32[2048,47]{0,1:T(8,128)S(1)}, f32[2048,47]{0,1:T(8,128)}, u32[]{:S(2)}) copy-start(f32[2048,47]{0,1:T(8,128)} %fusion) | copy-start | bytes 1155076
  662.1 16.1 %copy-start.6 = (f32[2048,100]{1,0:T(8,128)S(1)}, f32[2048,100]{1,0:T(8,128)}, u32[]{:S(2)}) copy-start(f32[2048,100]{1,0:T(8,128)} %copy-done.5) | copy-start | bytes 2457604
  662.1 16.1 %copy-start.20 = (f32[2048]{0:T(1024)S(1)}, f32[2048]{0:T(1024)}, u32[]{:S(2)}) copy-start(f32[2048]{0:T(1024)} %broadcast_add_fusion.1) | copy-start | bytes 24580
  707.0 33.9 %copy-start.31 = (f32[47]{0:T(128)S(1)}, f32[47]{0:T(128)}, u32[]{:S(2)}) copy-start(f32[47]{0:T(128)} %param.27) | copy-start | bytes 568
  707.0 35.2 %copy-start.54 = (f32[64]{0:T(128)S(1)}, f32[64]{0:T(128)}, u32[]{:S(2)}) copy-start(f32[64]{0:T(128)} %param.25) | copy-start | bytes 772
  707.1 35.8 %copy-start.18 = (f32[64,47]{0,1:T(8,128)S(1)}, f32[64,47]{0,1:T(8,128)}, u32[]{:S(2)}) copy-start(f32[64,47]{0,1:T(8,128)} %param.26) | copy-start | bytes 36100
  707.1 36.4 %copy-start.15 = (f32[100,64]{0,1:T(8,128)S(1)}, f32[100,64]{0,1:T(8,128)}, u32[]{:S(2)}) copy-start(f32[100,64]{0,1:T(8,128)} %param.24) | copy-start | bytes 76804
  707.1 39.6 %copy-start.4 = (f32[2048,47]{1,0:T(8,128)S(1)}, f32[2048,47]{1,0:T(8,128)}, u32[]{:S(2)}) copy-start(f32[2048,47]{1,0:T(8,128)} %scatter_custom_fusion.4) | copy-start | bytes 1155076
  707.1 141.5 %copy-start.50 = (f32[64]{0:T(128)S(1)}, f32[64]{0:T(128)}, u32[]{:S(2)}) copy-start(f32[64]{0:T(128)} %param.30) | copy-start | bytes 772
  707.1 276.6 %copy-start.55 = (f32[64]{0:T(128)S(1)}, f32[64]{0:T(128)}, u32[]{:S(2)}) copy-start(f32[64]{0:T(128)} %param.29) | copy-start | bytes 772
  707.1 313.7 %copy-start.56 = (f32[47]{0:T(128)S(1)}, f32[47]{0:T(128)}, u32[]{:S(2)}) copy-start(f32[47]{0:T(128)} %param.31) | copy-start | bytes 568
  707.1 313.7 %copy-start.51 = (f32[100]{0:T(128)S(1)}, f32[100]{0:T(128)}, u32[]{:S(2)}) copy-start(f32[100]{0:T(128)} %param.28) | copy-start | bytes 1204
  707.1 315.7 %copy-start.52 = (f32[64]{0:T(128)S(1)}, f32[64]{0:T(128)}, u32[]{:S(2)}) copy-start(f32[64]{0:T(128)} %param.32) | copy-start | bytes 772
  707.1 364.5 %copy-start.53 = (f32[47]{0:T(128)S(1)}, f32[47]{0:T(128)}, u32[]{:S(2)}) copy-start(f32[47]{0:T(128)} %param.33) | copy-start | bytes 568
  709.6 273.2 %reduce-scatter.5.cloned.1.call-start = ((), (), s32[]{:S(2)}) async-start(), calls=%async_computation.8 | async-start | bytes 1081344 | tf_op jit(solution)/shard_map/reduce_scatter | solution.py:115
  848.5 229.6 %copy-start.14 = (f32[64,47]{0,1:T(8,128)}, f32[64,47]{0,1:T(8,128)S(1)}, u32[]{:S(2)}) copy-start(f32[64,47]{0,1:T(8,128)S(1)} %copy.99) | copy-start | bytes 36100
  849.2 228.8 %copy-start.36 = (f32[64]{0:T(128)}, f32[64]{0:T(128)S(1)}, u32[]{:S(2)}) copy-start(f32[64]{0:T(128)S(1)} %get-tuple-element.41) | copy-start | bytes 772
  983.7 94.3 %copy-start.44 = (f32[64]{0:T(128)}, f32[64]{0:T(128)S(1)}, u32[]{:S(2)}) copy-start(f32[64]{0:T(128)S(1)} %multiply_add_fusion.6) | copy-start | bytes 772
  1020.8 57.2 %copy-start.45 = (f32[47]{0:T(128)}, f32[47]{0:T(128)S(1)}, u32[]{:S(2)}) copy-start(f32[47]{0:T(128)S(1)} %multiply_add_fusion.4) | copy-start | bytes 568
  1021.5 56.5 %copy-start.35 = (f32[100]{0:T(128)}, f32[100]{0:T(128)S(1)}, u32[]{:S(2)}) copy-start(f32[100]{0:T(128)S(1)} %get-tuple-element.39) | copy-start | bytes 1204
  1023.5 54.5 %copy-start.46 = (f32[64]{0:T(128)}, f32[64]{0:T(128)S(1)}, u32[]{:S(2)}) copy-start(f32[64]{0:T(128)S(1)} %get-tuple-element.36) | copy-start | bytes 772
  1023.5 54.5 %copy-start.47 = (f32[64]{0:T(128)}, f32[64]{0:T(128)S(1)}, u32[]{:S(2)}) copy-start(f32[64]{0:T(128)S(1)} %get-tuple-element.37) | copy-start | bytes 772
  1067.5 10.6 copy-start.48
  1072.2 5.9 copy-start.49
  (1 other events, 0.6 us)
Sparse Core Ops, SparseCore 0:
  709.7 137.8 reduce-scatter.6
  850.4 132.3 reduce-scatter.4
where the time goes:
time: 1100 us; the launch traced here: 1090 us
  local copies, waits for them, and re-layouts  281 us (26%)
  waiting for transfers between devices  241 us (22%)
  blocking collectives  205 us (19%)
  matrix products  195 us (18%)
  other arithmetic  103 us (9%)
  starting transfers between devices  36.7 us (3%)
  between operations  25 us (2%)
    gather x2, local copies, waits for them, and re-layouts, local(): buffer_x[neighbors[micro]] * weight_mask[..., None]  216 us
    reduce_scatter x1, waiting for transfers between devices, local(): lax.psum_scatter(grad_one, ('dom', 'rep'), scatter_dimension=1, tiled=True)  134 us
    unnamed x3, waiting for transfers between devices  100 us
    dot_general x4, matrix products, contract_rows(): lax.dot_general(left, right, (((0,), (0,)), ((), ())), precision=highest)  92.1 us
    all_gather x1, blocking collectives, local(): lax.all_gather(w_two, ('dom', 'rep'), axis=0, tiled=True)  42.8 us
    all_gather x1, blocking collectives, local(): lax.all_gather(w_one, ('dom', 'rep'), axis=1, tiled=True)  42.4 us
    psum x1, blocking collectives, local(): loss_total = lax.psum(local_loss, ('dom', 'rep'))  41.8 us
    unnamed x1, blocking collectives  40.6 us
  transfers between devices with their start and end apart: 8, of which 3 were waited for; matrix products, arithmetic and copies ran while one was open for 28% of the time, Pallas kernels for 0%

commit v1 on v0

v1 whole, which is shorter than its diff:
```python
import jax
import jax.numpy as jnp
from jax import lax
from jax.experimental import pallas as pl
from jax.experimental.pallas import tpu as pltpu
from jax.sharding import PartitionSpec as P

F = 100
HCAP = 8
STEP = 20
LANES = 128
HALF = 64
GROUP = 16
NODE_BLOCK = 256
HID_BLOCK = 256
COL_BLOCK = 512

tiny_eps = 1e-30
scale_eps = 0.001
clip_limit = 1.0
step_rate = 0.3
f32 = jnp.float32
bf16 = jnp.bfloat16


def dot(a, b, dims=((1,), (0,))):
    return lax.dot_general(a, b, (dims, ((), ())), preferred_element_type=f32)


def split(x):
    hi = x.astype(bf16)
    lo = (x - hi.astype(f32)).astype(bf16)
    return hi, lo


def iota(shape, dim):
    return lax.broadcasted_iota(jnp.int32, shape, dim)


def one_hot(cond):
    return jnp.where(cond, 1.0, 0.0).astype(bf16)


def local_sum_kernel(idx_ref, mask_ref, x_ref, sum_ref, halo_ref, xcat, counts):
    rows = x_ref.shape[1]
    blk = pl.program_id(1)
    high = counts.shape[1] // LANES

    @pl.when(blk == 0)
    def _():
        hi, lo = split(x_ref[0])
        xcat[:, :LANES] = hi
        xcat[:, LANES:] = lo

    width = idx_ref.shape[2]
    lane = iota((1, width), 1)
    key_rows = iota((high * GROUP, width), 0)
    low_rows = iota((LANES, width), 0)
    for g in range(idx_ref.shape[1]):
        v = idx_ref[0, g : g + 1, :]
        key = jnp.where(mask_ref[0, g : g + 1, :] > 0, (v >> 7) * GROUP + lane // GROUP, -1)
        left = one_hot(key_rows == key)
        right = one_hot(low_rows == (v & (LANES - 1)))
        found = dot(left, right, ((1,), (1,))).astype(bf16)
        for h in range(high):
            counts[g * GROUP : (g + 1) * GROUP, h * LANES : (h + 1) * LANES] = found[
                h * GROUP : (h + 1) * GROUP
            ]
    both = dot(counts[:, :rows], xcat[...])
    own = x_ref[0, pl.ds(pl.multiple_of(blk * NODE_BLOCK, NODE_BLOCK), NODE_BLOCK), :]
    sum_ref[0] = both[:, :LANES] + both[:, LANES:] + own
    halo_ref[0] = counts[:, rows:]


def local_sums(idx, mask, x, slots):
    micros, rows, _ = x.shape
    groups = NODE_BLOCK // GROUP
    width = idx.shape[2]
    return pl.pallas_call(
        local_sum_kernel,
        grid=(micros, rows // NODE_BLOCK),
        in_specs=[
            pl.BlockSpec((1, groups, width), lambda m, b: (m, b, 0)),
            pl.BlockSpec((1, groups, width), lambda m, b: (m, b, 0)),
            pl.BlockSpec((1, rows, LANES), lambda m, b: (m, 0, 0)),
        ],
        out_specs=[
            pl.BlockSpec((1, NODE_BLOCK, LANES), lambda m, b: (m, b, 0)),
            pl.BlockSpec((1, NODE_BLOCK, slots), lambda m, b: (m, b, 0)),
        ],
        out_shape=[
            jax.ShapeDtypeStruct((micros, rows, LANES), f32),
            jax.ShapeDtypeStruct((micros, rows, slots), bf16),
        ],
        scratch_shapes=[
            pltpu.VMEM((rows, 2 * LANES), bf16),
            pltpu.VMEM((NODE_BLOCK, rows + slots), bf16),
        ],
        name="local_sums",
    )(idx, mask, x)


def finish_kernel(sum_ref, halo_ref, arrived_ref, agg_ref):
    slots = halo_ref.shape[2]
    arrived = arrived_ref[...].reshape(slots, LANES)
    arrived = jnp.where(iota(arrived.shape, 1) == F, 1.0, arrived)
    hi, lo = split(arrived)
    counts = halo_ref[0]
    total = sum_ref[0] + dot(counts, hi) + dot(counts, lo)
    agg = total / total[:, F : F + 1]
    agg_ref[0] = jnp.where(iota(agg.shape, 1) == F, 1.0, agg)


def finish(sums, halo, arrived):
    micros, rows, slots = halo.shape
    peers = arrived.shape[0]
    block = rows // 2
    return pl.pallas_call(
        finish_kernel,
        grid=(micros, 2),
        in_specs=[
            pl.BlockSpec((1, block, LANES), lambda m, b: (m, b, 0)),
            pl.BlockSpec((1, block, slots), lambda m, b: (m, b, 0)),
            pl.BlockSpec((peers, 1, HCAP, LANES), lambda m, b: (0, m, 0, 0)),
        ],
        out_specs=pl.BlockSpec((1, block, LANES), lambda m, b: (m, b, 0)),
        out_shape=jax.ShapeDtypeStruct((micros, rows, LANES), f32),
        name="finish",
    )(sums, halo, arrived)


def pick_kernel(ends_ref, agg_ref, out_ref, cat):
    @pl.when(pl.program_id(1) == 0)
    def _():
        hi, lo = split(agg_ref[0])
        cat[:, :LANES] = hi
        cat[:, LANES:] = lo

    rows = agg_ref.shape[1]
    ends = ends_ref[0, 0]
    which = one_hot(iota((ends.shape[0], rows), 1) == ends)
    both = dot(which, cat[...])
    out_ref[0, 0] = both[:, :LANES] + both[:, LANES:]


def pick(ends, agg):
    micros, sides, count, _ = ends.shape
    rows = agg.shape[1]
    return pl.pallas_call(
        pick_kernel,
        grid=(micros, sides),
        in_specs=[
            pl.BlockSpec((1, 1, count, 1), lambda m, s: (m, s, 0, 0)),
            pl.BlockSpec((1, rows, LANES), lambda m, s: (m, 0, 0)),
        ],
        out_specs=pl.BlockSpec((1, 1, count, LANES), lambda m, s: (m, s, 0, 0)),
        out_shape=jax.ShapeDtypeStruct((micros, sides, count, LANES), f32),
        scratch_shapes=[pltpu.VMEM((rows, 2 * LANES), bf16)],
        name="pick",
    )(ends, agg)


def first_block(ref, start, shards, hs):
    return ref[pl.ds(start, shards), 0:hs, :].reshape(shards * hs, LANES)


def head_block(ref, start, shards, hs):
    if hs % GROUP:
        return ref[pl.ds(start, shards), hs : 2 * hs, :].reshape(shards * hs, LANES)
    half = hs // 2
    packed = ref[pl.ds(start, shards), hs : hs + half, :].reshape(shards * half, LANES)
    low = iota(packed.shape, 1) < HALF
    left = jnp.where(low, packed, 0.0).reshape(shards, half, LANES)
    right = jnp.where(low, pltpu.roll(packed, HALF, 1), 0.0).reshape(shards, half, LANES)
    return jnp.concatenate([left, right], axis=1).reshape(shards * hs, LANES)


def head_terms(block):
    hi = block.astype(bf16)
    rest = block - hi.astype(f32)
    return hi, (hi.astype(f32) + pltpu.roll(rest, HALF, 1)).astype(bf16)


def layers_kernel(
    part_ref, halo_ref, arrived_ref, mine_ref, other_ref, head_bias_ref,
    grad_mine_ref, grad_other_ref, stats_ref,
    agg_row, agg_col, hidden, out_col, dz_col, dz_row,
    *, hs, slope_scale,
):
    micros, sides, count, _ = part_ref.shape
    ends = micros * sides * count
    slots = arrived_ref.shape[0] * HCAP
    shards = HID_BLOCK // hs
    blocks = mine_ref.shape[0] // shards
    low_lanes = iota((ends, LANES), 1) < HALF

    for m in range(micros):
        arrived = arrived_ref[:, m].reshape(slots, LANES)
        hi, lo = split(arrived)
        which = one_hot(iota((count, slots), 1) == halo_ref[m])
        far = dot(which, hi) + dot(which, lo)
        for s in range(sides):
            rows = part_ref[m, s]
            if s == 1:
                rows = rows + far
            at = (m * sides + s) * count
            hi, lo = split(rows)
            agg_row[at : at + count, :LANES] = hi
            agg_row[at : at + count, LANES:] = lo
            turned = rows.T
            hi, lo = split(turned)
            agg_col[:LANES, at : at + count] = hi
            agg_col[LANES:, at : at + count] = lo

    out_col[...] = jnp.zeros(out_col.shape, f32)

    for side, ref in enumerate((mine_ref, other_ref)):

        def forward(c, carry, ref=ref, side=side):
            first = first_block(ref, c * shards, shards, hs)
            hi, lo = split(first)
            both = jnp.concatenate([hi, lo], axis=1)
            head_hi, head_both = head_terms(head_block(ref, c * shards, shards, hs))
            head = jnp.concatenate([head_both, head_hi], axis=0)
            slot = side * blocks + c
            for n in range(0, ends, COL_BLOCK):
                cols = slice(n, n + COL_BLOCK)
                upper = agg_col[:LANES, cols]
                pre = dot(both, jnp.concatenate([upper, upper], axis=0))
                pre = pre + dot(hi, agg_col[LANES:, cols])
                act_hi, act_lo = split(jnp.maximum(pre, 0.0))
                hidden[slot, :HID_BLOCK, cols] = act_hi
                hidden[slot, HID_BLOCK:, cols] = act_lo
                act = jnp.concatenate([act_hi, act_lo], axis=0)
                out_col[:, cols] += dot(head, act, ((0,), (0,)))
            return carry

        lax.fori_loop(0, blocks, forward, 0)

    bias = head_bias_ref[...]
    loss = jnp.zeros((1, 1), f32)
    head_grad = jnp.zeros((HALF, 1), f32)
    sign = jnp.where(iota((1, count), 1) < count // 2, -1.0, 1.0)
    for m in range(micros):
        at = m * sides * count
        mid = at + count
        end = mid + count
        z_u = out_col[:HALF, at:mid] + out_col[HALF:, at:mid] + bias
        z_v = out_col[:HALF, mid:end] + out_col[HALF:, mid:end] + bias
        score = jnp.sum(z_u * z_v, axis=0, keepdims=True) * sign
        tail = jnp.exp(-jnp.abs(score))
        plus = jnp.maximum(score, 0.0) + jnp.log1p(tail)
        loss = loss + jnp.sum(plus, axis=1, keepdims=True)
        slope = sign * jax.nn.sigmoid(score) * slope_scale
        for start, grad in ((at, slope * z_v), (mid, slope * z_u)):
            stop = start + count
            head_grad = head_grad + jnp.sum(grad, axis=1, keepdims=True)
            hi, lo = split(grad)
            dz_col[:HALF, start:stop] = hi
            dz_col[HALF : 2 * HALF, start:stop] = hi
            dz_col[2 * HALF : 3 * HALF, start:stop] = lo
            dz_col[3 * HALF :, start:stop] = jnp.zeros((HALF, count), bf16)
            both = jnp.concatenate([hi.astype(f32), lo.astype(f32)], axis=0)
            dz_row[start:stop] = both.T.astype(bf16)
    stats_ref[:HALF] = jnp.broadcast_to(head_grad, (HALF, LANES))
    stats_ref[HALF:] = jnp.broadcast_to(loss, (8, LANES))

    for side, (ref, grad_ref) in enumerate(((mine_ref, grad_mine_ref), (other_ref, grad_other_ref))):

        def backward(c, carry, ref=ref, grad_ref=grad_ref, side=side):
            head_hi, head_both = head_terms(head_block(ref, c * shards, shards, hs))
            head = jnp.concatenate([head_both, head_hi], axis=1)
            slot = side * blocks + c
            head_sum = jnp.zeros((HID_BLOCK, LANES), f32)
            first_sum = jnp.zeros((HID_BLOCK, LANES), f32)
            for n in range(0, ends, COL_BLOCK):
                cols = slice(n, n + COL_BLOCK)
                act_hi = hidden[slot, :HID_BLOCK, cols]
                act_lo = hidden[slot, HID_BLOCK:, cols]
                grad = dot(head, dz_col[:, cols])
                grad = jnp.where(act_hi.astype(f32) > 0.0, grad, 0.0)
                hi, lo = split(grad)
                head_sum = head_sum + dot(act_hi, dz_row[cols]) + dot(act_lo, dz_row[cols])
                both = dot(hi, agg_row[cols])
                first_sum = first_sum + both[:, :LANES] + both[:, LANES:]
                first_sum = first_sum + dot(lo, agg_row[cols, :LANES])
            grad_ref[pl.ds(c * shards, shards), 0:hs, :] = first_sum.reshape(shards, hs, LANES)
            folded = (head_sum + pltpu.roll(head_sum, HALF, 1)).reshape(shards, hs, LANES)
            if hs % GROUP:
                grad_ref[pl.ds(c * shards, shards), hs : 2 * hs, :] = folded
            else:
                half = hs // 2
                low = iota((shards, half, LANES), 2) < HALF
                grad_ref[pl.ds(c * shards, shards), hs : hs + half, :] = jnp.where(
                    low, folded[:, :half], folded[:, half:]
                )
            return carry

        lax.fori_loop(0, blocks, backward, 0)


def layers(part, halo_ends, arrived, mine, other, head_bias, hs, slope_scale):
    micros, sides, count, _ = part.shape
    ends = micros * sides * count
    blocks = 2 * mine.shape[0] * hs // HID_BLOCK
    shape = jax.ShapeDtypeStruct(mine.shape, f32)
    return pl.pallas_call(
        lambda *refs: layers_kernel(*refs, hs=hs, slope_scale=slope_scale),
        out_shape=[shape, shape, jax.ShapeDtypeStruct((HALF + 8, LANES), f32)],
        scratch_shapes=[
            pltpu.VMEM((ends, 2 * LANES), bf16),
            pltpu.VMEM((2 * LANES, ends), bf16),
            pltpu.VMEM((blocks, 2 * HID_BLOCK, ends), bf16),
            pltpu.VMEM((LANES, ends), f32),
            pltpu.VMEM((4 * HALF, ends), bf16),
            pltpu.VMEM((ends, LANES), bf16),
        ],
        name="layers",
    )(part, halo_ends, arrived, mine, other, head_bias)


def stages(size):
    found = []
    stride = 1
    while stride < size:
        radix = min(4, size // stride)
        found.append((stride, radix))
        stride *= radix
    return found


def trade(x, offset):
    size = lax.axis_size("dom")
    return lax.ppermute(x, "dom", [(i, i ^ offset) for i in range(size)])


def swap(x):
    return lax.ppermute(x, "rep", [(0, 1), (1, 0)])


def spread(x):
    x = x[None]
    for stride, radix in reversed(stages(lax.axis_size("dom"))):
        x = jnp.concatenate([x] + [trade(x, stride * k) for k in range(1, radix)], axis=0)
    return x, swap(x)


def collect(mine, other):
    x = mine + swap(other)
    for stride, radix in stages(lax.axis_size("dom")):
        parts = x.reshape((radix, x.shape[0] // radix) + x.shape[1:])
        y = parts[0]
        for k in range(1, radix):
            y = y + trade(parts[k], stride * k)
        x = y
    return x[0]


def pack_shard(w_one, b_one, w_two):
    hs = b_one.shape[0]
    first = jnp.concatenate([w_one.T, b_one[:, None]], axis=1)
    first = jnp.pad(first, ((0, 0), (0, LANES - first.shape[1])))
    if hs % GROUP:
        head = jnp.pad(w_two, ((0, 0), (0, LANES - w_two.shape[1])))
    else:
        head = jnp.pad(w_two, ((0, 0), (0, HALF - w_two.shape[1])))
        head = jnp.concatenate([head[: hs // 2], head[hs // 2 :]], axis=1)
    return jnp.concatenate([first, head], axis=0)


def unpack_shard(g, hs, classes):
    head = g[hs:]
    if hs % GROUP == 0:
        head = jnp.concatenate([head[:, :HALF], head[:, HALF:]], axis=0)
    return g[:hs, :F].T, g[:hs, F], head[:, :classes]


def global_sum(x):
    count = lax.axis_size("dom") * lax.axis_size("rep")
    size = -(-x.shape[0] // LANES)
    x = jnp.pad(x, (0, size * LANES - x.shape[0])).reshape(1, size, LANES)
    x = jnp.broadcast_to(x, (count, size, LANES))
    return jnp.sum(lax.all_to_all(x, ("dom", "rep"), 0, 0, tiled=True), axis=0).reshape(-1)


def local(
    features,
    neighbors,
    nbr_mask,
    send_rows,
    halo_count,
    pos_edges,
    neg_edges,
    w_one,
    b_one,
    w_two,
    b_two,
    w_one_row,
    w_one_col,
    w_two_row,
    w_two_col,
    b_one_second,
    b_two_second,
):
    peers = lax.axis_size("dom")
    ranks = lax.axis_size("rep")
    micros, rows, _ = features.shape
    classes = w_two.shape[1]
    hs = b_one.shape[0]
    hidden_units = hs * peers * ranks
    slots = peers * HCAP
    total_edges = pos_edges.shape[1] * peers * micros * ranks
    degree = neighbors.shape[2]

    mine, other = spread(pack_shard(w_one, b_one, w_two))

    x = jnp.concatenate([features, jnp.ones((micros, rows, 1), f32)], axis=2)
    x = jnp.pad(x, ((0, 0), (0, 0), (0, LANES - F - 1)))
    valid = (jnp.arange(HCAP) < halo_count[..., None]).astype(f32)

    def exchange(values):
        sent = jnp.stack([values[m][send_rows[m]] for m in range(micros)], axis=1)
        sent = sent * jnp.moveaxis(valid, 0, 1)[..., None]
        return lax.all_to_all(sent, "dom", 0, 0, tiled=True)

    arrived_x = exchange(x)
    width = GROUP * degree
    sums, halo = local_sums(
        neighbors.reshape(micros, rows // GROUP, width),
        nbr_mask.reshape(micros, rows // GROUP, width),
        x,
        slots,
    )
    agg = finish(sums, halo, arrived_x)
    arrived_agg = exchange(agg)
    edges = jnp.concatenate([pos_edges, neg_edges], axis=1)
    ends = jnp.moveaxis(edges, 2, 1)[..., None]
    part = pick(ends, agg)
    head_bias = jnp.pad(b_two, (0, HALF - classes))[:, None]
    grad_mine, grad_other, stats = layers(
        part, ends[:, 1] - rows, arrived_agg, mine, other, head_bias, hs, 1.0 / (2.0 * total_edges)
    )
    g_one, gb_one, g_two = unpack_shard(collect(grad_mine, grad_other), hs, classes)

    decay = 1.0 - f32(STEP) ** (-0.8)
    square = g_one * g_one
    square_two = g_two * g_two
    row_part = jnp.sum(square + tiny_eps, axis=1)
    col_one = decay * w_one_col + (1.0 - decay) * jnp.sum(square + tiny_eps, axis=0)
    row_two = decay * w_two_row + (1.0 - decay) * jnp.sum(square_two + tiny_eps, axis=1)
    col_part = jnp.sum(square_two + tiny_eps, axis=0)
    second_one = decay * b_one_second + (1.0 - decay) * (gb_one * gb_one + tiny_eps)
    step_bias = gb_one * lax.rsqrt(second_one)
    scalars = jnp.stack(
        [
            jnp.sum(row_two),
            jnp.sum(w_one * w_one),
            jnp.sum(w_two * w_two),
            jnp.sum(b_one * b_one),
            jnp.sum(step_bias * step_bias),
            stats[HALF, 0],
        ]
    )
    pieces = [
        row_part,
        jnp.sum(square / col_one[None, :], axis=1),
        col_part,
        jnp.sum(square_two / row_two[:, None], axis=0),
        stats[:classes, 0],
        scalars,
    ]
    sums = global_sum(jnp.concatenate(pieces))
    found = []
    start = 0
    for piece in pieces:
        found.append(sums[start : start + piece.shape[0]])
        start += piece.shape[0]
    row_sum, row_scaled, col_sum, col_scaled, gb_two, scalars = found
    row_two_total, total_one, total_two, total_bias, rms_bias, loss_total = scalars
    loss = loss_total / (2.0 * total_edges)
    row_one = decay * w_one_row + (1.0 - decay) * row_sum
    col_two = decay * w_two_col + (1.0 - decay) * col_sum
    second_two = decay * b_two_second + (1.0 - decay) * (gb_two * gb_two + tiny_eps)
    row_one_total = jnp.sum(row_one)
    rms_one = jnp.sum(row_scaled / row_one) * row_one_total
    rms_two = jnp.sum(col_scaled / col_two) * row_two_total
    step_one = g_one * lax.rsqrt(jnp.outer(row_one, col_one) / row_one_total)
    step_two = g_two * lax.rsqrt(jnp.outer(row_two, col_two) / row_two_total)
    step_head = gb_two * lax.rsqrt(second_two)

    def clip(step, mean):
        return step / jnp.maximum(1.0, jnp.sqrt(mean) / clip_limit)

    step_one = clip(step_one, rms_one / (F * hidden_units))
    step_two = clip(step_two, rms_two / (hidden_units * classes))
    step_bias = clip(step_bias, rms_bias / hidden_units)
    step_head = clip(step_head, jnp.mean(step_head * step_head))

    def moved(old, mean, step):
        return old - step_rate * jnp.maximum(scale_eps, jnp.sqrt(mean)) * step

    return (
        loss,
        g_one,
        moved(w_one, total_one / (F * hidden_units), step_one),
        row_one,
        col_one,
        g_two,
        moved(w_two, total_two / (hidden_units * classes), step_two),
        row_two,
        col_two,
        gb_one,
        moved(b_one, total_bias / hidden_units, step_bias),
        second_one,
        gb_two,
        moved(b_two, jnp.mean(b_two * b_two), step_head),
        second_two,
    )


def solution(mesh):
    return jax.shard_map(
        local,
        mesh=mesh,
        in_specs=(
            P("rep", "dom", None),
            P("rep", "dom", None),
            P("rep", "dom", None),
            P("rep", "dom", None),
            P("rep", "dom"),
            P("rep", "dom", None),
            P("rep", "dom", None),
            P(None, ("dom", "rep")),
            P(("dom", "rep")),
            P(("dom", "rep"), None),
            P(),
            P(),
            P(("dom", "rep")),
            P(("dom", "rep")),
            P(),
            P(("dom", "rep")),
            P(),
        ),
        out_specs=(
            P(),
            P(None, ("dom", "rep")),
            P(None, ("dom", "rep")),
            P(),
            P(("dom", "rep")),
            P(("dom", "rep"), None),
            P(("dom", "rep"), None),
            P(("dom", "rep")),
            P(),
            P(("dom", "rep")),
            P(("dom", "rep")),
            P(("dom", "rep")),
            P(),
            P(),
            P(),
        ),
        check_vma=False,
    )
```

time: 1100 us -> 180 us (0.16); the launches traced: 1090 us -> 179 us
  local copies, waits for them, and re-layouts: 281 us -> 26.8 us
  waiting for transfers between devices: 241 us -> 28.3 us
  blocking collectives: 205 us -> 0 us
  matrix products: 195 us -> 0 us
  other arithmetic: 103 us -> 13.3 us
  Pallas kernels: 0 us -> 68.3 us
  between operations: 25 us -> 9.74 us
    gather x14 -> x4, local copies, waits for them, and re-layouts: 233 us -> 2.58 us  [exchange(): sent = jnp.stack([values[m][send_rows[m]] for m in range(micros)], axis=1)]
    dot_general x10 -> x0, matrix products: 195 us -> none  [the longest x4 92.1 us: contract_rows(): lax.dot_general(left, right, (((0,), (0,)), ((), ())), precision=highest)]
    reduce_scatter x1 -> x0, waiting for transfers between devices: 134 us -> none  [local(): lax.psum_scatter(grad_one, ('dom', 'rep'), scatter_dimension=1, tiled=True)]
    unnamed x3 -> x0, waiting for transfers between devices: 100 us -> none
    all_gather x2 -> x0, blocking collectives: 85.2 us -> none  [the longest x1 42.8 us: local(): lax.all_gather(w_two, ('dom', 'rep'), axis=0, tiled=True)]
    psum x2 -> x0, blocking collectives: 78.8 us -> none  [the longest x1 41.8 us: local(): loss_total = lax.psum(local_loss, ('dom', 'rep'))]
    pallas_call x0 -> x4, Pallas kernels: none -> 68.3 us  [the longest x1 30.8 us: layers(): pl.pallas_call(lambda *refs: layers_kernel(*refs, hs=hs, slope_scale=slop...]
    unnamed x1 -> x0, blocking collectives: 40.6 us -> none
  transfers between devices with their start and end apart: 8 -> 17, of which waited for: 3 -> 8; matrix products, arithmetic and copies ran while one was open for 28% -> 11% of each run, Pallas kernels for 0% -> 21%
where the time goes in v1:
time: 180 us; the launch traced here: 179 us
  Pallas kernels  68.3 us (38%)
  starting transfers between devices  32.9 us (18%)
  waiting for transfers between devices  28.3 us (16%)
  local copies, waits for them, and re-layouts  26.8 us (15%)
  other arithmetic  13.3 us (7%)
  between operations  9.74 us (5%)
    pallas_call x1, Pallas kernels, layers(): pl.pallas_call(lambda *refs: layers_kernel(*refs, hs=hs, slope_scale=slop...  30.8 us
    pallas_call x1, Pallas kernels, local_sums(): pl.pallas_call(local_sum_kernel, grid=(micros, rows // NODE_BLOCK), in_sp...  26.8 us
    ppermute x12, waiting for transfers between devices, trade(): return lax.ppermute(x, 'dom', [(i, i ^ offset) for i in range(size)])  20.4 us
    ppermute x12, starting transfers between devices, trade(): return lax.ppermute(x, 'dom', [(i, i ^ offset) for i in range(size)])  17.2 us
    all_to_all x2, starting transfers between devices, exchange(): return lax.all_to_all(sent, 'dom', 0, 0, tiled=True)  12.4 us
    unnamed x69, local copies, waits for them, and re-layouts  8.84 us
    all_to_all x1, waiting for transfers between devices, global_sum(): lax.all_to_all(x, ('dom', 'rep'), 0, 0, tiled=True)  6.11 us
    pallas_call x1, Pallas kernels, pick(): pl.pallas_call(pick_kernel, grid=(micros, sides), in_specs=[pl.BlockSpec(...  6.08 us
  transfers between devices with their start and end apart: 17, of which 8 were waited for; matrix products, arithmetic and copies ran while one was open for 11% of the time, Pallas kernels for 21%

profile of v1, /device:TPU:0, one launch (start us, length us, event | category | flops | bytes accessed | tf_op | source)
XLA Modules:
  0.0 179.3 jit_solution(13162423399458594475)
XLA Ops:
  0.6 0.8 copy.96
  1.5 0.7 copy.95
  2.2 0.8 select_maximum_fusion
  3.1 3.1 %collective-permute-start = (f32[1,96,128]{2,1,0:T(8,128)S(1)}, f32[1,96,128]{2,1,0:T(8,128)S(1)}, u32[]{:S(2)}, u32[]{:S(2)}) collective-permute-start(f32[1,96,128]{2,1,0:T(8,128)S(1)} %get-tuple-element.119), channel_id=1, source_target_pairs={{0,8},{2,10},{4,12},{6,14},{8,0},{10,2},{12,4},{14,6},{16,24},{18,... | collective-permute-start | bytes 147464 | tf_op jit(solution)/shard_map/ppermute | solution.py:334
  6.2 2.6 %collective-permute-start.1 = (f32[1,96,128]{2,1,0:T(8,128)S(1)}, f32[1,96,128]{2,1,0:T(8,128)S(1)}, u32[]{:S(2)}, u32[]{:S(2)}) collective-permute-start(f32[1,96,128]{2,1,0:T(8,128)S(1)} %get-tuple-element.119), channel_id=1, source_target_pairs={{0,16},{2,18},{4,20},{6,22},{8,24},{10,26},{12,28},{14,30},{16,0},... | collective-permute-start | bytes 147464 | tf_op jit(solution)/shard_map/ppermute | solution.py:334
  8.8 0.7 compare_select_fusion.1
  9.8 2.7 %copy.90 = f32[2,2048,100]{2,1,0:T(8,128)S(1)} copy(f32[2,2048,100]{1,0,2:T(2,128)} %param.17) | data formatting | bytes 3276800 | tf_op args[0]
  12.9 1.1 copy-done
  14.2 0.6 gather_fusion
  14.9 0.6 gather_fusion.1
  15.5 0.8 maximum_multiply_fusion
  16.3 7.1 %all-to-all-start = ((f32[16,2,8,128]{3,2,1,0:T(8,128)}), f32[16,2,8,128]{3,2,1,0:T(8,128)S(1)}, u32[]{:S(2)}, u32[]{:S(2)}) async-start(f32[16,2,8,128]{3,2,1,0:T(8,128)} %maximum_multiply_fusion), calls=%async_computation | async-start | bytes 262144 | tf_op jit(solution)/shard_map/all_to_all | solution.py:424
  23.4 0.6 copy.88
  24.0 1.6 reshape.169.idx_ref
  25.6 0.6 copy.89
  26.2 1.5 reshape.170.mask_ref
  27.7 26.8 %local_sums.1 = (f32[2,2048,128]{2,1,0:T(8,128)}, bf16[2,2048,128]{2,1,0:T(8,128)(2,1)}) custom-call(s32[2,128,256]{2,1,0:T(8,128)} %reshape.169.idx_ref, s32[2,128,256]{2,1,0:T(8,128)} %reshape.170.mask_ref, f32[2,2048,128]{2,1,0:T(8,128)} %copy-done), custom_call_target="tpu_custom_call" | custom-call | tf_op jit(solution)/shard_map/local_sums/pallas_call | solution.py:79
  54.5 2.0 %collective-permute-start.3 = (f32[4,96,128]{2,1,0:T(8,128)S(1)}, f32[4,96,128]{2,1,0:T(8,128)S(1)}, u32[]{:S(2)}, u32[]{:S(2)}) collective-permute-start(f32[4,96,128]{2,1,0:T(8,128)S(1)} %pad_maximum_fusion), channel_id=1, source_target_pairs={{0,2},{2,0},{4,6},{6,4},{8,10},{10,8},{12,14},{14,12},{16,18},{18,... | collective-permute-start | bytes 589832 | tf_op jit(solution)/shard_map/ppermute | solution.py:334
  56.5 1.5 collective-permute-start.4
  58.1 4.0 %collective-permute-done.3 = f32[4,96,128]{2,1,0:T(8,128)S(1)} collective-permute-done((f32[4,96,128]{2,1,0:T(8,128)S(1)}, f32[4,96,128]{2,1,0:T(8,128)S(1)}, u32[]{:S(2)}, u32[]{:S(2)}) %collective-permute-start.3) | collective-permute-done | bytes 196640 | tf_op jit(solution)/shard_map/ppermute | solution.py:334
  62.1 3.9 %collective-permute-done.4 = f32[4,96,128]{2,1,0:T(8,128)S(1)} collective-permute-done((f32[4,96,128]{2,1,0:T(8,128)S(1)}, f32[4,96,128]{2,1,0:T(8,128)S(1)}, u32[]{:S(2)}, u32[]{:S(2)}) %collective-permute-start.4) | collective-permute-done | bytes 196640 | tf_op jit(solution)/shard_map/ppermute | solution.py:334
  66.1 0.8 copy-done.3
  66.9 4.6 %finish.1.agg_ref = f32[2,2048,128]{2,1,0:T(8,128)} custom-call(f32[2,2048,128]{2,1,0:T(8,128)} %get-tuple-element.20.sum_ref, bf16[2,2048,128]{2,1,0:T(8,128)(2,1)} %get-tuple-element.21.halo_ref, f32[16,2,8,128]{3,2,1,0:T(8,128)} %copy-done.3), custom_call_target="tpu_custom_call" | custom-call | tf_op jit(solution)/shard_map/finish/pallas_call | solution.py:118
  71.5 1.7 slice_bitcast_fusion.1
  73.2 0.6 gather_fusion.2
  73.9 0.6 gather_fusion.3
  74.5 0.8 maximum_multiply_fusion.1
  75.3 5.3 %all-to-all-start.1 = ((f32[16,2,8,128]{3,2,1,0:T(8,128)}), f32[16,2,8,128]{3,2,1,0:T(8,128)S(1)}, u32[]{:S(2)}, u32[]{:S(2)}) async-start(f32[16,2,8,128]{3,2,1,0:T(8,128)} %maximum_multiply_fusion.1), calls=%async_computation.1 | async-start | bytes 262144 | tf_op jit(solution)/shard_map/all_to_all | solution.py:424
  80.6 1.4 copy.94.ends_ref
  82.1 1.0 sub.31.refs_1_
  83.1 0.7 copy.98.refs_5_
  83.8 6.1 %pick.1.refs_0_ = f32[2,2,512,128]{3,2,1,0:T(8,128)} custom-call(s32[2,2,512,1]{3,2,1,0:T(8,128)} %copy.94.ends_ref, f32[2,2048,128]{2,1,0:T(8,128)} %finish.1.agg_ref), custom_call_target="tpu_custom_call" | custom-call | tf_op jit(solution)/shard_map/pick/pallas_call | solution.py:149
  89.9 0.6 copy-done.2
  90.5 30.8 %layers.1 = (f32[16,96,128]{2,1,0:T(8,128)}, f32[16,96,128]{2,1,0:T(8,128)}, f32[72,128]{1,0:T(8,128)}) custom-call(f32[2,2,512,128]{3,2,1,0:T(8,128)} %pick.1.refs_0_, s32[2,512,1]{2,1,0:T(8,128)} %sub.31.refs_1_, f32[16,2,8,128]{3,2,1,0:T(8,128)} %copy-done.2, f32[16,96,128]{2,1,0:T(8,128)} %copy-done.1, f32[16,96,128]{2,1,0:T(8,128)} %collective-permute-done.6.refs_4_, ...), custom_call_target="tpu_custom_call" | custom-call | tf_op jit(solution)/shard_map/layers/pallas_call | solution.py:307
  121.4 0.6 multiply_reduce_fusion.1
  122.0 1.8 %collective-permute-done.7 = f32[16,96,128]{2,1,0:T(8,128)S(1)} collective-permute-done((f32[16,96,128]{2,1,0:T(8,128)}, f32[16,96,128]{2,1,0:T(8,128)S(1)}, u32[]{:S(2)}, u32[]{:S(2)}) %collective-permute-start.7) | collective-permute-done | bytes 786464 | tf_op jit(solution)/shard_map/ppermute | solution.py:338
  123.8 1.2 add.105
  125.2 2.9 %collective-permute-start.10 = (f32[4,96,128]{2,1,0:T(8,128)S(1)}, f32[4,96,128]{2,1,0:T(8,128)S(1)}, u32[]{:S(2)}, u32[]{:S(2)}) collective-permute-start(f32[4,96,128]{2,1,0:T(8,128)S(1)} %get-tuple-element.125), channel_id=1, source_target_pairs={{0,6},{2,4},{4,2},{6,0},{8,14},{10,12},{12,10},{14,8},{16,22},{18,... | collective-permute-start | bytes 589832 | tf_op jit(solution)/shard_map/ppermute | solution.py:334
  128.0 0.6 collective-permute-start.8
  128.7 0.6 multiply_reduce_fusion.5
  129.3 0.6 multiply_reduce_fusion
  129.9 4.0 %collective-permute-done.10 = f32[4,96,128]{2,1,0:T(8,128)S(1)} collective-permute-done((f32[4,96,128]{2,1,0:T(8,128)S(1)}, f32[4,96,128]{2,1,0:T(8,128)S(1)}, u32[]{:S(2)}, u32[]{:S(2)}) %collective-permute-start.10) | collective-permute-done | bytes 196640 | tf_op jit(solution)/shard_map/ppermute | solution.py:334
  133.9 3.8 %collective-permute-done.8 = f32[4,96,128]{2,1,0:T(8,128)S(1)} collective-permute-done((f32[4,96,128]{2,1,0:T(8,128)S(1)}, f32[4,96,128]{2,1,0:T(8,128)S(1)}, u32[]{:S(2)}, u32[]{:S(2)}) %collective-permute-start.8) | collective-permute-done | bytes 196640 | tf_op jit(solution)/shard_map/ppermute | solution.py:334
  137.9 1.5 collective-permute-start.11
  139.4 2.4 %collective-permute-start.12 = (f32[1,96,128]{2,1,0:T(8,128)S(1)}, f32[1,96,128]{2,1,0:T(8,128)S(1)}, u32[]{:S(2)}, u32[]{:S(2)}) collective-permute-start(f32[1,96,128]{2,1,0:T(8,128)S(1)} %get-tuple-element.129), channel_id=1, source_target_pairs={{0,16},{2,18},{4,20},{6,22},{8,24},{10,26},{12,28},{14,30},{16,0},... | collective-permute-start | bytes 147464 | tf_op jit(solution)/shard_map/ppermute | solution.py:334
  141.8 0.6 collective-permute-start.13
  142.4 0.5 slice.135
  142.9 2.4 %collective-permute-done.12 = f32[1,96,128]{2,1,0:T(8,128)S(1)} collective-permute-done((f32[1,96,128]{2,1,0:T(8,128)S(1)}, f32[1,96,128]{2,1,0:T(8,128)S(1)}, u32[]{:S(2)}, u32[]{:S(2)}) %collective-permute-start.12) | collective-permute-done | bytes 49184 | tf_op jit(solution)/shard_map/ppermute | solution.py:334
  145.3 2.3 %collective-permute-done.13 = f32[1,96,128]{2,1,0:T(8,128)S(1)} collective-permute-done((f32[1,96,128]{2,1,0:T(8,128)S(1)}, f32[1,96,128]{2,1,0:T(8,128)S(1)}, u32[]{:S(2)}, u32[]{:S(2)}) %collective-permute-start.13) | collective-permute-done | bytes 49184 | tf_op jit(solution)/shard_map/ppermute | solution.py:334
  148.2 0.6 fusion.8
  149.0 0.6 multiply_reduce_fusion.4
  149.6 4.0 %concatenate.36 = f32[347]{0:T(512)S(1)} concatenate(f32[100]{0:T(128)S(1)} %get-tuple-element.103, f32[100]{0:T(128)S(1)} %get-tuple-element.102, f32[47]{0:T(128)S(1)} %get-tuple-element.101, f32[47]{0:T(128)S(1)} %get-tuple-element.100, f32[47]{0:T(128)S(1)} %slice_reduce_fusion.1, f32[1]{0:T(128)} %bitcast.21, f32[1]{0:T(128)} %bitcast.22, f32[1]{0:T(128)} %bitcast.23, ...), dimensions={0} | concatenate | bytes 2776 | tf_op jit(solution)/shard_map/concatenate | solution.py:472
  153.6 0.6 broadcast_in_dim.17
  154.2 3.1 %all-to-all-start.2 = ((f32[32,3,128]{2,1,0:T(4,128)}), f32[32,3,128]{2,1,0:T(4,128)S(1)}, u32[]{:S(2)}, u32[]{:S(2)}) async-start(f32[32,3,128]{2,1,0:T(4,128)} %broadcast_in_dim.17), calls=%async_computation.2 | async-start | bytes 131072 | tf_op jit(solution)/shard_map/all_to_all | solution.py:383
  157.4 0.6 multiply_reduce_fusion.3
  158.7 6.1 %all-to-all-done.2 = f32[32,3,128]{2,1,0:T(4,128)S(1)} async-done(((f32[32,3,128]{2,1,0:T(4,128)}), f32[32,3,128]{2,1,0:T(4,128)S(1)}, u32[]{:S(2)}, u32[]{:S(2)}) %all-to-all-start.2) | async-done | bytes 49184 | tf_op jit(solution)/shard_map/all_to_all | solution.py:383
  164.8 0.7 fusion.12
  165.5 0.7 multiply_reduce_fusion.2
  170.3 0.7 multiply_subtract_fusion
  171.0 0.7 copy.101
  171.7 0.7 copy.102
  172.4 0.7 fusion.7
  175.8 0.5 multiply_subtract_fusion.3
  176.3 1.3 multiply_subtract_fusion.1
  (106 shorter events, 3.0 us)
Async XLA Ops:
  3.1 51.4 %collective-permute-start = (f32[1,96,128]{2,1,0:T(8,128)S(1)}, f32[1,96,128]{2,1,0:T(8,128)S(1)}, u32[]{:S(2)}, u32[]{:S(2)}) collective-permute-start(f32[1,96,128]{2,1,0:T(8,128)S(1)} %get-tuple-element.119), channel_id=1, source_target_pairs={{0,8},{2,10},{4,12},{6,14},{8,0},{10,2},{12,4},{14,6},{16,24},{18,... | collective-permute-start | bytes 147464 | tf_op jit(solution)/shard_map/ppermute | solution.py:334
  6.2 48.3 %collective-permute-start.1 = (f32[1,96,128]{2,1,0:T(8,128)S(1)}, f32[1,96,128]{2,1,0:T(8,128)S(1)}, u32[]{:S(2)}, u32[]{:S(2)}) collective-permute-start(f32[1,96,128]{2,1,0:T(8,128)S(1)} %get-tuple-element.119), channel_id=1, source_target_pairs={{0,16},{2,18},{4,20},{6,22},{8,24},{10,26},{12,28},{14,30},{16,0},... | collective-permute-start | bytes 147464 | tf_op jit(solution)/shard_map/ppermute | solution.py:334
  8.8 45.7 %collective-permute-start.2 = (f32[1,96,128]{2,1,0:T(8,128)S(1)}, f32[1,96,128]{2,1,0:T(8,128)S(1)}, u32[]{:S(2)}, u32[]{:S(2)}) collective-permute-start(f32[1,96,128]{2,1,0:T(8,128)S(1)} %get-tuple-element.119), channel_id=1, source_target_pairs={{0,24},{2,26},{4,28},{6,30},{8,16},{10,18},{12,20},{14,22},{16,8},... | collective-permute-start | bytes 147464 | tf_op jit(solution)/shard_map/ppermute | solution.py:334
  12.7 1.3 copy-start
  12.7 1.3 copy-start.21
  12.8 10.6 %copy-start.6 = (s32[2,2048,16]{1,2,0:T(8,128)S(1)}, s32[2,2048,16]{1,2,0:T(8,128)}, u32[]{:S(2)}) copy-start(s32[2,2048,16]{1,2,0:T(8,128)} %param.18) | copy-start | bytes 786436
  16.3 49.8 %all-to-all-start = ((f32[16,2,8,128]{3,2,1,0:T(8,128)}), f32[16,2,8,128]{3,2,1,0:T(8,128)S(1)}, u32[]{:S(2)}, u32[]{:S(2)}) async-start(f32[16,2,8,128]{3,2,1,0:T(8,128)} %maximum_multiply_fusion), calls=%async_computation | async-start | bytes 262144 | tf_op jit(solution)/shard_map/all_to_all | solution.py:424
  24.0 1.6 copy-start.7
  54.5 7.5 %collective-permute-start.3 = (f32[4,96,128]{2,1,0:T(8,128)S(1)}, f32[4,96,128]{2,1,0:T(8,128)S(1)}, u32[]{:S(2)}, u32[]{:S(2)}) collective-permute-start(f32[4,96,128]{2,1,0:T(8,128)S(1)} %pad_maximum_fusion), channel_id=1, source_target_pairs={{0,2},{2,0},{4,6},{6,4},{8,10},{10,8},{12,14},{14,12},{16,18},{18,... | collective-permute-start | bytes 589832 | tf_op jit(solution)/shard_map/ppermute | solution.py:334
  56.5 9.4 %collective-permute-start.4 = (f32[4,96,128]{2,1,0:T(8,128)S(1)}, f32[4,96,128]{2,1,0:T(8,128)S(1)}, u32[]{:S(2)}, u32[]{:S(2)}) collective-permute-start(f32[4,96,128]{2,1,0:T(8,128)S(1)} %pad_maximum_fusion), channel_id=1, source_target_pairs={{0,4},{2,6},{4,0},{6,2},{8,12},{10,14},{12,8},{14,10},{16,20},{18,... | collective-permute-start | bytes 589832 | tf_op jit(solution)/shard_map/ppermute | solution.py:334
  58.0 8.0 %collective-permute-start.5 = (f32[4,96,128]{2,1,0:T(8,128)S(1)}, f32[4,96,128]{2,1,0:T(8,128)S(1)}, u32[]{:S(2)}, u32[]{:S(2)}) collective-permute-start(f32[4,96,128]{2,1,0:T(8,128)S(1)} %pad_maximum_fusion), channel_id=1, source_target_pairs={{0,6},{2,4},{4,2},{6,0},{8,14},{10,12},{12,10},{14,8},{16,22},{18,... | collective-permute-start | bytes 589832 | tf_op jit(solution)/shard_map/ppermute | solution.py:334
  66.0 5.5 %copy-start.1 = (f32[16,96,128]{2,1,0:T(8,128)}, f32[16,96,128]{2,1,0:T(8,128)S(1)}, u32[]{:S(2)}) copy-start(f32[16,96,128]{2,1,0:T(8,128)S(1)} %constant_dynamic-update-slice_fusion.refs_3_) | copy-start | bytes 2359300
  66.0 23.9 %collective-permute-start.6 = (f32[16,96,128]{2,1,0:T(8,128)S(1)}, f32[16,96,128]{2,1,0:T(8,128)}, u32[]{:S(2)}, u32[]{:S(2)}) collective-permute-start(f32[16,96,128]{2,1,0:T(8,128)S(1)} %constant_dynamic-update-slice_fusion.refs_3_), channel_id=1, source_target_pairs={{0,1},{1,0},{2,3},{3,2},{4,5},{5,4},{6,7},{7,6},{8,9},{9,8},{10,11... | collective-permute-start | bytes 2359304 | tf_op jit(solution)/shard_map/ppermute | solution.py:338
  66.1 0.8 copy-start.3
  71.5 9.1 %copy-start.12 = (s32[2,256,2]{1,2,0:T(2,128)S(1)}, s32[2,256,2]{1,2,0:T(2,128)}, u32[]{:S(2)}) copy-start(s32[2,256,2]{1,2,0:T(2,128)} %param.23) | copy-start | bytes 12292
  71.5 9.1 %copy-start.13 = (s32[2,256,2]{1,2,0:T(2,128)S(1)}, s32[2,256,2]{1,2,0:T(2,128)}, u32[]{:S(2)}) copy-start(s32[2,256,2]{1,2,0:T(2,128)} %param.22) | copy-start | bytes 12292
  73.2 9.8 %copy-start.27 = (f32[47]{0:T(128)S(1)}, f32[47]{0:T(128)}, u32[]{:S(2)}) copy-start(f32[47]{0:T(128)} %param.27) | copy-start | bytes 568
  75.3 14.6 %all-to-all-start.1 = ((f32[16,2,8,128]{3,2,1,0:T(8,128)}), f32[16,2,8,128]{3,2,1,0:T(8,128)S(1)}, u32[]{:S(2)}, u32[]{:S(2)}) async-start(f32[16,2,8,128]{3,2,1,0:T(8,128)} %maximum_multiply_fusion.1), calls=%async_computation.1 | async-start | bytes 262144 | tf_op jit(solution)/shard_map/all_to_all | solution.py:424
  89.9 31.5 %copy-start.8 = (f32[64,47]{0,1:T(8,128)S(1)}, f32[64,47]{0,1:T(8,128)}, u32[]{:S(2)}) copy-start(f32[64,47]{0,1:T(8,128)} %param.26) | copy-start | bytes 36100
  89.9 0.7 copy-start.2
  121.3 7.4 %copy-start.16 = (f32[64]{0:T(128)S(1)}, f32[64]{0:T(128)}, u32[]{:S(2)}) copy-start(f32[64]{0:T(128)} %param.25) | copy-start | bytes 772
  121.3 8.0 %copy-start.4 = (f32[100,64]{0,1:T(8,128)S(1)}, f32[100,64]{0,1:T(8,128)}, u32[]{:S(2)}) copy-start(f32[100,64]{0,1:T(8,128)} %param.24) | copy-start | bytes 76804
  121.3 2.5 %collective-permute-start.7 = (f32[16,96,128]{2,1,0:T(8,128)}, f32[16,96,128]{2,1,0:T(8,128)S(1)}, u32[]{:S(2)}, u32[]{:S(2)}) collective-permute-start(f32[16,96,128]{2,1,0:T(8,128)} %get-tuple-element.23), channel_id=1, source_target_pairs={{0,1},{1,0},{2,3},{3,2},{4,5},{5,4},{6,7},{7,6},{8,9},{9,8},{10,11... | collective-permute-start | bytes 2359304 | tf_op jit(solution)/shard_map/ppermute | solution.py:338
  123.8 18.5 %copy-start.9 = (f32[72,128]{1,0:T(8,128)S(1)}, f32[72,128]{1,0:T(8,128)}, u32[]{:S(2)}) copy-start(f32[72,128]{1,0:T(8,128)} %get-tuple-element.24) | copy-start | bytes 110596
  125.0 23.1 %copy-start.24 = (f32[64]{0:T(128)S(1)}, f32[64]{0:T(128)}, u32[]{:S(2)}) copy-start(f32[64]{0:T(128)} %param.30) | copy-start | bytes 772
  125.1 23.8 %copy-start.28 = (f32[64]{0:T(128)S(1)}, f32[64]{0:T(128)}, u32[]{:S(2)}) copy-start(f32[64]{0:T(128)} %param.29) | copy-start | bytes 772
  125.1 24.0 %copy-start.25 = (f32[64]{0:T(128)S(1)}, f32[64]{0:T(128)}, u32[]{:S(2)}) copy-start(f32[64]{0:T(128)} %param.32) | copy-start | bytes 772
  125.1 40.4 %copy-start.22 = (f32[47]{0:T(128)S(1)}, f32[47]{0:T(128)}, u32[]{:S(2)}) copy-start(f32[47]{0:T(128)} %param.33) | copy-start | bytes 568
  125.1 40.4 %copy-start.23 = (f32[47]{0:T(128)S(1)}, f32[47]{0:T(128)}, u32[]{:S(2)}) copy-start(f32[47]{0:T(128)} %param.31) | copy-start | bytes 568
  125.1 47.3 %copy-start.26 = (f32[100]{0:T(128)S(1)}, f32[100]{0:T(128)}, u32[]{:S(2)}) copy-start(f32[100]{0:T(128)} %param.28) | copy-start | bytes 1204
  125.2 8.8 %collective-permute-start.10 = (f32[4,96,128]{2,1,0:T(8,128)S(1)}, f32[4,96,128]{2,1,0:T(8,128)S(1)}, u32[]{:S(2)}, u32[]{:S(2)}) collective-permute-start(f32[4,96,128]{2,1,0:T(8,128)S(1)} %get-tuple-element.125), channel_id=1, source_target_pairs={{0,6},{2,4},{4,2},{6,0},{8,14},{10,12},{12,10},{14,8},{16,22},{18,... | collective-permute-start | bytes 589832 | tf_op jit(solution)/shard_map/ppermute | solution.py:334
  128.0 9.7 %collective-permute-start.8 = (f32[4,96,128]{2,1,0:T(8,128)S(1)}, f32[4,96,128]{2,1,0:T(8,128)S(1)}, u32[]{:S(2)}, u32[]{:S(2)}) collective-permute-start(f32[4,96,128]{2,1,0:T(8,128)S(1)} %get-tuple-element.124), channel_id=1, source_target_pairs={{0,2},{2,0},{4,6},{6,4},{8,10},{10,8},{12,14},{14,12},{16,18},{18,... | collective-permute-start | bytes 589832 | tf_op jit(solution)/shard_map/ppermute | solution.py:334
  128.6 9.2 %collective-permute-start.9 = (f32[4,96,128]{2,1,0:T(8,128)S(1)}, f32[4,96,128]{2,1,0:T(8,128)S(1)}, u32[]{:S(2)}, u32[]{:S(2)}) collective-permute-start(f32[4,96,128]{2,1,0:T(8,128)S(1)} %get-tuple-element.126), channel_id=1, source_target_pairs={{0,4},{2,6},{4,0},{6,2},{8,12},{10,14},{12,8},{14,10},{16,20},{18,... | collective-permute-start | bytes 589832 | tf_op jit(solution)/shard_map/ppermute | solution.py:334
  137.9 5.1 %collective-permute-start.11 = (f32[1,96,128]{2,1,0:T(8,128)S(1)}, f32[1,96,128]{2,1,0:T(8,128)S(1)}, u32[]{:S(2)}, u32[]{:S(2)}) collective-permute-start(f32[1,96,128]{2,1,0:T(8,128)S(1)} %get-tuple-element.127), channel_id=1, source_target_pairs={{0,8},{2,10},{4,12},{6,14},{8,0},{10,2},{12,4},{14,6},{16,24},{18,... | collective-permute-start | bytes 147464 | tf_op jit(solution)/shard_map/ppermute | solution.py:334
  139.4 6.0 %collective-permute-start.12 = (f32[1,96,128]{2,1,0:T(8,128)S(1)}, f32[1,96,128]{2,1,0:T(8,128)S(1)}, u32[]{:S(2)}, u32[]{:S(2)}) collective-permute-start(f32[1,96,128]{2,1,0:T(8,128)S(1)} %get-tuple-element.129), channel_id=1, source_target_pairs={{0,16},{2,18},{4,20},{6,22},{8,24},{10,26},{12,28},{14,30},{16,0},... | collective-permute-start | bytes 147464 | tf_op jit(solution)/shard_map/ppermute | solution.py:334
  141.8 5.9 %collective-permute-start.13 = (f32[1,96,128]{2,1,0:T(8,128)S(1)}, f32[1,96,128]{2,1,0:T(8,128)S(1)}, u32[]{:S(2)}, u32[]{:S(2)}) collective-permute-start(f32[1,96,128]{2,1,0:T(8,128)S(1)} %get-tuple-element.128), channel_id=1, source_target_pairs={{0,24},{2,26},{4,28},{6,30},{8,16},{10,18},{12,20},{14,22},{16,8},... | collective-permute-start | bytes 147464 | tf_op jit(solution)/shard_map/ppermute | solution.py:334
  147.8 30.4 %copy-start.5 = (f32[100,64]{0,1:T(8,128)}, f32[100,64]{0,1:T(8,128)S(1)}, u32[]{:S(2)}) copy-start(f32[100,64]{0,1:T(8,128)S(1)} %get-tuple-element.117) | copy-start | bytes 76804
  148.0 30.2 %copy-start.11 = (f32[64]{0:T(128)}, f32[64]{0:T(128)S(1)}, u32[]{:S(2)}) copy-start(f32[64]{0:T(128)S(1)} %slice_reduce_fusion) | copy-start | bytes 772
  148.8 29.4 %copy-start.10 = (f32[64]{0:T(128)}, f32[64]{0:T(128)S(1)}, u32[]{:S(2)}) copy-start(f32[64]{0:T(128)S(1)} %get-tuple-element.115) | copy-start | bytes 772
  148.9 29.3 %copy-start.14 = (f32[64]{0:T(128)}, f32[64]{0:T(128)S(1)}, u32[]{:S(2)}) copy-start(f32[64]{0:T(128)S(1)} %multiply_add_fusion.5) | copy-start | bytes 772
  149.6 28.5 %copy-start.20 = (f32[64]{0:T(128)}, f32[64]{0:T(128)S(1)}, u32[]{:S(2)}) copy-start(f32[64]{0:T(128)S(1)} %get-tuple-element.113) | copy-start | bytes 772
  154.2 10.6 %all-to-all-start.2 = ((f32[32,3,128]{2,1,0:T(4,128)}), f32[32,3,128]{2,1,0:T(4,128)S(1)}, u32[]{:S(2)}, u32[]{:S(2)}) async-start(f32[32,3,128]{2,1,0:T(4,128)} %broadcast_in_dim.17), calls=%async_computation.2 | async-start | bytes 131072 | tf_op jit(solution)/shard_map/all_to_all | solution.py:383
  166.2 12.0 %copy-start.15 = (f32[47]{0:T(128)}, f32[47]{0:T(128)S(1)}, u32[]{:S(2)}) copy-start(f32[47]{0:T(128)S(1)} %get-tuple-element.139) | copy-start | bytes 568
  166.2 12.0 %copy-start.18 = (f32[47]{0:T(128)}, f32[47]{0:T(128)S(1)}, u32[]{:S(2)}) copy-start(f32[47]{0:T(128)S(1)} %get-tuple-element.107) | copy-start | bytes 568
  166.2 12.0 %copy-start.19 = (f32[47]{0:T(128)}, f32[47]{0:T(128)S(1)}, u32[]{:S(2)}) copy-start(f32[47]{0:T(128)S(1)} %get-tuple-element.108) | copy-start | bytes 568
  173.1 5.1 %copy-start.17 = (f32[100]{0:T(128)}, f32[100]{0:T(128)S(1)}, u32[]{:S(2)}) copy-start(f32[100]{0:T(128)S(1)} %get-tuple-element.111) | copy-start | bytes 1204

commit v2 on v1

v2 whole, which is shorter than its diff:
```python
import jax
import jax.numpy as jnp
from jax import lax
from jax.experimental import pallas as pl
from jax.experimental.pallas import tpu as pltpu
from jax.sharding import PartitionSpec as P

F = 100
HCAP = 8
STEP = 20
LANES = 128
HALF = 64
GROUP = 16
NODE_BLOCK = 256
HID_BLOCK = 256
COL_BLOCK = 512

tiny_eps = 1e-30
scale_eps = 0.001
clip_limit = 1.0
step_rate = 0.3
keep_rate = 1.0 - STEP**-0.8
new_rate = STEP**-0.8
f32 = jnp.float32
bf16 = jnp.bfloat16


def dot(a, b, dims=((1,), (0,))):
    return lax.dot_general(a, b, (dims, ((), ())), preferred_element_type=f32)


def split(x):
    hi = x.astype(bf16)
    lo = (x - hi.astype(f32)).astype(bf16)
    return hi, lo


def iota(shape, dim):
    return lax.broadcasted_iota(jnp.int32, shape, dim)


def one_hot(cond):
    return jnp.where(cond, 1.0, 0.0).astype(bf16)


def picked(table, index, base=0):
    which = one_hot(iota((table.shape[1], index.shape[1]), 0) + base == index)
    both = dot(table, which)
    return both[:LANES] + both[LANES:]


def sent_rows(table, index, out_ref, micro):
    rows = picked(table, index).T
    out_ref[:, micro] = rows.reshape(out_ref.shape[0], HCAP, LANES)


def front_kernel(x_ref, send_ref, table_ref, out_ref, full):
    full[...] = jnp.where(iota(full.shape, 0) == F, 1.0, 0.0)
    for m in range(send_ref.shape[0]):
        full[:F] = x_ref[:, m, :]
        hi, lo = split(full[...])
        table_ref[m, :LANES] = hi
        table_ref[m, LANES:] = lo
        sent_rows(table_ref[m], send_ref[m], out_ref, m)


def front(x, send):
    _, micros, rows = x.shape
    peers = send.shape[2] // HCAP
    return pl.pallas_call(
        front_kernel,
        out_shape=[
            jax.ShapeDtypeStruct((micros, 2 * LANES, rows), bf16),
            jax.ShapeDtypeStruct((peers, micros, HCAP, LANES), f32),
        ],
        scratch_shapes=[pltpu.VMEM((LANES, rows), f32)],
        name="front",
    )(x, send)


def local_sum_kernel(idx_ref, mask_ref, table_ref, sum_ref, halo_ref, counts):
    rows = table_ref.shape[2]
    high = counts.shape[1] // LANES
    degree, nodes = idx_ref.shape[1:]
    groups = nodes // GROUP
    v = jnp.where(mask_ref[0] > 0, idx_ref[0], counts.shape[1])
    lane_part = iota((degree, nodes), 1) // GROUP
    row = iota((degree, nodes), 0)
    turned = v
    for d in range(1, GROUP):
        moved = pltpu.roll(pltpu.roll(v, d, 0), nodes - GROUP * d, 1)
        turned = jnp.where(lane_part == ((row - d) & (GROUP - 1)), moved, turned)
    high_part = (turned >> 7).astype(f32)
    low_part = (turned & (LANES - 1)).astype(f32)
    width = degree * GROUP
    same = (iota((GROUP, width), 1) & (GROUP - 1)) == iota((GROUP, width), 0)
    same = jnp.where(same, 1.0, 0.0).astype(bf16)
    none = jnp.zeros((GROUP, width), bf16)
    low_rows = iota((LANES, width), 0).astype(f32).astype(bf16)
    one = jnp.ones((LANES, width), bf16)
    zero = jnp.zeros((LANES, width), bf16)
    for g in range(groups):
        hi = jnp.broadcast_to(high_part[g : g + 1], (GROUP, width)).astype(bf16)
        lo = jnp.broadcast_to(low_part[g : g + 1], (LANES, width)).astype(bf16)
        left = jnp.concatenate([jnp.where(hi == h, same, none) for h in range(high)], axis=0)
        right = jnp.where(low_rows == lo, one, zero)
        found = dot(left, right, ((1,), (1,))).astype(bf16)
        for h in range(high):
            counts[g * GROUP : (g + 1) * GROUP, h * LANES : (h + 1) * LANES] = found[
                h * GROUP : (h + 1) * GROUP
            ]
    both = dot(table_ref[0], counts[:, :rows], ((1,), (1,)))
    at = pl.multiple_of(pl.program_id(0) * nodes, nodes)
    own = table_ref[0, :, pl.ds(at, nodes)].astype(f32)
    both = both + own
    sum_ref[...] = both[:LANES] + both[LANES:]
    halo_ref[...] = counts[:, rows:]


def local_sums(idx, mask, table, micro, slots):
    _, degree, rows = idx.shape
    return pl.pallas_call(
        local_sum_kernel,
        grid=(rows // NODE_BLOCK,),
        in_specs=[
            pl.BlockSpec((1, degree, NODE_BLOCK), lambda b: (micro, 0, b)),
            pl.BlockSpec((1, degree, NODE_BLOCK), lambda b: (micro, 0, b)),
            pl.BlockSpec((1, 2 * LANES, rows), lambda b: (micro, 0, 0)),
        ],
        out_specs=[
            pl.BlockSpec((LANES, NODE_BLOCK), lambda b: (0, b)),
            pl.BlockSpec((NODE_BLOCK, slots), lambda b: (b, 0)),
        ],
        out_shape=[
            jax.ShapeDtypeStruct((LANES, rows), f32),
            jax.ShapeDtypeStruct((rows, slots), bf16),
        ],
        scratch_shapes=[pltpu.VMEM((NODE_BLOCK, rows + slots), bf16)],
        name="local_sums",
    )(idx, mask, table)


def finish_kernel(*refs):
    micros = (len(refs) - 4) // 2
    sums, halos = refs[:micros], refs[micros : 2 * micros]
    arrived_ref, send_ref, table_ref, out_ref = refs[2 * micros :]
    for m in range(micros):
        hi, lo = arrived_table(arrived_ref, m, 1.0)
        counts = halos[m][...]
        total = sums[m][...] + dot(hi, counts, ((1,), (1,))) + dot(lo, counts, ((1,), (1,)))
        agg = total / total[F : F + 1]
        agg = jnp.where(iota(agg.shape, 0) == F, 1.0, agg)
        hi, lo = split(agg)
        table_ref[m, :LANES] = hi
        table_ref[m, LANES:] = lo
        sent_rows(table_ref[m], send_ref[m], out_ref, m)


def arrived_table(ref, micro, degree=None):
    slots = ref.shape[0] * HCAP
    rows = ref[:, micro].reshape(slots, LANES)
    if degree is not None:
        rows = jnp.where(iota(rows.shape, 1) == F, degree, rows)
    return split(rows.T)


def finish(sums, halos, arrived, send):
    micros = len(sums)
    rows = sums[0].shape[1]
    return pl.pallas_call(
        finish_kernel,
        out_shape=[
            jax.ShapeDtypeStruct((micros, 2 * LANES, rows), bf16),
            jax.ShapeDtypeStruct(arrived.shape, f32),
        ],
        name="finish",
    )(*sums, *halos, arrived, send)


def edge_row(pos_ref, neg_ref, micro, side):
    pos = pos_ref[micro, side : side + 1, :]
    return jnp.concatenate([pos, neg_ref[micro, side : side + 1, :]], axis=1)


def pick_kernel(pos_ref, neg_ref, table_ref, out_ref):
    count = 2 * pos_ref.shape[2]
    for m in range(pos_ref.shape[0]):
        for s in range(2):
            at = (2 * m + s) * count
            out_ref[:, at : at + count] = picked(table_ref[m], edge_row(pos_ref, neg_ref, m, s))


def pick(pos, neg, table):
    ends = pos.shape[0] * 4 * pos.shape[2]
    return pl.pallas_call(
        pick_kernel, out_shape=jax.ShapeDtypeStruct((LANES, ends), f32), name="pick"
    )(pos, neg, table)


def first_block(ref, start, shards, hs):
    return ref[pl.ds(start, shards), 0:hs, :].reshape(shards * hs, LANES)


def head_block(ref, start, shards, hs):
    if hs % GROUP:
        return ref[pl.ds(start, shards), hs : 2 * hs, :].reshape(shards * hs, LANES)
    half = hs // 2
    packed = ref[pl.ds(start, shards), hs : hs + half, :].reshape(shards * half, LANES)
    low = iota(packed.shape, 1) < HALF
    left = jnp.where(low, packed, 0.0).reshape(shards, half, LANES)
    right = jnp.where(low, pltpu.roll(packed, HALF, 1), 0.0).reshape(shards, half, LANES)
    return jnp.concatenate([left, right], axis=1).reshape(shards * hs, LANES)


def head_terms(block):
    hi = block.astype(bf16)
    rest = block - hi.astype(f32)
    return hi, (hi.astype(f32) + pltpu.roll(rest, HALF, 1)).astype(bf16)


def layers_kernel(
    part_ref, pos_ref, neg_ref, arrived_ref, mine_ref, other_ref, head_bias_ref,
    grad_mine_ref, grad_other_ref, stats_ref,
    agg_row, agg_col, hidden, out_col, dz_col, dz_row,
    *, hs, nodes, slope_scale,
):
    micros, sides, count = pos_ref.shape[0], 2, 2 * pos_ref.shape[2]
    ends = micros * sides * count
    shards = HID_BLOCK // hs
    blocks = mine_ref.shape[0] // shards

    for m in range(micros):
        far = jnp.concatenate(arrived_table(arrived_ref, m), axis=0)
        far = picked(far, edge_row(pos_ref, neg_ref, m, 1), nodes)
        for s in range(sides):
            at = (m * sides + s) * count
            cols = part_ref[:, at : at + count]
            if s == 1:
                cols = cols + far
            hi, lo = split(cols)
            agg_col[:LANES, at : at + count] = hi
            agg_col[LANES:, at : at + count] = lo
            hi, lo = split(cols.T)
            agg_row[at : at + count, :LANES] = hi
            agg_row[at : at + count, LANES:] = lo

    out_col[...] = jnp.zeros(out_col.shape, f32)

    for side, ref in enumerate((mine_ref, other_ref)):

        def forward(c, carry, ref=ref, side=side):
            first = first_block(ref, c * shards, shards, hs)
            hi, lo = split(first)
            both = jnp.concatenate([hi, lo], axis=1)
            head_hi, head_both = head_terms(head_block(ref, c * shards, shards, hs))
            head = jnp.concatenate([head_both, head_hi], axis=0)
            slot = side * blocks + c
            for n in range(0, ends, COL_BLOCK):
                cols = slice(n, n + COL_BLOCK)
                upper = agg_col[:LANES, cols]
                pre = dot(both, jnp.concatenate([upper, upper], axis=0))
                pre = pre + dot(hi, agg_col[LANES:, cols])
                act_hi, act_lo = split(jnp.maximum(pre, 0.0))
                hidden[slot, :HID_BLOCK, cols] = act_hi
                hidden[slot, HID_BLOCK:, cols] = act_lo
                act = jnp.concatenate([act_hi, act_lo], axis=0)
                out_col[:, cols] += dot(head, act, ((0,), (0,)))
            return carry

        lax.fori_loop(0, blocks, forward, 0)

    bias = head_bias_ref[...].T[:HALF, :1]
    loss = jnp.zeros((1, 1), f32)
    head_grad = jnp.zeros((HALF, 1), f32)
    sign = jnp.where(iota((1, count), 1) < count // 2, -1.0, 1.0)
    for m in range(micros):
        at = m * sides * count
        mid = at + count
        end = mid + count
        z_u = out_col[:HALF, at:mid] + out_col[HALF:, at:mid] + bias
        z_v = out_col[:HALF, mid:end] + out_col[HALF:, mid:end] + bias
        score = jnp.sum(z_u * z_v, axis=0, keepdims=True) * sign
        tail = jnp.exp(-jnp.abs(score))
        plus = jnp.maximum(score, 0.0) + jnp.log1p(tail)
        loss = loss + jnp.sum(plus, axis=1, keepdims=True)
        slope = sign * jax.nn.sigmoid(score) * slope_scale
        for start, grad in ((at, slope * z_v), (mid, slope * z_u)):
            stop = start + count
            head_grad = head_grad + jnp.sum(grad, axis=1, keepdims=True)
            hi, lo = split(grad)
            dz_col[:HALF, start:stop] = hi
            dz_col[HALF : 2 * HALF, start:stop] = hi
            dz_col[2 * HALF : 3 * HALF, start:stop] = lo
            dz_col[3 * HALF :, start:stop] = jnp.zeros((HALF, count), bf16)
            both = jnp.concatenate([hi.astype(f32), lo.astype(f32)], axis=0)
            dz_row[start:stop] = both.T.astype(bf16)
    wide = jnp.broadcast_to(head_grad, (HALF, LANES))
    wide = jnp.concatenate([wide, jnp.broadcast_to(loss, (HALF, LANES))], axis=0)
    stats_ref[...] = wide.T[:8]

    for side, (ref, grad_ref) in enumerate(((mine_ref, grad_mine_ref), (other_ref, grad_other_ref))):

        def backward(c, carry, ref=ref, grad_ref=grad_ref, side=side):
            head_hi, head_both = head_terms(head_block(ref, c * shards, shards, hs))
            head = jnp.concatenate([head_both, head_hi], axis=1)
            slot = side * blocks + c
            head_sum = jnp.zeros((HID_BLOCK, LANES), f32)
            first_sum = jnp.zeros((HID_BLOCK, LANES), f32)
            for n in range(0, ends, COL_BLOCK):
                cols = slice(n, n + COL_BLOCK)
                act_hi = hidden[slot, :HID_BLOCK, cols]
                act_lo = hidden[slot, HID_BLOCK:, cols]
                grad = dot(head, dz_col[:, cols])
                grad = jnp.where(act_hi.astype(f32) > 0.0, grad, 0.0)
                hi, lo = split(grad)
                head_sum = head_sum + dot(act_hi, dz_row[cols]) + dot(act_lo, dz_row[cols])
                both = dot(hi, agg_row[cols])
                first_sum = first_sum + both[:, :LANES] + both[:, LANES:]
                first_sum = first_sum + dot(lo, agg_row[cols, :LANES])
            grad_ref[pl.ds(c * shards, shards), 0:hs, :] = first_sum.reshape(shards, hs, LANES)
            folded = (head_sum + pltpu.roll(head_sum, HALF, 1)).reshape(shards, hs, LANES)
            if hs % GROUP:
                grad_ref[pl.ds(c * shards, shards), hs : 2 * hs, :] = folded
            else:
                half = hs // 2
                low = iota((shards, half, LANES), 2) < HALF
                grad_ref[pl.ds(c * shards, shards), hs : hs + half, :] = jnp.where(
                    low, folded[:, :half], folded[:, half:]
                )
            return carry

        lax.fori_loop(0, blocks, backward, 0)


def layers(part, pos, neg, arrived, mine, other, head_bias, hs, nodes, slope_scale):
    ends = part.shape[1]
    blocks = 2 * mine.shape[0] * hs // HID_BLOCK
    shape = jax.ShapeDtypeStruct(mine.shape, f32)
    return pl.pallas_call(
        lambda *refs: layers_kernel(*refs, hs=hs, nodes=nodes, slope_scale=slope_scale),
        out_shape=[shape, shape, jax.ShapeDtypeStruct((8, LANES), f32)],
        scratch_shapes=[
            pltpu.VMEM((ends, 2 * LANES), bf16),
            pltpu.VMEM((2 * LANES, ends), bf16),
            pltpu.VMEM((blocks, 2 * HID_BLOCK, ends), bf16),
            pltpu.VMEM((LANES, ends), f32),
            pltpu.VMEM((4 * HALF, ends), bf16),
            pltpu.VMEM((ends, LANES), bf16),
        ],
        name="layers",
    )(part, pos, neg, arrived, mine, other, head_bias)


def stages(size):
    found = []
    stride = 1
    while stride < size:
        radix = min(4, size // stride)
        found.append((stride, radix))
        stride *= radix
    return found


def trade(x, offset):
    size = lax.axis_size("dom")
    return lax.ppermute(x, "dom", [(i, i ^ offset) for i in range(size)])


def swap(x):
    return lax.ppermute(x, "rep", [(0, 1), (1, 0)])


def spread_stage(x, stride, radix):
    return jnp.concatenate([x] + [trade(x, stride * k) for k in range(1, radix)], axis=0)


def collect(mine, other):
    x = mine + swap(other)
    for stride, radix in stages(lax.axis_size("dom")):
        parts = x.reshape((radix, x.shape[0] // radix) + x.shape[1:])
        y = parts[0]
        for k in range(1, radix):
            y = y + trade(parts[k], stride * k)
        x = y
    return x[0]


def pack_shard(w_one, b_one, w_two):
    hs = b_one.shape[0]
    first = jnp.concatenate([w_one.T, b_one[:, None]], axis=1)
    first = jnp.pad(first, ((0, 0), (0, LANES - first.shape[1])))
    if hs % GROUP:
        head = jnp.pad(w_two, ((0, 0), (0, LANES - w_two.shape[1])))
    else:
        head = jnp.pad(w_two, ((0, 0), (0, HALF - w_two.shape[1])))
        head = jnp.concatenate([head[: hs // 2], head[hs // 2 :]], axis=1)
    return jnp.concatenate([first, head], axis=0)


def unpack_head(g, hs):
    head = g[hs:]
    if hs % GROUP:
        return head
    low = iota((hs // 2, LANES), 1) < HALF
    right = jnp.where(low, pltpu.roll(head, HALF, 1), 0.0)
    return jnp.concatenate([jnp.where(low, head, 0.0), right], axis=0)


def to_column(row, hs):
    wide = jnp.broadcast_to(row, (8, row.shape[1]))
    if row.shape[1] < LANES:
        wide = jnp.concatenate([wide, jnp.zeros((8, LANES - row.shape[1]), f32)], axis=1)
    return wide.T[:hs, :1]


def total(x):
    return jnp.sum(jnp.sum(x, axis=1, keepdims=True), axis=0, keepdims=True)


def stats_kernel(
    g_ref, stats_ref, w_one_ref, b_one_ref, w_two_ref, col_ref, row_ref, second_ref,
    g_one_ref, g_two_ref, g_bias_ref, col_new_ref, row_new_ref, second_new_ref,
    step_one_ref, step_two_ref, sums_ref,
):
    hs = b_one_ref.shape[1]
    classes = w_two_ref.shape[0]
    g = g_ref[...]
    one = g[:hs]
    one_t = one.T
    two = unpack_head(g, hs)
    two_t = two.T
    feature = iota((hs, LANES), 1) < F
    label = iota((hs, LANES), 1) < classes
    g_one_ref[...] = one[:, :F]
    g_two_ref[...] = two_t[:classes]
    g_bias = one_t[F : F + 1]
    g_bias_ref[...] = g_bias
    square = jnp.where(feature, one * one + tiny_eps, 0.0)
    square_t = jnp.where(iota((LANES, hs), 0) < F, one_t * one_t + tiny_eps, 0.0)
    two_square = jnp.where(label, two * two + tiny_eps, 0.0)
    two_square_t = jnp.where(iota((LANES, hs), 0) < classes, two_t * two_t + tiny_eps, 0.0)
    col_new = keep_rate * col_ref[...] + new_rate * jnp.sum(square_t, axis=0, keepdims=True)
    row_new = keep_rate * row_ref[...] + new_rate * jnp.sum(two_square_t, axis=0, keepdims=True)
    second_new = keep_rate * second_ref[...] + new_rate * (g_bias * g_bias + tiny_eps)
    col_new_ref[...] = col_new
    row_new_ref[...] = row_new
    second_new_ref[...] = second_new
    step_one = one * lax.rsqrt(to_column(col_new, hs))
    step_one = jnp.where(feature, step_one, 0.0)
    step_one_ref[...] = step_one
    step_two_ref[...] = two_t * lax.rsqrt(row_new)
    step_two = jnp.where(label, two * lax.rsqrt(to_column(row_new, hs)), 0.0)
    step_bias = g_bias * lax.rsqrt(second_new)
    w_one = w_one_ref[...]
    w_two = w_two_ref[...]
    b_one = b_one_ref[...]
    lane = iota((1, LANES), 1)
    scalars = [
        total(row_new),
        total(w_one * w_one),
        total(w_two * w_two),
        total(b_one * b_one),
        total(step_bias * step_bias),
        stats_ref[0:1, HALF : HALF + 1],
    ]
    first = jnp.sum(square, axis=0, keepdims=True)
    for i, value in enumerate(scalars):
        first = jnp.where(lane == F + 1 + i, value, first)
    head = jnp.sum(step_two * step_two, axis=0, keepdims=True)
    sums = jnp.concatenate(
        [
            first,
            jnp.sum(step_one * step_one, axis=0, keepdims=True),
            jnp.sum(two_square, axis=0, keepdims=True) + pltpu.roll(jnp.broadcast_to(head, (8, LANES)), HALF, 1)[:1],
            jnp.where(lane < HALF, stats_ref[0:1], 0.0),
        ],
        axis=0,
    )
    sums_ref[...] = jnp.broadcast_to(sums[None], sums_ref.shape)


def update_kernel(
    sums_ref, step_one_ref, step_two_ref, g_bias_ref, second_new_ref,
    w_one_ref, b_one_ref, w_two_ref, b_two_ref, row_ref, col_ref, second_ref,
    loss_ref, w_one_new_ref, row_new_ref, w_two_new_ref, col_new_ref, b_one_new_ref,
    g_head_ref, b_two_new_ref, second_new_head_ref,
    *, hidden_units, slope_scale,
):
    hs = b_one_ref.shape[1]
    classes = w_two_ref.shape[0]
    sums = jnp.sum(sums_ref[...], axis=0)
    row_total, one_total, two_total, bias_total, bias_rms, loss = [
        sums[0:1, F + 1 + i : F + 2 + i] for i in range(6)
    ]
    loss_ref[...] = loss * slope_scale
    row_new = keep_rate * row_ref[...] + new_rate * sums[0:1, :F]
    row_new_ref[...] = row_new
    col_new = keep_rate * col_ref[...] + new_rate * sums[2:3, :classes]
    col_new_ref[...] = col_new
    g_head = sums[3:4, :classes]
    g_head_ref[...] = g_head
    second = keep_rate * second_ref[...] + new_rate * (g_head * g_head + tiny_eps)
    second_new_head_ref[...] = second

    def clip(mean):
        return 1.0 / jnp.maximum(1.0, jnp.sqrt(mean) / clip_limit)

    def rate(mean):
        return step_rate * jnp.maximum(scale_eps, jnp.sqrt(mean))

    row_sum = jnp.sum(row_new, axis=1, keepdims=True)
    one_rms = jnp.sum(sums[1:2, :F] / row_new, axis=1, keepdims=True) * row_sum
    head_sums = pltpu.roll(jnp.broadcast_to(sums[2:3], (8, LANES)), HALF, 1)[:1, :classes]
    two_rms = jnp.sum(head_sums / col_new, axis=1, keepdims=True) * row_total
    one_rate = clip(one_rms / (F * hidden_units)) * rate(one_total / (F * hidden_units))
    step_one = step_one_ref[:, :F] * lax.rsqrt(row_new / row_sum)
    w_one_new_ref[...] = w_one_ref[...] - one_rate * step_one
    size = hidden_units * classes
    two_rate = clip(two_rms / size) * rate(two_total / size)
    scale = to_column(lax.rsqrt(col_new / row_total), classes)
    w_two_new_ref[...] = w_two_ref[...] - two_rate * (step_two_ref[:classes] * scale)
    bias_rate = clip(bias_rms / hidden_units) * rate(bias_total / hidden_units)
    b_one_new_ref[...] = b_one_ref[...] - bias_rate * (g_bias_ref[...] * lax.rsqrt(second_new_ref[...]))
    step_head = g_head * lax.rsqrt(second)
    b_two = b_two_ref[...]
    head_rate = clip(jnp.sum(step_head * step_head, axis=1, keepdims=True) / classes)
    head_rate = head_rate * rate(jnp.sum(b_two * b_two, axis=1, keepdims=True) / classes)
    b_two_new_ref[...] = b_two - head_rate * step_head


def local(
    features,
    neighbors,
    nbr_mask,
    send_rows,
    halo_count,
    pos_edges,
    neg_edges,
    w_one,
    b_one,
    w_two,
    b_two,
    w_one_row,
    w_one_col,
    w_two_row,
    w_two_col,
    b_one_second,
    b_two_second,
):
    peers = lax.axis_size("dom")
    ranks = lax.axis_size("rep")
    micros, rows, _ = features.shape
    classes = w_two.shape[1]
    hs = b_one.shape[0]
    slots = peers * HCAP
    total_edges = pos_edges.shape[1] * peers * micros * ranks

    x = jnp.transpose(features, (2, 0, 1))
    idx = jnp.transpose(neighbors, (0, 2, 1))
    mask = jnp.transpose(nbr_mask, (0, 2, 1))
    pos = jnp.transpose(pos_edges, (0, 2, 1))
    neg = jnp.transpose(neg_edges, (0, 2, 1))
    send = jnp.where(jnp.arange(HCAP) < halo_count[..., None], send_rows, -1)
    send = send.reshape(micros, 1, slots)
    slope_scale = 1.0 / (2.0 * total_edges)

    def exchange(sent):
        return lax.all_to_all(sent, "dom", 0, 0, tiled=True)

    table, sent = front(x, send)
    arrived_x = exchange(sent)
    weights = pack_shard(w_one, b_one, w_two)[None]
    sums, halos = [], []
    turns = list(reversed(stages(peers)))
    for m in range(micros):
        if m < len(turns):
            weights = spread_stage(weights, *turns[m])
        total_rows, halo = local_sums(idx, mask, table, m, slots)
        if m + 1 < len(turns):
            total_rows, weights, table = lax.optimization_barrier((total_rows, weights, table))
        sums.append(total_rows)
        halos.append(halo)
    for turn in turns[micros:]:
        weights = spread_stage(weights, *turn)
    other = swap(weights)
    table, sent = finish(sums, halos, arrived_x, send)
    arrived_agg = exchange(sent)
    part = pick(pos, neg, table)
    head_bias = jnp.broadcast_to(jnp.pad(b_two, (0, LANES - classes)), (8, LANES))
    grad_mine, grad_other, stats = layers(
        part, pos, neg, arrived_agg, weights, other, head_bias, hs, rows, slope_scale
    )
    g = collect(grad_mine, grad_other)

    w_one_t = w_one.T
    w_two_t = w_two.T
    b_one_row = b_one[None]

    def out(*shape):
        return jax.ShapeDtypeStruct(shape, f32)

    vec = out(1, hs)
    count = peers * ranks
    g_one, g_two, g_bias, col_one, row_two, second_one, step_one, step_two, parts = pl.pallas_call(
        stats_kernel,
        out_shape=[
            out(hs, F), out(classes, hs), vec, vec, vec, vec,
            out(hs, LANES), out(LANES, hs), out(count, 4, LANES),
        ],
        name="stats",
    )(g, stats, w_one_t, b_one_row, w_two_t, w_one_col[None], w_two_row[None], b_one_second[None])
    parts = lax.all_to_all(parts, ("dom", "rep"), 0, 0, tiled=True)
    head = out(1, classes)
    loss, w_one_new, row_one, w_two_new, col_two, b_one_new, g_head, b_two_new, second_two = pl.pallas_call(
        lambda *refs: update_kernel(
            *refs, hidden_units=hs * count, slope_scale=slope_scale
        ),
        out_shape=[
            out(1, 1), out(hs, F), out(1, F), out(classes, hs), head, vec, head, head, head,
        ],
        name="update",
    )(
        parts, step_one, step_two, g_bias, second_one,
        w_one_t, b_one_row, w_two_t, b_two[None], w_one_row[None], w_two_col[None], b_two_second[None],
    )
    return (
        loss[0, 0],
        g_one.T,
        w_one_new.T,
        row_one[0],
        col_one[0],
        g_two.T,
        w_two_new.T,
        row_two[0],
        col_two[0],
        g_bias[0],
        b_one_new[0],
        second_one[0],
        g_head[0],
        b_two_new[0],
        second_two[0],
    )


def solution(mesh):
    return jax.shard_map(
        local,
        mesh=mesh,
        in_specs=(
            P("rep", "dom", None),
            P("rep", "dom", None),
            P("rep", "dom", None),
            P("rep", "dom", None),
            P("rep", "dom"),
            P("rep", "dom", None),
            P("rep", "dom", None),
            P(None, ("dom", "rep")),
            P(("dom", "rep")),
            P(("dom", "rep"), None),
            P(),
            P(),
            P(("dom", "rep")),
            P(("dom", "rep")),
            P(),
            P(("dom", "rep")),
            P(),
        ),
        out_specs=(
            P(),
            P(None, ("dom", "rep")),
            P(None, ("dom", "rep")),
            P(),
            P(("dom", "rep")),
            P(("dom", "rep"), None),
            P(("dom", "rep"), None),
            P(("dom", "rep")),
            P(),
            P(("dom", "rep")),
            P(("dom", "rep")),
            P(("dom", "rep")),
            P(),
            P(),
            P(),
        ),
        check_vma=False,
    )
```

time: 180 us -> 153 us (0.85)
  local copies, waits for them, and re-layouts: 26.8 us -> 4.02 us
  blocking collectives: 0 us -> 10.8 us
  Pallas kernels: 68.3 us -> 78.8 us
  other arithmetic: 13.3 us -> 3.53 us
  between operations: 9.74 us -> 0.93 us
  waiting for transfers between devices: 28.3 us -> 24.5 us
  starting transfers between devices: 32.9 us -> 30.1 us
    all_to_all x0 -> x1, blocking collectives: none -> 10.8 us  [local(): parts = lax.all_to_all(parts, ('dom', 'rep'), 0, 0, tiled=True)]
    pallas_call x4 -> x8, Pallas kernels: 68.3 us -> 78.8 us  [the longest x1 30.7 us: layers(): pl.pallas_call(lambda *refs: layers_kernel(*refs, hs=hs, nodes=nodes, slo...]
    unnamed x69 -> x14, local copies, waits for them, and re-layouts: 8.84 us -> 1.82 us
    all_to_all x1 -> x0, waiting for transfers between devices: 6.11 us -> none  [global_sum(): lax.all_to_all(x, ('dom', 'rep'), 0, 0, tiled=True)]
    reduce_sum x13 -> x0, other arithmetic: 5.44 us -> none  [the longest x1 0.68 us: local(): step_head = clip(step_head, jnp.mean(step_head * step_head))]
    concatenate x2 -> x1, local copies, waits for them, and re-layouts: 3.98 us -> 0.02 us  [spread_stage(): jnp.concatenate([x] + [trade(x, stride * k) for k in range(1, radix)], ax...]
    sub x5 -> x0, other arithmetic: 3.15 us -> none  [the longest x4 3.13 us: moved(): return old - step_rate * jnp.maximum(scale_eps, jnp.sqrt(mean)) * step]
    all_to_all x1 -> x0, starting transfers between devices: 3.14 us -> none  [global_sum(): lax.all_to_all(x, ('dom', 'rep'), 0, 0, tiled=True)]
  transfers between devices with their start and end apart: 17 -> 16, of which waited for: 8 -> 8; matrix products, arithmetic and copies ran while one was open for 11% -> 1% of each run, Pallas kernels for 21% -> 29%
where the time goes in v2:
time: 153 us
  Pallas kernels  78.8 us (52%)
  starting transfers between devices  30.1 us (20%)
  waiting for transfers between devices  24.5 us (16%)
  blocking collectives  10.8 us (7%)
  local copies, waits for them, and re-layouts  4.02 us (3%)
  other arithmetic  3.53 us (2%)
    pallas_call x1, Pallas kernels, layers(): pl.pallas_call(lambda *refs: layers_kernel(*refs, hs=hs, nodes=nodes, slo...  30.7 us
    pallas_call x2, Pallas kernels, local_sums(): pl.pallas_call(local_sum_kernel, grid=(rows // NODE_BLOCK,), in_specs=[pl...  30.6 us
    ppermute x12, waiting for transfers between devices, trade(): return lax.ppermute(x, 'dom', [(i, i ^ offset) for i in range(size)])  19.3 us
    ppermute x12, starting transfers between devices, trade(): return lax.ppermute(x, 'dom', [(i, i ^ offset) for i in range(size)])  17.3 us
    all_to_all x2, starting transfers between devices, exchange(): return lax.all_to_all(sent, 'dom', 0, 0, tiled=True)  12.7 us
    all_to_all x1, blocking collectives, local(): parts = lax.all_to_all(parts, ('dom', 'rep'), 0, 0, tiled=True)  10.8 us
    pallas_call x1, Pallas kernels, pick(): pl.pallas_call(pick_kernel, out_shape=jax.ShapeDtypeStruct((LANES, ends),...  5.03 us
    pallas_call x1, Pallas kernels, finish(): pl.pallas_call(finish_kernel, out_shape=[jax.ShapeDtypeStruct((micros, 2...  4.69 us
  transfers between devices with their start and end apart: 16, of which 8 were waited for; matrix products, arithmetic and copies ran while one was open for 1% of the time, Pallas kernels for 29%

profile of v2, /device:TPU:0, one launch (start us, length us, event | category | flops | bytes accessed | tf_op | source)
XLA Modules:
  0.0 152.7 jit_solution(8590175861663718886)
XLA Ops:
  0.6 0.8 copy.38
  1.5 0.7 copy.37
  2.2 0.8 select_maximum_fusion
  3.1 0.1 maximum_bitcast_fusion
  3.1 5.1 %collective-permute-start.2 = (f32[1,96,128]{2,1,0:T(8,128)S(1)}, f32[1,96,128]{2,1,0:T(8,128)S(1)}, u32[]{:S(2)}, u32[]{:S(2)}) collective-permute-start(f32[1,96,128]{2,1,0:T(8,128)S(1)} %maximum_bitcast_fusion), channel_id=1, source_target_pairs={{0,24},{2,26},{4,28},{6,30},{8,16},{10,18},{12,20},{14,22},{16,8},... | collective-permute-start | bytes 147464 | tf_op jit(solution)/shard_map/ppermute | solution.py:366
  8.2 0.0 collective-permute-start.1
  8.2 0.6 collective-permute-start
  8.9 0.7 fusion.5
  9.6 0.1 copy.35
  9.6 0.7 reshape.52
  10.3 3.8 %front.1 = (bf16[2,256,2048]{2,1,0:T(8,128)(2,1)}, f32[16,2,8,128]{3,2,1,0:T(8,128)}) custom-call(f32[100,2,2048]{2,1,0:T(2,128)} %bitcast.36, s32[2,1,128]{2,1,0:T(1,128)} %bitcast.50), custom_call_target="tpu_custom_call" | custom-call | tf_op jit(solution)/shard_map/front/pallas_call | solution.py:70
  14.1 15.3 %local_sums.2 = (f32[128,2048]{1,0:T(8,128)}, bf16[2048,128]{1,0:T(8,128)(2,1)}) custom-call(s32[2,16,2048]{2,1,0:T(8,128)} %bitcast.37, s32[2,16,2048]{2,1,0:T(8,128)} %bitcast.39, bf16[2,256,2048]{2,1,0:T(8,128)(2,1)} %get-tuple-element.50.table_ref), custom_call_target="tpu_custom_call" | custom-call | tf_op jit(solution)/shard_map/local_sums/pallas_call | solution.py:122
  29.4 0.0 collective-permute-done.2
  29.4 0.0 collective-permute-done.1
  29.4 0.0 collective-permute-done
  29.4 1.7 %collective-permute-start.3 = (f32[4,96,128]{2,1,0:T(8,128)S(1)}, f32[4,96,128]{2,1,0:T(8,128)S(1)}, u32[]{:S(2)}, u32[]{:S(2)}) collective-permute-start(f32[4,96,128]{2,1,0:T(8,128)S(1)} %pad_maximum_fusion), channel_id=1, source_target_pairs={{0,2},{2,0},{4,6},{6,4},{8,10},{10,8},{12,14},{14,12},{16,18},{18,... | collective-permute-start | bytes 589832 | tf_op jit(solution)/shard_map/ppermute | solution.py:366
  31.1 1.5 collective-permute-start.4
  32.6 0.3 collective-permute-start.5
  33.0 4.3 %collective-permute-done.3 = f32[4,96,128]{2,1,0:T(8,128)S(1)} collective-permute-done((f32[4,96,128]{2,1,0:T(8,128)S(1)}, f32[4,96,128]{2,1,0:T(8,128)S(1)}, u32[]{:S(2)}, u32[]{:S(2)}) %collective-permute-start.3) | collective-permute-done | bytes 196640 | tf_op jit(solution)/shard_map/ppermute | solution.py:366
  37.3 3.7 %collective-permute-done.4 = f32[4,96,128]{2,1,0:T(8,128)S(1)} collective-permute-done((f32[4,96,128]{2,1,0:T(8,128)S(1)}, f32[4,96,128]{2,1,0:T(8,128)S(1)}, u32[]{:S(2)}, u32[]{:S(2)}) %collective-permute-start.4) | collective-permute-done | bytes 196640 | tf_op jit(solution)/shard_map/ppermute | solution.py:366
  41.0 0.0 collective-permute-done.5
  41.1 0.0 copy-start
  41.1 0.1 collective-permute-start.6
  41.1 5.8 %all-to-all-start = ((f32[16,2,8,128]{3,2,1,0:T(8,128)}), f32[16,2,8,128]{3,2,1,0:T(8,128)S(1)}, u32[]{:S(2)}, u32[]{:S(2)}) async-start(f32[16,2,8,128]{3,2,1,0:T(8,128)} %get-tuple-element.54), calls=%async_computation | async-start | bytes 262144 | tf_op jit(solution)/shard_map/all_to_all | solution.py:568
  47.0 15.3 %local_sums.3 = (f32[128,2048]{1,0:T(8,128)}, bf16[2048,128]{1,0:T(8,128)(2,1)}) custom-call(s32[2,16,2048]{2,1,0:T(8,128)} %bitcast.38, s32[2,16,2048]{2,1,0:T(8,128)} %bitcast.40, bf16[2,256,2048]{2,1,0:T(8,128)(2,1)} %get-tuple-element.50.table_ref), custom_call_target="tpu_custom_call" | custom-call | tf_op jit(solution)/shard_map/local_sums/pallas_call | solution.py:122
  62.3 0.0 copy-start.4
  62.3 0.0 all-to-all-done.refs_4_
  62.3 0.0 copy-start.2
  62.3 0.7 copy-done.2
  62.9 4.7 %finish.1 = (bf16[2,256,2048]{2,1,0:T(8,128)(2,1)}, f32[16,2,8,128]{3,2,1,0:T(8,128)}) custom-call(f32[128,2048]{1,0:T(8,128)} %get-tuple-element.49.refs_0_, f32[128,2048]{1,0:T(8,128)} %get-tuple-element.51.refs_1_, bf16[2048,128]{1,0:T(8,128)(2,1)} %get-tuple-element.52.refs_2_, bf16[2048,128]{1,0:T(8,128)(2,1)} %get-tuple-element.53.refs_3_, ...), custom_call_target="tpu_custom_call" | custom-call | tf_op jit(solution)/shard_map/finish/pallas_call | solution.py:170
  67.6 0.0 copy-done
  67.6 6.9 %all-to-all-start.1 = ((f32[16,2,8,128]{3,2,1,0:T(8,128)}), f32[16,2,8,128]{3,2,1,0:T(8,128)S(1)}, u32[]{:S(2)}, u32[]{:S(2)}) async-start(f32[16,2,8,128]{3,2,1,0:T(8,128)} %get-tuple-element.56), calls=%async_computation.1 | async-start | bytes 262144 | tf_op jit(solution)/shard_map/all_to_all | solution.py:568
  74.5 0.0 copy-done.4
  74.6 5.0 %pick.1.refs_0_ = f32[128,2048]{1,0:T(8,128)} custom-call(s32[2,2,256]{2,1,0:T(2,128)} %bitcast.46, s32[2,2,256]{2,1,0:T(2,128)} %bitcast.48, bf16[2,256,2048]{2,1,0:T(8,128)(2,1)} %get-tuple-element.55.table_ref), custom_call_target="tpu_custom_call" | custom-call | tf_op jit(solution)/shard_map/pick/pallas_call | solution.py:195
  79.6 2.7 %all-to-all-done.1.refs_3_ = f32[16,2,8,128]{3,2,1,0:T(8,128)S(1)} async-done(((f32[16,2,8,128]{3,2,1,0:T(8,128)}), f32[16,2,8,128]{3,2,1,0:T(8,128)S(1)}, u32[]{:S(2)}, u32[]{:S(2)}) %all-to-all-start.1) | async-done | bytes 131104 | tf_op jit(solution)/shard_map/all_to_all | solution.py:568
  82.3 0.0 copy-start.3
  82.3 0.0 collective-permute-done.6.refs_5_
  82.3 0.0 copy-start.1
  82.3 0.6 broadcast_in_dim.42.refs_6_
  83.0 0.0 copy-done.3
  83.0 0.3 copy-done.1
  83.3 30.7 %layers.1 = (f32[16,96,128]{2,1,0:T(8,128)}, f32[16,96,128]{2,1,0:T(8,128)}, f32[8,128]{1,0:T(8,128)}) custom-call(f32[128,2048]{1,0:T(8,128)} %pick.1.refs_0_, s32[2,2,256]{2,1,0:T(2,128)} %bitcast.47, s32[2,2,256]{2,1,0:T(2,128)} %bitcast.49, f32[16,2,8,128]{3,2,1,0:T(8,128)} %copy-done.3, f32[16,96,128]{2,1,0:T(8,128)} %copy-done, ...), custom_call_target="tpu_custom_call" | custom-call | tf_op jit(solution)/shard_map/layers/pallas_call | solution.py:339
  114.0 0.0 collective-permute-start.7
  114.0 2.5 %collective-permute-done.7 = f32[16,96,128]{2,1,0:T(8,128)S(1)} collective-permute-done((f32[16,96,128]{2,1,0:T(8,128)}, f32[16,96,128]{2,1,0:T(8,128)S(1)}, u32[]{:S(2)}, u32[]{:S(2)}) %collective-permute-start.7) | collective-permute-done | bytes 786464 | tf_op jit(solution)/shard_map/ppermute | solution.py:370
  116.5 1.2 add.27
  117.8 0.8 collective-permute-start.10
  118.6 1.8 %collective-permute-start.9 = (f32[4,96,128]{2,1,0:T(8,128)S(1)}, f32[4,96,128]{2,1,0:T(8,128)S(1)}, u32[]{:S(2)}, u32[]{:S(2)}) collective-permute-start(f32[4,96,128]{2,1,0:T(8,128)S(1)} %get-tuple-element.81), channel_id=1, source_target_pairs={{0,4},{2,6},{4,0},{6,2},{8,12},{10,14},{12,8},{14,10},{16,20},{18,... | collective-permute-start | bytes 589832 | tf_op jit(solution)/shard_map/ppermute | solution.py:366
  120.4 0.9 collective-permute-start.8
  121.4 5.2 %collective-permute-done.10 = f32[4,96,128]{2,1,0:T(8,128)S(1)} collective-permute-done((f32[4,96,128]{2,1,0:T(8,128)S(1)}, f32[4,96,128]{2,1,0:T(8,128)S(1)}, u32[]{:S(2)}, u32[]{:S(2)}) %collective-permute-start.10) | collective-permute-done | bytes 196640 | tf_op jit(solution)/shard_map/ppermute | solution.py:366
  126.6 3.0 %collective-permute-done.9 = f32[4,96,128]{2,1,0:T(8,128)S(1)} collective-permute-done((f32[4,96,128]{2,1,0:T(8,128)S(1)}, f32[4,96,128]{2,1,0:T(8,128)S(1)}, u32[]{:S(2)}, u32[]{:S(2)}) %collective-permute-start.9) | collective-permute-done | bytes 196640 | tf_op jit(solution)/shard_map/ppermute | solution.py:366
  129.6 0.0 collective-permute-done.8
  129.6 0.1 fusion.1
  129.6 1.7 %collective-permute-start.13 = (f32[1,96,128]{2,1,0:T(8,128)S(1)}, f32[1,96,128]{2,1,0:T(8,128)S(1)}, u32[]{:S(2)}, u32[]{:S(2)}) collective-permute-start(f32[1,96,128]{2,1,0:T(8,128)S(1)} %get-tuple-element.83), channel_id=1, source_target_pairs={{0,24},{2,26},{4,28},{6,30},{8,16},{10,18},{12,20},{14,22},{16,8},... | collective-permute-start | bytes 147464 | tf_op jit(solution)/shard_map/ppermute | solution.py:366
  131.4 0.5 collective-permute-start.12
  131.9 2.2 %collective-permute-start.11 = (f32[1,96,128]{2,1,0:T(8,128)S(1)}, f32[1,96,128]{2,1,0:T(8,128)S(1)}, u32[]{:S(2)}, u32[]{:S(2)}) collective-permute-start(f32[1,96,128]{2,1,0:T(8,128)S(1)} %get-tuple-element.82), channel_id=1, source_target_pairs={{0,8},{2,10},{4,12},{6,14},{8,0},{10,2},{12,4},{14,6},{16,24},{18,... | collective-permute-start | bytes 147464 | tf_op jit(solution)/shard_map/ppermute | solution.py:366
  134.1 1.5 collective-permute-done.13
  135.6 1.5 %collective-permute-done.12 = f32[1,96,128]{2,1,0:T(8,128)S(1)} collective-permute-done((f32[1,96,128]{2,1,0:T(8,128)S(1)}, f32[1,96,128]{2,1,0:T(8,128)S(1)}, u32[]{:S(2)}, u32[]{:S(2)}) %collective-permute-start.12) | collective-permute-done | bytes 49184 | tf_op jit(solution)/shard_map/ppermute | solution.py:366
  137.1 0.0 collective-permute-done.11
  137.1 0.6 fusion.4.g_ref
  137.8 2.0 %stats.1 = (f32[64,100]{1,0:T(8,128)}, f32[47,64]{1,0:T(8,128)}, f32[1,64]{1,0:T(1,128)}, f32[1,64]{1,0:T(1,128)}, f32[1,64]{1,0:T(1,128)}, /*index=5*/f32[1,64]...) custom-call(f32[96,128]{1,0:T(8,128)} %fusion.4.g_ref, f32[8,128]{1,0:T(8,128)} %get-tuple-element.60.stats_ref, ...), custom_call_target="tpu_custom_call" | custom-call | tf_op jit(solution)/shard_map/stats/pallas_call | solution.py:604
  139.7 10.8 %all_to_all.15.refs_0_ = f32[32,4,128]{2,1,0:T(4,128)} all-to-all(f32[32,4,128]{2,1,0:T(4,128)} %get-tuple-element.61), channel_id=1, replica_groups=mesh['dom'=16,'rep'=2] {'dom','rep'}, dimensions={0} | all-to-all | bytes 131072 | tf_op jit(solution)/shard_map/all_to_all | solution.py:612
  150.6 2.0 %update.1 = (f32[1,1]{1,0:T(1,128)}, f32[64,100]{1,0:T(8,128)}, f32[1,100]{1,0:T(1,128)}, f32[47,64]{1,0:T(8,128)}, f32[1,47]{1,0:T(1,128)}, /*index=5*/f32[1,64...) custom-call(f32[32,4,128]{2,1,0:T(4,128)} %all_to_all.15.refs_0_, f32[64,128]{1,0:T(8,128)} %get-tuple-element.62.refs_1_, ...), custom_call_target="tpu_custom_call" | custom-call | tf_op jit(solution)/shard_map/update/pallas_call | solution.py:614
  (9 shorter events, 0.1 us)
Async XLA Ops:
  3.1 26.2 %collective-permute-start.2 = (f32[1,96,128]{2,1,0:T(8,128)S(1)}, f32[1,96,128]{2,1,0:T(8,128)S(1)}, u32[]{:S(2)}, u32[]{:S(2)}) collective-permute-start(f32[1,96,128]{2,1,0:T(8,128)S(1)} %maximum_bitcast_fusion), channel_id=1, source_target_pairs={{0,24},{2,26},{4,28},{6,30},{8,16},{10,18},{12,20},{14,22},{16,8},... | collective-permute-start | bytes 147464 | tf_op jit(solution)/shard_map/ppermute | solution.py:366
  8.2 21.2 %collective-permute-start.1 = (f32[1,96,128]{2,1,0:T(8,128)S(1)}, f32[1,96,128]{2,1,0:T(8,128)S(1)}, u32[]{:S(2)}, u32[]{:S(2)}) collective-permute-start(f32[1,96,128]{2,1,0:T(8,128)S(1)} %maximum_bitcast_fusion), channel_id=1, source_target_pairs={{0,16},{2,18},{4,20},{6,22},{8,24},{10,26},{12,28},{14,30},{16,0},... | collective-permute-start | bytes 147464 | tf_op jit(solution)/shard_map/ppermute | solution.py:366
  8.2 21.2 %collective-permute-start = (f32[1,96,128]{2,1,0:T(8,128)S(1)}, f32[1,96,128]{2,1,0:T(8,128)S(1)}, u32[]{:S(2)}, u32[]{:S(2)}) collective-permute-start(f32[1,96,128]{2,1,0:T(8,128)S(1)} %maximum_bitcast_fusion), channel_id=1, source_target_pairs={{0,8},{2,10},{4,12},{6,14},{8,0},{10,2},{12,4},{14,6},{16,24},{18,... | collective-permute-start | bytes 147464 | tf_op jit(solution)/shard_map/ppermute | solution.py:366
  29.4 7.8 %collective-permute-start.3 = (f32[4,96,128]{2,1,0:T(8,128)S(1)}, f32[4,96,128]{2,1,0:T(8,128)S(1)}, u32[]{:S(2)}, u32[]{:S(2)}) collective-permute-start(f32[4,96,128]{2,1,0:T(8,128)S(1)} %pad_maximum_fusion), channel_id=1, source_target_pairs={{0,2},{2,0},{4,6},{6,4},{8,10},{10,8},{12,14},{14,12},{16,18},{18,... | collective-permute-start | bytes 589832 | tf_op jit(solution)/shard_map/ppermute | solution.py:366
  31.1 9.9 %collective-permute-start.4 = (f32[4,96,128]{2,1,0:T(8,128)S(1)}, f32[4,96,128]{2,1,0:T(8,128)S(1)}, u32[]{:S(2)}, u32[]{:S(2)}) collective-permute-start(f32[4,96,128]{2,1,0:T(8,128)S(1)} %pad_maximum_fusion), channel_id=1, source_target_pairs={{0,4},{2,6},{4,0},{6,2},{8,12},{10,14},{12,8},{14,10},{16,20},{18,... | collective-permute-start | bytes 589832 | tf_op jit(solution)/shard_map/ppermute | solution.py:366
  32.6 8.4 %collective-permute-start.5 = (f32[4,96,128]{2,1,0:T(8,128)S(1)}, f32[4,96,128]{2,1,0:T(8,128)S(1)}, u32[]{:S(2)}, u32[]{:S(2)}) collective-permute-start(f32[4,96,128]{2,1,0:T(8,128)S(1)} %pad_maximum_fusion), channel_id=1, source_target_pairs={{0,6},{2,4},{4,2},{6,0},{8,14},{10,12},{12,10},{14,8},{16,22},{18,... | collective-permute-start | bytes 589832 | tf_op jit(solution)/shard_map/ppermute | solution.py:366
  41.1 26.6 %copy-start = (f32[16,96,128]{2,1,0:T(8,128)}, f32[16,96,128]{2,1,0:T(8,128)S(1)}, u32[]{:S(2)}) copy-start(f32[16,96,128]{2,1,0:T(8,128)S(1)} %constant_dynamic-update-slice_fusion.refs_4_) | copy-start | bytes 2359300
  41.1 41.3 %collective-permute-start.6 = (f32[16,96,128]{2,1,0:T(8,128)S(1)}, f32[16,96,128]{2,1,0:T(8,128)S(1)}, u32[]{:S(2)}, u32[]{:S(2)}) collective-permute-start(f32[16,96,128]{2,1,0:T(8,128)S(1)} %constant_dynamic-update-slice_fusion.refs_4_), channel_id=1, source_target_pairs={{0,1},{1,0},{2,3},{3,2},{4,5},{5,4},{6,7},{7,6},{8,9},{9,8},{10,11... | collective-permute-start | bytes 2359304 | tf_op jit(solution)/shard_map/ppermute | solution.py:370
  41.1 21.1 %all-to-all-start = ((f32[16,2,8,128]{3,2,1,0:T(8,128)}), f32[16,2,8,128]{3,2,1,0:T(8,128)S(1)}, u32[]{:S(2)}, u32[]{:S(2)}) async-start(f32[16,2,8,128]{3,2,1,0:T(8,128)} %get-tuple-element.54), calls=%async_computation | async-start | bytes 262144 | tf_op jit(solution)/shard_map/all_to_all | solution.py:568
  62.3 12.3 %copy-start.4 = (f32[47]{0:T(128)S(1)}, f32[47]{0:T(128)}, u32[]{:S(2)}) copy-start(f32[47]{0:T(128)} %param.27) | copy-start | bytes 568
  62.3 0.7 copy-start.2
  67.6 14.7 %all-to-all-start.1 = ((f32[16,2,8,128]{3,2,1,0:T(8,128)}), f32[16,2,8,128]{3,2,1,0:T(8,128)S(1)}, u32[]{:S(2)}, u32[]{:S(2)}) async-start(f32[16,2,8,128]{3,2,1,0:T(8,128)} %get-tuple-element.56), calls=%async_computation.1 | async-start | bytes 262144 | tf_op jit(solution)/shard_map/all_to_all | solution.py:568
  82.3 0.7 copy-start.3
  82.3 0.9 copy-start.1
  114.0 2.5 %collective-permute-start.7 = (f32[16,96,128]{2,1,0:T(8,128)}, f32[16,96,128]{2,1,0:T(8,128)S(1)}, u32[]{:S(2)}, u32[]{:S(2)}) collective-permute-start(f32[16,96,128]{2,1,0:T(8,128)} %get-tuple-element.59), channel_id=1, source_target_pairs={{0,1},{1,0},{2,3},{3,2},{4,5},{5,4},{6,7},{7,6},{8,9},{9,8},{10,11... | collective-permute-start | bytes 2359304 | tf_op jit(solution)/shard_map/ppermute | solution.py:370
  117.8 8.8 %collective-permute-start.10 = (f32[4,96,128]{2,1,0:T(8,128)S(1)}, f32[4,96,128]{2,1,0:T(8,128)S(1)}, u32[]{:S(2)}, u32[]{:S(2)}) collective-permute-start(f32[4,96,128]{2,1,0:T(8,128)S(1)} %get-tuple-element.80), channel_id=1, source_target_pairs={{0,6},{2,4},{4,2},{6,0},{8,14},{10,12},{12,10},{14,8},{16,22},{18,... | collective-permute-start | bytes 589832 | tf_op jit(solution)/shard_map/ppermute | solution.py:366
  118.6 11.0 %collective-permute-start.9 = (f32[4,96,128]{2,1,0:T(8,128)S(1)}, f32[4,96,128]{2,1,0:T(8,128)S(1)}, u32[]{:S(2)}, u32[]{:S(2)}) collective-permute-start(f32[4,96,128]{2,1,0:T(8,128)S(1)} %get-tuple-element.81), channel_id=1, source_target_pairs={{0,4},{2,6},{4,0},{6,2},{8,12},{10,14},{12,8},{14,10},{16,20},{18,... | collective-permute-start | bytes 589832 | tf_op jit(solution)/shard_map/ppermute | solution.py:366
  120.4 9.1 %collective-permute-start.8 = (f32[4,96,128]{2,1,0:T(8,128)S(1)}, f32[4,96,128]{2,1,0:T(8,128)S(1)}, u32[]{:S(2)}, u32[]{:S(2)}) collective-permute-start(f32[4,96,128]{2,1,0:T(8,128)S(1)} %get-tuple-element.79), channel_id=1, source_target_pairs={{0,2},{2,0},{4,6},{6,4},{8,10},{10,8},{12,14},{14,12},{16,18},{18,... | collective-permute-start | bytes 589832 | tf_op jit(solution)/shard_map/ppermute | solution.py:366
  129.6 6.0 %collective-permute-start.13 = (f32[1,96,128]{2,1,0:T(8,128)S(1)}, f32[1,96,128]{2,1,0:T(8,128)S(1)}, u32[]{:S(2)}, u32[]{:S(2)}) collective-permute-start(f32[1,96,128]{2,1,0:T(8,128)S(1)} %get-tuple-element.83), channel_id=1, source_target_pairs={{0,24},{2,26},{4,28},{6,30},{8,16},{10,18},{12,20},{14,22},{16,8},... | collective-permute-start | bytes 147464 | tf_op jit(solution)/shard_map/ppermute | solution.py:366
  131.4 5.7 %collective-permute-start.12 = (f32[1,96,128]{2,1,0:T(8,128)S(1)}, f32[1,96,128]{2,1,0:T(8,128)S(1)}, u32[]{:S(2)}, u32[]{:S(2)}) collective-permute-start(f32[1,96,128]{2,1,0:T(8,128)S(1)} %get-tuple-element.84), channel_id=1, source_target_pairs={{0,16},{2,18},{4,20},{6,22},{8,24},{10,26},{12,28},{14,30},{16,0},... | collective-permute-start | bytes 147464 | tf_op jit(solution)/shard_map/ppermute | solution.py:366
  131.9 5.2 %collective-permute-start.11 = (f32[1,96,128]{2,1,0:T(8,128)S(1)}, f32[1,96,128]{2,1,0:T(8,128)S(1)}, u32[]{:S(2)}, u32[]{:S(2)}) collective-permute-start(f32[1,96,128]{2,1,0:T(8,128)S(1)} %get-tuple-element.82), channel_id=1, source_target_pairs={{0,8},{2,10},{4,12},{6,14},{8,0},{10,2},{12,4},{14,6},{16,24},{18,... | collective-permute-start | bytes 147464 | tf_op jit(solution)/shard_map/ppermute | solution.py:366

commit v3 on v2

--- a/solution.py
+++ b/solution.py
@@ -11,7 +11,6 @@
 LANES = 128
 HALF = 64
 GROUP = 16
-NODE_BLOCK = 256
 HID_BLOCK = 256
 COL_BLOCK = 512
 
@@ -78,103 +77,12 @@
     )(x, send)
 
 
-def local_sum_kernel(idx_ref, mask_ref, table_ref, sum_ref, halo_ref, counts):
-    rows = table_ref.shape[2]
-    high = counts.shape[1] // LANES
-    degree, nodes = idx_ref.shape[1:]
-    groups = nodes // GROUP
-    v = jnp.where(mask_ref[0] > 0, idx_ref[0], counts.shape[1])
-    lane_part = iota((degree, nodes), 1) // GROUP
-    row = iota((degree, nodes), 0)
-    turned = v
-    for d in range(1, GROUP):
-        moved = pltpu.roll(pltpu.roll(v, d, 0), nodes - GROUP * d, 1)
-        turned = jnp.where(lane_part == ((row - d) & (GROUP - 1)), moved, turned)
-    high_part = (turned >> 7).astype(f32)
-    low_part = (turned & (LANES - 1)).astype(f32)
-    width = degree * GROUP
-    same = (iota((GROUP, width), 1) & (GROUP - 1)) == iota((GROUP, width), 0)
-    same = jnp.where(same, 1.0, 0.0).astype(bf16)
-    none = jnp.zeros((GROUP, width), bf16)
-    low_rows = iota((LANES, width), 0).astype(f32).astype(bf16)
-    one = jnp.ones((LANES, width), bf16)
-    zero = jnp.zeros((LANES, width), bf16)
-    for g in range(groups):
-        hi = jnp.broadcast_to(high_part[g : g + 1], (GROUP, width)).astype(bf16)
-        lo = jnp.broadcast_to(low_part[g : g + 1], (LANES, width)).astype(bf16)
-        left = jnp.concatenate([jnp.where(hi == h, same, none) for h in range(high)], axis=0)
-        right = jnp.where(low_rows == lo, one, zero)
-        found = dot(left, right, ((1,), (1,))).astype(bf16)
-        for h in range(high):
-            counts[g * GROUP : (g + 1) * GROUP, h * LANES : (h + 1) * LANES] = found[
-                h * GROUP : (h + 1) * GROUP
-            ]
-    both = dot(table_ref[0], counts[:, :rows], ((1,), (1,)))
-    at = pl.multiple_of(pl.program_id(0) * nodes, nodes)
-    own = table_ref[0, :, pl.ds(at, nodes)].astype(f32)
-    both = both + own
-    sum_ref[...] = both[:LANES] + both[LANES:]
-    halo_ref[...] = counts[:, rows:]
-
-
-def local_sums(idx, mask, table, micro, slots):
-    _, degree, rows = idx.shape
-    return pl.pallas_call(
-        local_sum_kernel,
-        grid=(rows // NODE_BLOCK,),
-        in_specs=[
-            pl.BlockSpec((1, degree, NODE_BLOCK), lambda b: (micro, 0, b)),
-            pl.BlockSpec((1, degree, NODE_BLOCK), lambda b: (micro, 0, b)),
-            pl.BlockSpec((1, 2 * LANES, rows), lambda b: (micro, 0, 0)),
-        ],
-        out_specs=[
-            pl.BlockSpec((LANES, NODE_BLOCK), lambda b: (0, b)),
-            pl.BlockSpec((NODE_BLOCK, slots), lambda b: (b, 0)),
-        ],
-        out_shape=[
-            jax.ShapeDtypeStruct((LANES, rows), f32),
-            jax.ShapeDtypeStruct((rows, slots), bf16),
-        ],
-        scratch_shapes=[pltpu.VMEM((NODE_BLOCK, rows + slots), bf16)],
-        name="local_sums",
-    )(idx, mask, table)
-
-
-def finish_kernel(*refs):
-    micros = (len(refs) - 4) // 2
-    sums, halos = refs[:micros], refs[micros : 2 * micros]
-    arrived_ref, send_ref, table_ref, out_ref = refs[2 * micros :]
-    for m in range(micros):
-        hi, lo = arrived_table(arrived_ref, m, 1.0)
-        counts = halos[m][...]
-        total = sums[m][...] + dot(hi, counts, ((1,), (1,))) + dot(lo, counts, ((1,), (1,)))
-        agg = total / total[F : F + 1]
-        agg = jnp.where(iota(agg.shape, 0) == F, 1.0, agg)
-        hi, lo = split(agg)
-        table_ref[m, :LANES] = hi
-        table_ref[m, LANES:] = lo
-        sent_rows(table_ref[m], send_ref[m], out_ref, m)
-
-
 def arrived_table(ref, micro, degree=None):
     slots = ref.shape[0] * HCAP
     rows = ref[:, micro].reshape(slots, LANES)
     if degree is not None:
         rows = jnp.where(iota(rows.shape, 1) == F, degree, rows)
-    return split(rows.T)
-
-
-def finish(sums, halos, arrived, send):
-    micros = len(sums)
-    rows = sums[0].shape[1]
-    return pl.pallas_call(
-        finish_kernel,
-        out_shape=[
-            jax.ShapeDtypeStruct((micros, 2 * LANES, rows), bf16),
-            jax.ShapeDtypeStruct(arrived.shape, f32),
-        ],
-        name="finish",
-    )(*sums, *halos, arrived, send)
+    return jnp.concatenate(split(rows.T), axis=0)
 
 
 def edge_row(pos_ref, neg_ref, micro, side):
@@ -182,19 +90,147 @@
     return jnp.concatenate([pos, neg_ref[micro, side : side + 1, :]], axis=1)
 
 
-def pick_kernel(pos_ref, neg_ref, table_ref, out_ref):
-    count = 2 * pos_ref.shape[2]
-    for m in range(pos_ref.shape[0]):
-        for s in range(2):
-            at = (2 * m + s) * count
-            out_ref[:, at : at + count] = picked(table_ref[m], edge_row(pos_ref, neg_ref, m, s))
-
-
-def pick(pos, neg, table):
-    ends = pos.shape[0] * 4 * pos.shape[2]
+def select_kernel(
+    idx_ref, mask_ref, table_ref, send_ref, pos_ref, neg_ref,
+    sent_slot_ref, sent_own_ref, slot_ref, own_ref, wide,
+):
+    degree = idx_ref.shape[1]
+    for m in range(idx_ref.shape[0]):
+        slot = jnp.where(mask_ref[m] > 0, idx_ref[m] + 1, 0)
+        wide[:degree] = (slot >> 8).astype(f32).astype(bf16)
+        wide[degree : 2 * degree] = (slot & 255).astype(f32).astype(bf16)
+        wide[2 * degree :] = table_ref[m]
+        count = 2 * pos_ref.shape[2]
+        ends = [(edge_row(pos_ref, neg_ref, m, k), slot_ref, own_ref, k * count) for k in range(2)]
+        for index, slots, owns, at in [(send_ref[m], sent_slot_ref, sent_own_ref, 0)] + ends:
+            stop = at + index.shape[1]
+            which = one_hot(iota((wide.shape[1], index.shape[1]), 0) == index)
+            found = dot(wide[...], which)
+            high = found[:degree].astype(jnp.int32)
+            slots[m, :, at:stop] = high * 256 + found[degree : 2 * degree].astype(jnp.int32)
+            own = found[2 * degree :]
+            owns[m, :, at:stop] = own[:LANES] + own[LANES:]
+
+
+def select(idx, mask, table, send, pos, neg):
+    micros, degree, rows = idx.shape
+    shapes = []
+    for count in (send.shape[2], 4 * pos.shape[2]):
+        shapes.append(jax.ShapeDtypeStruct((micros, degree, count), jnp.int32))
+        shapes.append(jax.ShapeDtypeStruct((micros, LANES, count), f32))
     return pl.pallas_call(
-        pick_kernel, out_shape=jax.ShapeDtypeStruct((LANES, ends), f32), name="pick"
-    )(pos, neg, table)
+        select_kernel,
+        out_shape=shapes,
+        scratch_shapes=[pltpu.VMEM((2 * degree + 2 * LANES, rows), bf16)],
+        name="select",
+    )(idx, mask, table, send, pos, neg)
+
+
+def count_slots(slots, counts):
+    degree, nodes = slots.shape
+    width = degree * GROUP
+    span = 2 * LANES
+    high = -(-counts.shape[1] // span)
+    slots = slots - 1
+    lane_part = iota((degree, width), 1) // GROUP
+    row = iota((degree, width), 0)
+    parts = []
+    for at in range(0, nodes, width):
+        size = min(width, nodes - at)
+        piece = slots[:, at : at + size]
+        if size < width:
+            piece = jnp.concatenate([piece, jnp.full((degree, width - size), -1, jnp.int32)], axis=1)
+        turned = piece
+        for d in range(1, GROUP):
+            moved = pltpu.roll(pltpu.roll(piece, d, 0), width - GROUP * d, 1)
+            turned = jnp.where(lane_part == ((row - d) & (GROUP - 1)), moved, turned)
+        parts.append(turned)
+    turned = jnp.concatenate(parts, axis=0)
+    high_part = (turned >> 8).astype(f32)
+    low_part = (turned & (span - 1)).astype(f32)
+    same = (iota((GROUP, width), 1) & (GROUP - 1)) == iota((GROUP, width), 0)
+    same = one_hot(same)
+    none = jnp.zeros((GROUP, width), bf16)
+    low_rows = iota((span, width), 0).astype(f32).astype(bf16)
+    one = jnp.ones((span, width), bf16)
+    zero = jnp.zeros((span, width), bf16)
+    for g in range(nodes // GROUP):
+        hi = jnp.broadcast_to(high_part[g : g + 1], (GROUP, width)).astype(bf16)
+        lo = jnp.broadcast_to(low_part[g : g + 1], (span, width)).astype(bf16)
+        left = jnp.concatenate([jnp.where(hi == h, same, none) for h in range(high)], axis=0)
+        right = jnp.where(low_rows == lo, one, zero)
+        found = dot(left, right, ((1,), (1,))).astype(bf16)
+        for h in range(high):
+            at = h * span
+            size = min(span, counts.shape[1] - at)
+            counts[g * GROUP : (g + 1) * GROUP, at : at + size] = found[
+                h * GROUP : (h + 1) * GROUP, :size
+            ]
+
+
+def mean_columns(slots, own, table, arrived, counts):
+    count_slots(slots, counts)
+    rows = table.shape[1]
+    both = dot(table, counts[:, :rows], ((1,), (1,)))
+    both = both + dot(arrived, counts[:, rows:], ((1,), (1,)))
+    total = both[:LANES] + both[LANES:] + own
+    degree = total[F : F + 1]
+    mean = jnp.where(degree > 0.5, total / jnp.maximum(degree, 1.0), 0.0)
+    return jnp.where(iota(mean.shape, 0) == F, jnp.minimum(degree, 1.0), mean)
+
+
+def mean_sent_kernel(slot_ref, own_ref, table_ref, arrived_ref, out_ref, counts):
+    for m in range(slot_ref.shape[0]):
+        arrived = arrived_table(arrived_ref, m, 1.0)
+        mean = mean_columns(slot_ref[m], own_ref[m], table_ref[m], arrived, counts)
+        out_ref[:, m] = mean.T.reshape(out_ref.shape[0], HCAP, LANES)
+
+
+def mean_sent(slot, own, table, arrived):
+    micros, degree, _ = slot.shape
+    sent = arrived.shape[0] * HCAP
+    rows = table.shape[2]
+    return pl.pallas_call(
+        mean_sent_kernel,
+        grid=(1,),
+        in_specs=[
+            pl.BlockSpec((micros, degree, sent), lambda i: (0, 0, 0)),
+            pl.BlockSpec((micros, LANES, sent), lambda i: (0, 0, 0)),
+            pl.BlockSpec(table.shape, lambda i: (0, 0, 0)),
+            pl.BlockSpec(arrived.shape, lambda i: (0, 0, 0, 0)),
+        ],
+        out_specs=pl.BlockSpec(arrived.shape, lambda i: (0, 0, 0, 0)),
+        out_shape=jax.ShapeDtypeStruct(arrived.shape, f32),
+        scratch_shapes=[pltpu.VMEM((sent, rows + sent), bf16)],
+        name="mean_sent",
+    )(slot, own, table, arrived)
+
+
+def mean_ends_kernel(slot_ref, own_ref, table_ref, arrived_ref, out_ref, counts):
+    arrived = arrived_table(arrived_ref, 0, 1.0)
+    out_ref[...] = mean_columns(slot_ref[0], own_ref[0], table_ref[0], arrived, counts)
+
+
+def mean_ends(slot, own, table, arrived, micro, block):
+    degree = slot.shape[1]
+    peers = arrived.shape[0]
+    sent = peers * HCAP
+    rows = table.shape[2]
+    count = slot.shape[2]
+    return pl.pallas_call(
+        mean_ends_kernel,
+        grid=(count // block,),
+        in_specs=[
+            pl.BlockSpec((1, degree, block), lambda b: (micro, 0, b)),
+            pl.BlockSpec((1, LANES, block), lambda b: (micro, 0, b)),
+            pl.BlockSpec((1, 2 * LANES, rows), lambda b: (micro, 0, 0)),
+            pl.BlockSpec((peers, 1, HCAP, LANES), lambda b: (0, micro, 0, 0)),
+        ],
+        out_specs=pl.BlockSpec((LANES, block), lambda b: (0, b)),
+        out_shape=jax.ShapeDtypeStruct((LANES, count), f32),
+        scratch_shapes=[pltpu.VMEM((block, rows + sent), bf16)],
+        name="mean_ends",
+    )(slot, own, table, arrived)
 
 
 def first_block(ref, start, shards, hs):
@@ -219,22 +255,22 @@
 
 
 def layers_kernel(
-    part_ref, pos_ref, neg_ref, arrived_ref, mine_ref, other_ref, head_bias_ref,
-    grad_mine_ref, grad_other_ref, stats_ref,
-    agg_row, agg_col, hidden, out_col, dz_col, dz_row,
-    *, hs, nodes, slope_scale,
+    *refs, hs, nodes, slope_scale,
 ):
+    agg_row, agg_col, hidden, out_col, dz_col, dz_row = refs[-6:]
+    grad_mine_ref, grad_other_ref, stats_ref = refs[-9:-6]
+    pos_ref, neg_ref, arrived_ref, mine_ref, other_ref, head_bias_ref = refs[-15:-9]
+    parts = refs[:-15]
     micros, sides, count = pos_ref.shape[0], 2, 2 * pos_ref.shape[2]
     ends = micros * sides * count
     shards = HID_BLOCK // hs
     blocks = mine_ref.shape[0] // shards
 
     for m in range(micros):
-        far = jnp.concatenate(arrived_table(arrived_ref, m), axis=0)
-        far = picked(far, edge_row(pos_ref, neg_ref, m, 1), nodes)
+        far = picked(arrived_table(arrived_ref, m), edge_row(pos_ref, neg_ref, m, 1), nodes)
         for s in range(sides):
             at = (m * sides + s) * count
-            cols = part_ref[:, at : at + count]
+            cols = parts[m][:, s * count : (s + 1) * count]
             if s == 1:
                 cols = cols + far
             hi, lo = split(cols)
@@ -332,8 +368,8 @@
         lax.fori_loop(0, blocks, backward, 0)
 
 
-def layers(part, pos, neg, arrived, mine, other, head_bias, hs, nodes, slope_scale):
-    ends = part.shape[1]
+def layers(parts, pos, neg, arrived, mine, other, head_bias, hs, nodes, slope_scale):
+    ends = len(parts) * parts[0].shape[1]
     blocks = 2 * mine.shape[0] * hs // HID_BLOCK
     shape = jax.ShapeDtypeStruct(mine.shape, f32)
     return pl.pallas_call(
@@ -348,7 +384,7 @@
             pltpu.VMEM((ends, LANES), bf16),
         ],
         name="layers",
-    )(part, pos, neg, arrived, mine, other, head_bias)
+    )(*parts, pos, neg, arrived, mine, other, head_bias)
 
 
 def stages(size):
@@ -486,7 +522,6 @@
     g_head_ref, b_two_new_ref, second_new_head_ref,
     *, hidden_units, slope_scale,
 ):
-    hs = b_one_ref.shape[1]
     classes = w_two_ref.shape[0]
     sums = jnp.sum(sums_ref[...], axis=0)
     row_total, one_total, two_total, bias_total, bias_rms, loss = [
@@ -567,28 +602,23 @@
     def exchange(sent):
         return lax.all_to_all(sent, "dom", 0, 0, tiled=True)
 
+    turns = list(reversed(stages(peers)))
+    weights = pack_shard(w_one, b_one, w_two)[None]
+    weights = spread_stage(weights, *turns[0])
     table, sent = front(x, send)
     arrived_x = exchange(sent)
-    weights = pack_shard(w_one, b_one, w_two)[None]
-    sums, halos = [], []
-    turns = list(reversed(stages(peers)))
-    for m in range(micros):
-        if m < len(turns):
-            weights = spread_stage(weights, *turns[m])
-        total_rows, halo = local_sums(idx, mask, table, m, slots)
-        if m + 1 < len(turns):
-            total_rows, weights, table = lax.optimization_barrier((total_rows, weights, table))
-        sums.append(total_rows)
-        halos.append(halo)
-    for turn in turns[micros:]:
+    sent_slot, sent_own, slot, own = select(idx, mask, table, send, pos, neg)
+    sent = mean_sent(sent_slot, sent_own, table, arrived_x)
+    arrived_agg = exchange(sent)
+    for turn in turns[1:]:
         weights = spread_stage(weights, *turn)
     other = swap(weights)
-    table, sent = finish(sums, halos, arrived_x, send)
-    arrived_agg = exchange(sent)
-    part = pick(pos, neg, table)
+    means = []
+    for m in range(micros):
+        means.append(mean_ends(slot, own, table, arrived_x, m, 2 * pos.shape[2]))
     head_bias = jnp.broadcast_to(jnp.pad(b_two, (0, LANES - classes)), (8, LANES))
     grad_mine, grad_other, stats = layers(
-        part, pos, neg, arrived_agg, weights, other, head_bias, hs, rows, slope_scale
+        means, pos, neg, arrived_agg, weights, other, head_bias, hs, rows, slope_scale
     )
     g = collect(grad_mine, grad_other)
 

time: 153 us -> 138 us (0.902)
  Pallas kernels: 78.8 us -> 62.5 us
  waiting for transfers between devices: 24.5 us -> 30.8 us
  starting transfers between devices: 30.1 us -> 25.4 us
    pallas_call x4, Pallas kernels: 40.3 us -> 24.1 us  [the longest x2 13.9 us: mean_ends(): pl.pallas_call(mean_ends_kernel, grid=(count // block,), in_specs=[pl.Blo...]
    ppermute x12, waiting for transfers between devices: 19.3 us -> 26 us  [trade(): return lax.ppermute(x, 'dom', [(i, i ^ offset) for i in range(size)])]
    all_to_all x2, starting transfers between devices: 12.7 us -> 8.14 us  [exchange(): return lax.all_to_all(sent, 'dom', 0, 0, tiled=True)]
  transfers between devices with their start and end apart: 16 -> 16, of which waited for: 8 -> 11; matrix products, arithmetic and copies ran while one was open for 1% -> 1% of each run, Pallas kernels for 29% -> 20%
where the time goes in v3:
time: 138 us
  Pallas kernels  62.5 us (45%)
  waiting for transfers between devices  30.8 us (22%)
  starting transfers between devices  25.4 us (18%)
  blocking collectives  11.1 us (8%)
  local copies, waits for them, and re-layouts  4.05 us (3%)
  other arithmetic  2.83 us (2%)
    pallas_call x1, Pallas kernels, layers(): pl.pallas_call(lambda *refs: layers_kernel(*refs, hs=hs, nodes=nodes, slo...  30.7 us
    ppermute x12, waiting for transfers between devices, trade(): return lax.ppermute(x, 'dom', [(i, i ^ offset) for i in range(size)])  26 us
    ppermute x12, starting transfers between devices, trade(): return lax.ppermute(x, 'dom', [(i, i ^ offset) for i in range(size)])  17.2 us
    pallas_call x2, Pallas kernels, mean_ends(): pl.pallas_call(mean_ends_kernel, grid=(count // block,), in_specs=[pl.Blo...  13.9 us
    all_to_all x1, blocking collectives, local(): parts = lax.all_to_all(parts, ('dom', 'rep'), 0, 0, tiled=True)  11.1 us
    all_to_all x2, starting transfers between devices, exchange(): return lax.all_to_all(sent, 'dom', 0, 0, tiled=True)  8.14 us
    pallas_call x1, Pallas kernels, select(): pl.pallas_call(select_kernel, out_shape=shapes, scratch_shapes=[pltpu.VME...  6.01 us
    pallas_call x1, Pallas kernels, mean_sent(): pl.pallas_call(mean_sent_kernel, grid=(1,), in_specs=[pl.BlockSpec((micro...  4.21 us
  transfers between devices with their start and end apart: 16, of which 11 were waited for; matrix products, arithmetic and copies ran while one was open for 1% of the time, Pallas kernels for 20%

profile of v3, /device:TPU:0, one launch (start us, length us, event | category | flops | bytes accessed | tf_op | source)
XLA Modules:
  0.0 137.6 jit_solution(8672687598202215542)
XLA Ops:
  0.6 0.0 copy-start.4
  0.7 0.0 copy-start.5
  0.7 0.8 copy.39
  1.5 0.7 copy.38
  2.3 0.8 select_maximum_fusion
  3.1 0.1 constant_dynamic-update-slice_fusion.6
  3.2 3.1 %collective-permute-start = (f32[1,96,128]{2,1,0:T(8,128)S(1)}, f32[1,96,128]{2,1,0:T(8,128)S(1)}, u32[]{:S(2)}, u32[]{:S(2)}) collective-permute-start(f32[1,96,128]{2,1,0:T(8,128)S(1)} %get-tuple-element.70), channel_id=1, source_target_pairs={{0,8},{2,10},{4,12},{6,14},{8,0},{10,2},{12,4},{14,6},{16,24},{18,... | collective-permute-start | bytes 147464 | tf_op jit(solution)/shard_map/ppermute | solution.py:402
  6.2 2.6 %collective-permute-start.1 = (f32[1,96,128]{2,1,0:T(8,128)S(1)}, f32[1,96,128]{2,1,0:T(8,128)S(1)}, u32[]{:S(2)}, u32[]{:S(2)}) collective-permute-start(f32[1,96,128]{2,1,0:T(8,128)S(1)} %get-tuple-element.70), channel_id=1, source_target_pairs={{0,16},{2,18},{4,20},{6,22},{8,24},{10,26},{12,28},{14,30},{16,0},... | collective-permute-start | bytes 147464 | tf_op jit(solution)/shard_map/ppermute | solution.py:402
  8.8 0.0 collective-permute-start.2
  8.8 0.0 collective-permute-done
  8.8 3.3 %collective-permute-done.1 = f32[1,96,128]{2,1,0:T(8,128)S(1)} collective-permute-done((f32[1,96,128]{2,1,0:T(8,128)S(1)}, f32[1,96,128]{2,1,0:T(8,128)S(1)}, u32[]{:S(2)}, u32[]{:S(2)}) %collective-permute-start.1) | collective-permute-done | bytes 49184 | tf_op jit(solution)/shard_map/ppermute | solution.py:402
  12.1 2.6 %collective-permute-done.2 = f32[1,96,128]{2,1,0:T(8,128)S(1)} collective-permute-done((f32[1,96,128]{2,1,0:T(8,128)S(1)}, f32[1,96,128]{2,1,0:T(8,128)S(1)}, u32[]{:S(2)}, u32[]{:S(2)}) %collective-permute-start.2) | collective-permute-done | bytes 49184 | tf_op jit(solution)/shard_map/ppermute | solution.py:402
  14.7 1.6 %collective-permute-start.3 = (f32[4,96,128]{2,1,0:T(8,128)S(1)}, f32[4,96,128]{2,1,0:T(8,128)S(1)}, u32[]{:S(2)}, u32[]{:S(2)}) collective-permute-start(f32[4,96,128]{2,1,0:T(8,128)S(1)} %pad_maximum_fusion), channel_id=1, source_target_pairs={{0,2},{2,0},{4,6},{6,4},{8,10},{10,8},{12,14},{14,12},{16,18},{18,... | collective-permute-start | bytes 589832 | tf_op jit(solution)/shard_map/ppermute | solution.py:402
  16.3 1.5 %collective-permute-start.4 = (f32[4,96,128]{2,1,0:T(8,128)S(1)}, f32[4,96,128]{2,1,0:T(8,128)S(1)}, u32[]{:S(2)}, u32[]{:S(2)}) collective-permute-start(f32[4,96,128]{2,1,0:T(8,128)S(1)} %pad_maximum_fusion), channel_id=1, source_target_pairs={{0,4},{2,6},{4,0},{6,2},{8,12},{10,14},{12,8},{14,10},{16,20},{18,... | collective-permute-start | bytes 589832 | tf_op jit(solution)/shard_map/ppermute | solution.py:402
  17.8 0.5 collective-permute-start.5
  18.3 3.9 %collective-permute-done.3 = f32[4,96,128]{2,1,0:T(8,128)S(1)} collective-permute-done((f32[4,96,128]{2,1,0:T(8,128)S(1)}, f32[4,96,128]{2,1,0:T(8,128)S(1)}, u32[]{:S(2)}, u32[]{:S(2)}) %collective-permute-start.3) | collective-permute-done | bytes 196640 | tf_op jit(solution)/shard_map/ppermute | solution.py:402
  22.2 3.3 %collective-permute-done.4 = f32[4,96,128]{2,1,0:T(8,128)S(1)} collective-permute-done((f32[4,96,128]{2,1,0:T(8,128)S(1)}, f32[4,96,128]{2,1,0:T(8,128)S(1)}, u32[]{:S(2)}, u32[]{:S(2)}) %collective-permute-start.4) | collective-permute-done | bytes 196640 | tf_op jit(solution)/shard_map/ppermute | solution.py:402
  25.6 0.0 collective-permute-done.5
  25.6 0.0 copy-start.1
  25.6 0.1 collective-permute-start.6
  25.7 0.0 copy-done.4
  25.7 0.0 copy-done.5
  25.7 0.1 copy.35
  25.8 0.7 reshape.52
  26.4 3.8 %front.1 = (bf16[2,256,2048]{2,1,0:T(8,128)(2,1)}, f32[16,2,8,128]{3,2,1,0:T(8,128)}) custom-call(f32[100,2,2048]{2,1,0:T(2,128)} %bitcast.37, s32[2,1,128]{2,1,0:T(1,128)} %bitcast.49), custom_call_target="tpu_custom_call" | custom-call | tf_op jit(solution)/shard_map/front/pallas_call | solution.py:69
  30.2 3.5 %all-to-all-start = ((f32[16,2,8,128]{3,2,1,0:T(8,128)}), f32[16,2,8,128]{3,2,1,0:T(8,128)S(1)}, u32[]{:S(2)}, u32[]{:S(2)}) async-start(f32[16,2,8,128]{3,2,1,0:T(8,128)} %get-tuple-element.45), calls=%async_computation | async-start | bytes 262144 | tf_op jit(solution)/shard_map/all_to_all | solution.py:603
  33.7 0.0 copy-start.6
  33.7 6.0 %select.8 = (s32[2,16,128]{2,1,0:T(8,128)}, f32[2,128,128]{2,1,0:T(8,128)}, s32[2,16,1024]{2,1,0:T(8,128)}, f32[2,128,1024]{2,1,0:T(8,128)}) custom-call(s32[2,16,2048]{2,1,0:T(8,128)} %bitcast.41, s32[2,16,2048]{2,1,0:T(8,128)} %bitcast.42, bf16[2,256,2048]{2,1,0:T(8,128)(2,1)} %get-tuple-element.42.table_ref, s32[2,1,128]{2,1,0:T(1,128)} %bitcast.50, ...), custom_call_target="tpu_custom_call" | custom-call | tf_op jit(solution)/shard_map/select/pallas_call | solution.py:121
  39.8 0.0 copy-done.1
  39.8 2.3 %all-to-all-done.arrived_ref = f32[16,2,8,128]{3,2,1,0:T(8,128)S(1)} async-done(((f32[16,2,8,128]{3,2,1,0:T(8,128)}), f32[16,2,8,128]{3,2,1,0:T(8,128)S(1)}, u32[]{:S(2)}, u32[]{:S(2)}) %all-to-all-start) | async-done | bytes 131104 | tf_op jit(solution)/shard_map/all_to_all | solution.py:603
  42.0 0.0 copy-start
  42.0 0.7 copy-done
  42.7 4.2 %mean_sent.1 = f32[16,2,8,128]{3,2,1,0:T(8,128)} custom-call(s32[2,16,128]{2,1,0:T(8,128)} %get-tuple-element.46.slot_ref, f32[2,128,128]{2,1,0:T(8,128)} %get-tuple-element.47.own_ref, bf16[2,256,2048]{2,1,0:T(8,128)(2,1)} %get-tuple-element.42.table_ref, f32[16,2,8,128]{3,2,1,0:T(8,128)} %copy-done), custom_call_target="tpu_custom_call" | custom-call | tf_op jit(solution)/shard_map/mean_sent/pallas_call | solution.py:193
  46.9 4.6 %all-to-all-start.1 = ((f32[16,2,8,128]{3,2,1,0:T(8,128)}), f32[16,2,8,128]{3,2,1,0:T(8,128)S(1)}, u32[]{:S(2)}, u32[]{:S(2)}) async-start(f32[16,2,8,128]{3,2,1,0:T(8,128)} %mean_sent.1), calls=%async_computation.1 | async-start | bytes 262144 | tf_op jit(solution)/shard_map/all_to_all | solution.py:603
  51.5 0.0 copy-done.6
  51.6 7.0 %mean_ends.2.refs_0_ = f32[128,1024]{1,0:T(8,128)} custom-call(s32[2,16,1024]{2,1,0:T(8,128)} %get-tuple-element.43.slot_ref, f32[2,128,1024]{2,1,0:T(8,128)} %get-tuple-element.44.own_ref, bf16[2,256,2048]{2,1,0:T(8,128)(2,1)} %get-tuple-element.42.table_ref, f32[16,2,8,128]{3,2,1,0:T(8,128)} %copy-done), custom_call_target="tpu_custom_call" | custom-call | tf_op jit(solution)/shard_map/mean_ends/pallas_call | solution.py:220
  58.5 6.9 %mean_ends.3.refs_1_ = f32[128,1024]{1,0:T(8,128)} custom-call(s32[2,16,1024]{2,1,0:T(8,128)} %get-tuple-element.43.slot_ref, f32[2,128,1024]{2,1,0:T(8,128)} %get-tuple-element.44.own_ref, bf16[2,256,2048]{2,1,0:T(8,128)(2,1)} %get-tuple-element.42.table_ref, f32[16,2,8,128]{3,2,1,0:T(8,128)} %copy-done), custom_call_target="tpu_custom_call" | custom-call | tf_op jit(solution)/shard_map/mean_ends/pallas_call | solution.py:220
  65.4 0.0 all-to-all-done.1.refs_4_
  65.5 0.0 collective-permute-done.6.refs_6_
  65.5 0.0 copy-start.2
  65.5 0.7 broadcast_in_dim.42.refs_7_
  66.1 0.0 copy-done.3
  66.1 0.3 copy-done.2
  66.4 30.7 %layers.1 = (f32[16,96,128]{2,1,0:T(8,128)}, f32[16,96,128]{2,1,0:T(8,128)}, f32[8,128]{1,0:T(8,128)}) custom-call(f32[128,1024]{1,0:T(8,128)} %mean_ends.2.refs_0_, f32[128,1024]{1,0:T(8,128)} %mean_ends.3.refs_1_, s32[2,2,256]{2,1,0:T(2,128)} %bitcast.46, s32[2,2,256]{2,1,0:T(2,128)} %bitcast.48, f32[16,2,8,128]{3,2,1,0:T(8,128)} %copy-done.3, ...), custom_call_target="tpu_custom_call" | custom-call | tf_op jit(solution)/shard_map/layers/pallas_call | solution.py:375
  97.1 0.0 collective-permute-start.7
  97.1 2.5 %collective-permute-done.7 = f32[16,96,128]{2,1,0:T(8,128)S(1)} collective-permute-done((f32[16,96,128]{2,1,0:T(8,128)}, f32[16,96,128]{2,1,0:T(8,128)S(1)}, u32[]{:S(2)}, u32[]{:S(2)}) %collective-permute-start.7) | collective-permute-done | bytes 786464 | tf_op jit(solution)/shard_map/ppermute | solution.py:406
  99.6 1.2 add.27
  100.9 2.9 %collective-permute-start.10 = (f32[4,96,128]{2,1,0:T(8,128)S(1)}, f32[4,96,128]{2,1,0:T(8,128)S(1)}, u32[]{:S(2)}, u32[]{:S(2)}) collective-permute-start(f32[4,96,128]{2,1,0:T(8,128)S(1)} %get-tuple-element.72), channel_id=1, source_target_pairs={{0,6},{2,4},{4,2},{6,0},{8,14},{10,12},{12,10},{14,8},{16,22},{18,... | collective-permute-start | bytes 589832 | tf_op jit(solution)/shard_map/ppermute | solution.py:402
  103.8 0.5 collective-permute-start.9
  104.3 0.1 collective-permute-start.8
  104.4 5.2 %collective-permute-done.10 = f32[4,96,128]{2,1,0:T(8,128)S(1)} collective-permute-done((f32[4,96,128]{2,1,0:T(8,128)S(1)}, f32[4,96,128]{2,1,0:T(8,128)S(1)}, u32[]{:S(2)}, u32[]{:S(2)}) %collective-permute-start.10) | collective-permute-done | bytes 196640 | tf_op jit(solution)/shard_map/ppermute | solution.py:402
  109.7 3.5 %collective-permute-done.9 = f32[4,96,128]{2,1,0:T(8,128)S(1)} collective-permute-done((f32[4,96,128]{2,1,0:T(8,128)S(1)}, f32[4,96,128]{2,1,0:T(8,128)S(1)}, u32[]{:S(2)}, u32[]{:S(2)}) %collective-permute-start.9) | collective-permute-done | bytes 196640 | tf_op jit(solution)/shard_map/ppermute | solution.py:402
  113.2 0.3 collective-permute-done.8
  113.5 0.1 fusion.1
  113.6 3.3 %collective-permute-start.13 = (f32[1,96,128]{2,1,0:T(8,128)S(1)}, f32[1,96,128]{2,1,0:T(8,128)S(1)}, u32[]{:S(2)}, u32[]{:S(2)}) collective-permute-start(f32[1,96,128]{2,1,0:T(8,128)S(1)} %get-tuple-element.75), channel_id=1, source_target_pairs={{0,24},{2,26},{4,28},{6,30},{8,16},{10,18},{12,20},{14,22},{16,8},... | collective-permute-start | bytes 147464 | tf_op jit(solution)/shard_map/ppermute | solution.py:402
  116.9 0.0 collective-permute-start.12
  116.9 1.1 collective-permute-start.11
  118.0 1.8 %collective-permute-done.13 = f32[1,96,128]{2,1,0:T(8,128)S(1)} collective-permute-done((f32[1,96,128]{2,1,0:T(8,128)S(1)}, f32[1,96,128]{2,1,0:T(8,128)S(1)}, u32[]{:S(2)}, u32[]{:S(2)}) %collective-permute-start.13) | collective-permute-done | bytes 49184 | tf_op jit(solution)/shard_map/ppermute | solution.py:402
  119.9 2.0 %collective-permute-done.12 = f32[1,96,128]{2,1,0:T(8,128)S(1)} collective-permute-done((f32[1,96,128]{2,1,0:T(8,128)S(1)}, f32[1,96,128]{2,1,0:T(8,128)S(1)}, u32[]{:S(2)}, u32[]{:S(2)}) %collective-permute-start.12) | collective-permute-done | bytes 49184 | tf_op jit(solution)/shard_map/ppermute | solution.py:402
  121.9 0.0 collective-permute-done.11
  121.9 0.6 fusion.4.g_ref
  122.5 1.9 %stats.1 = (f32[64,100]{1,0:T(8,128)}, f32[47,64]{1,0:T(8,128)}, f32[1,64]{1,0:T(1,128)}, f32[1,64]{1,0:T(1,128)}, f32[1,64]{1,0:T(1,128)}, /*index=5*/f32[1,64]...) custom-call(f32[96,128]{1,0:T(8,128)} %fusion.4.g_ref, f32[8,128]{1,0:T(8,128)} %get-tuple-element.50.stats_ref, ...), custom_call_target="tpu_custom_call" | custom-call | tf_op jit(solution)/shard_map/stats/pallas_call | solution.py:634
  124.5 11.1 %all_to_all.15.refs_0_ = f32[32,4,128]{2,1,0:T(4,128)} all-to-all(f32[32,4,128]{2,1,0:T(4,128)} %get-tuple-element.51), channel_id=1, replica_groups=mesh['dom'=16,'rep'=2] {'dom','rep'}, dimensions={0} | all-to-all | bytes 131072 | tf_op jit(solution)/shard_map/all_to_all | solution.py:642
  135.5 2.0 %update.1 = (f32[1,1]{1,0:T(1,128)}, f32[64,100]{1,0:T(8,128)}, f32[1,100]{1,0:T(1,128)}, f32[47,64]{1,0:T(8,128)}, f32[1,47]{1,0:T(1,128)}, /*index=5*/f32[1,64...) custom-call(f32[32,4,128]{2,1,0:T(4,128)} %all_to_all.15.refs_0_, f32[64,128]{1,0:T(8,128)} %get-tuple-element.52.refs_1_, ...), custom_call_target="tpu_custom_call" | custom-call | tf_op jit(solution)/shard_map/update/pallas_call | solution.py:644
  (13 shorter events, 0.1 us)
Async XLA Ops:
  0.6 25.0 %copy-start.4 = (s32[2,16,8]{1,2,0:T(8,128)S(1)}, s32[2,16,8]{1,2,0:T(8,128)}, u32[]{:S(2)}) copy-start(s32[2,16,8]{1,2,0:T(8,128)} %param.20) | copy-start | bytes 3076
  0.7 25.0 %copy-start.5 = (s32[2,16]{1,0:T(2,128)S(1)}, s32[2,16]{1,0:T(2,128)}, u32[]{:S(2)}) copy-start(s32[2,16]{1,0:T(2,128)} %param.21) | copy-start | bytes 388
  3.2 5.7 %collective-permute-start = (f32[1,96,128]{2,1,0:T(8,128)S(1)}, f32[1,96,128]{2,1,0:T(8,128)S(1)}, u32[]{:S(2)}, u32[]{:S(2)}) collective-permute-start(f32[1,96,128]{2,1,0:T(8,128)S(1)} %get-tuple-element.70), channel_id=1, source_target_pairs={{0,8},{2,10},{4,12},{6,14},{8,0},{10,2},{12,4},{14,6},{16,24},{18,... | collective-permute-start | bytes 147464 | tf_op jit(solution)/shard_map/ppermute | solution.py:402
  6.2 5.9 %collective-permute-start.1 = (f32[1,96,128]{2,1,0:T(8,128)S(1)}, f32[1,96,128]{2,1,0:T(8,128)S(1)}, u32[]{:S(2)}, u32[]{:S(2)}) collective-permute-start(f32[1,96,128]{2,1,0:T(8,128)S(1)} %get-tuple-element.70), channel_id=1, source_target_pairs={{0,16},{2,18},{4,20},{6,22},{8,24},{10,26},{12,28},{14,30},{16,0},... | collective-permute-start | bytes 147464 | tf_op jit(solution)/shard_map/ppermute | solution.py:402
  8.8 5.9 %collective-permute-start.2 = (f32[1,96,128]{2,1,0:T(8,128)S(1)}, f32[1,96,128]{2,1,0:T(8,128)S(1)}, u32[]{:S(2)}, u32[]{:S(2)}) collective-permute-start(f32[1,96,128]{2,1,0:T(8,128)S(1)} %get-tuple-element.70), channel_id=1, source_target_pairs={{0,24},{2,26},{4,28},{6,30},{8,16},{10,18},{12,20},{14,22},{16,8},... | collective-permute-start | bytes 147464 | tf_op jit(solution)/shard_map/ppermute | solution.py:402
  14.7 7.5 %collective-permute-start.3 = (f32[4,96,128]{2,1,0:T(8,128)S(1)}, f32[4,96,128]{2,1,0:T(8,128)S(1)}, u32[]{:S(2)}, u32[]{:S(2)}) collective-permute-start(f32[4,96,128]{2,1,0:T(8,128)S(1)} %pad_maximum_fusion), channel_id=1, source_target_pairs={{0,2},{2,0},{4,6},{6,4},{8,10},{10,8},{12,14},{14,12},{16,18},{18,... | collective-permute-start | bytes 589832 | tf_op jit(solution)/shard_map/ppermute | solution.py:402
  16.3 9.3 %collective-permute-start.4 = (f32[4,96,128]{2,1,0:T(8,128)S(1)}, f32[4,96,128]{2,1,0:T(8,128)S(1)}, u32[]{:S(2)}, u32[]{:S(2)}) collective-permute-start(f32[4,96,128]{2,1,0:T(8,128)S(1)} %pad_maximum_fusion), channel_id=1, source_target_pairs={{0,4},{2,6},{4,0},{6,2},{8,12},{10,14},{12,8},{14,10},{16,20},{18,... | collective-permute-start | bytes 589832 | tf_op jit(solution)/shard_map/ppermute | solution.py:402
  17.8 7.8 %collective-permute-start.5 = (f32[4,96,128]{2,1,0:T(8,128)S(1)}, f32[4,96,128]{2,1,0:T(8,128)S(1)}, u32[]{:S(2)}, u32[]{:S(2)}) collective-permute-start(f32[4,96,128]{2,1,0:T(8,128)S(1)} %pad_maximum_fusion), channel_id=1, source_target_pairs={{0,6},{2,4},{4,2},{6,0},{8,14},{10,12},{12,10},{14,8},{16,22},{18,... | collective-permute-start | bytes 589832 | tf_op jit(solution)/shard_map/ppermute | solution.py:402
  25.6 14.2 %copy-start.1 = (f32[16,96,128]{2,1,0:T(8,128)}, f32[16,96,128]{2,1,0:T(8,128)S(1)}, u32[]{:S(2)}) copy-start(f32[16,96,128]{2,1,0:T(8,128)S(1)} %constant_dynamic-update-slice_fusion.refs_5_) | copy-start | bytes 2359300
  25.6 39.9 %collective-permute-start.6 = (f32[16,96,128]{2,1,0:T(8,128)S(1)}, f32[16,96,128]{2,1,0:T(8,128)S(1)}, u32[]{:S(2)}, u32[]{:S(2)}) collective-permute-start(f32[16,96,128]{2,1,0:T(8,128)S(1)} %constant_dynamic-update-slice_fusion.refs_5_), channel_id=1, source_target_pairs={{0,1},{1,0},{2,3},{3,2},{4,5},{5,4},{6,7},{7,6},{8,9},{9,8},{10,11... | collective-permute-start | bytes 2359304 | tf_op jit(solution)/shard_map/ppermute | solution.py:406
  30.2 11.8 %all-to-all-start = ((f32[16,2,8,128]{3,2,1,0:T(8,128)}), f32[16,2,8,128]{3,2,1,0:T(8,128)S(1)}, u32[]{:S(2)}, u32[]{:S(2)}) async-start(f32[16,2,8,128]{3,2,1,0:T(8,128)} %get-tuple-element.45), calls=%async_computation | async-start | bytes 262144 | tf_op jit(solution)/shard_map/all_to_all | solution.py:603
  33.7 17.8 %copy-start.6 = (f32[47]{0:T(128)S(1)}, f32[47]{0:T(128)}, u32[]{:S(2)}) copy-start(f32[47]{0:T(128)} %param.27) | copy-start | bytes 568
  42.0 0.7 copy-start
  46.9 18.6 %all-to-all-start.1 = ((f32[16,2,8,128]{3,2,1,0:T(8,128)}), f32[16,2,8,128]{3,2,1,0:T(8,128)S(1)}, u32[]{:S(2)}, u32[]{:S(2)}) async-start(f32[16,2,8,128]{3,2,1,0:T(8,128)} %mean_sent.1), calls=%async_computation.1 | async-start | bytes 262144 | tf_op jit(solution)/shard_map/all_to_all | solution.py:603
  65.5 0.7 copy-start.3
  65.5 1.0 copy-start.2
  97.1 2.5 %collective-permute-start.7 = (f32[16,96,128]{2,1,0:T(8,128)}, f32[16,96,128]{2,1,0:T(8,128)S(1)}, u32[]{:S(2)}, u32[]{:S(2)}) collective-permute-start(f32[16,96,128]{2,1,0:T(8,128)} %get-tuple-element.49), channel_id=1, source_target_pairs={{0,1},{1,0},{2,3},{3,2},{4,5},{5,4},{6,7},{7,6},{8,9},{9,8},{10,11... | collective-permute-start | bytes 2359304 | tf_op jit(solution)/shard_map/ppermute | solution.py:406
  100.9 8.8 %collective-permute-start.10 = (f32[4,96,128]{2,1,0:T(8,128)S(1)}, f32[4,96,128]{2,1,0:T(8,128)S(1)}, u32[]{:S(2)}, u32[]{:S(2)}) collective-permute-start(f32[4,96,128]{2,1,0:T(8,128)S(1)} %get-tuple-element.72), channel_id=1, source_target_pairs={{0,6},{2,4},{4,2},{6,0},{8,14},{10,12},{12,10},{14,8},{16,22},{18,... | collective-permute-start | bytes 589832 | tf_op jit(solution)/shard_map/ppermute | solution.py:402
  103.8 9.4 %collective-permute-start.9 = (f32[4,96,128]{2,1,0:T(8,128)S(1)}, f32[4,96,128]{2,1,0:T(8,128)S(1)}, u32[]{:S(2)}, u32[]{:S(2)}) collective-permute-start(f32[4,96,128]{2,1,0:T(8,128)S(1)} %get-tuple-element.73), channel_id=1, source_target_pairs={{0,4},{2,6},{4,0},{6,2},{8,12},{10,14},{12,8},{14,10},{16,20},{18,... | collective-permute-start | bytes 589832 | tf_op jit(solution)/shard_map/ppermute | solution.py:402
  104.3 9.2 %collective-permute-start.8 = (f32[4,96,128]{2,1,0:T(8,128)S(1)}, f32[4,96,128]{2,1,0:T(8,128)S(1)}, u32[]{:S(2)}, u32[]{:S(2)}) collective-permute-start(f32[4,96,128]{2,1,0:T(8,128)S(1)} %get-tuple-element.71), channel_id=1, source_target_pairs={{0,2},{2,0},{4,6},{6,4},{8,10},{10,8},{12,14},{14,12},{16,18},{18,... | collective-permute-start | bytes 589832 | tf_op jit(solution)/shard_map/ppermute | solution.py:402
  113.6 6.3 %collective-permute-start.13 = (f32[1,96,128]{2,1,0:T(8,128)S(1)}, f32[1,96,128]{2,1,0:T(8,128)S(1)}, u32[]{:S(2)}, u32[]{:S(2)}) collective-permute-start(f32[1,96,128]{2,1,0:T(8,128)S(1)} %get-tuple-element.75), channel_id=1, source_target_pairs={{0,24},{2,26},{4,28},{6,30},{8,16},{10,18},{12,20},{14,22},{16,8},... | collective-permute-start | bytes 147464 | tf_op jit(solution)/shard_map/ppermute | solution.py:402
  116.9 5.0 %collective-permute-start.12 = (f32[1,96,128]{2,1,0:T(8,128)S(1)}, f32[1,96,128]{2,1,0:T(8,128)S(1)}, u32[]{:S(2)}, u32[]{:S(2)}) collective-permute-start(f32[1,96,128]{2,1,0:T(8,128)S(1)} %get-tuple-element.76), channel_id=1, source_target_pairs={{0,16},{2,18},{4,20},{6,22},{8,24},{10,26},{12,28},{14,30},{16,0},... | collective-permute-start | bytes 147464 | tf_op jit(solution)/shard_map/ppermute | solution.py:402
  116.9 5.0 %collective-permute-start.11 = (f32[1,96,128]{2,1,0:T(8,128)S(1)}, f32[1,96,128]{2,1,0:T(8,128)S(1)}, u32[]{:S(2)}, u32[]{:S(2)}) collective-permute-start(f32[1,96,128]{2,1,0:T(8,128)S(1)} %get-tuple-element.74), channel_id=1, source_target_pairs={{0,8},{2,10},{4,12},{6,14},{8,0},{10,2},{12,4},{14,6},{16,24},{18,... | collective-permute-start | bytes 147464 | tf_op jit(solution)/shard_map/ppermute | solution.py:402

commit v4 on v3

--- a/solution.py
+++ b/solution.py
@@ -5,14 +5,15 @@
 from jax.experimental.pallas import tpu as pltpu
 from jax.sharding import PartitionSpec as P
 
+
 F = 100
 HCAP = 8
 STEP = 20
 LANES = 128
 HALF = 64
 GROUP = 16
-HID_BLOCK = 256
-COL_BLOCK = 512
+HID_BLOCK = 512
+COL_BLOCK = 2048
 
 tiny_eps = 1e-30
 scale_eps = 0.001
@@ -129,8 +130,6 @@
 def count_slots(slots, counts):
     degree, nodes = slots.shape
     width = degree * GROUP
-    span = 2 * LANES
-    high = -(-counts.shape[1] // span)
     slots = slots - 1
     lane_part = iota((degree, width), 1) // GROUP
     row = iota((degree, width), 0)
@@ -146,19 +145,22 @@
             turned = jnp.where(lane_part == ((row - d) & (GROUP - 1)), moved, turned)
         parts.append(turned)
     turned = jnp.concatenate(parts, axis=0)
-    high_part = (turned >> 8).astype(f32)
-    low_part = (turned & (span - 1)).astype(f32)
     same = (iota((GROUP, width), 1) & (GROUP - 1)) == iota((GROUP, width), 0)
     same = one_hot(same)
     none = jnp.zeros((GROUP, width), bf16)
-    low_rows = iota((span, width), 0).astype(f32).astype(bf16)
-    one = jnp.ones((span, width), bf16)
-    zero = jnp.zeros((span, width), bf16)
+    forms = []
+    for span in (LANES, 2 * LANES):
+        high_part = (turned >> (span.bit_length() - 1)).astype(f32)
+        low_part = (turned & (span - 1)).astype(f32)
+        low_rows = iota((span, width), 0).astype(f32).astype(bf16)
+        forms.append((span, high_part, low_part, low_rows))
     for g in range(nodes // GROUP):
+        span, high_part, low_part, low_rows = forms[g & 1]
+        high = -(-counts.shape[1] // span)
         hi = jnp.broadcast_to(high_part[g : g + 1], (GROUP, width)).astype(bf16)
         lo = jnp.broadcast_to(low_part[g : g + 1], (span, width)).astype(bf16)
         left = jnp.concatenate([jnp.where(hi == h, same, none) for h in range(high)], axis=0)
-        right = jnp.where(low_rows == lo, one, zero)
+        right = jnp.where(low_rows == lo, jnp.ones((span, width), bf16), jnp.zeros((span, width), bf16))
         found = dot(left, right, ((1,), (1,))).astype(bf16)
         for h in range(high):
             at = h * span
@@ -305,7 +307,7 @@
 
         lax.fori_loop(0, blocks, forward, 0)
 
-    bias = head_bias_ref[...].T[:HALF, :1]
+    bias = to_column(head_bias_ref[...], HALF)
     loss = jnp.zeros((1, 1), f32)
     head_grad = jnp.zeros((HALF, 1), f32)
     sign = jnp.where(iota((1, count), 1) < count // 2, -1.0, 1.0)
@@ -616,7 +618,7 @@
     means = []
     for m in range(micros):
         means.append(mean_ends(slot, own, table, arrived_x, m, 2 * pos.shape[2]))
-    head_bias = jnp.broadcast_to(jnp.pad(b_two, (0, LANES - classes)), (8, LANES))
+    head_bias = b_two[None]
     grad_mine, grad_other, stats = layers(
         means, pos, neg, arrived_agg, weights, other, head_bias, hs, rows, slope_scale
     )

time: 138 us -> 132 us (0.957)
  Pallas kernels: 62.5 us -> 56.1 us
    pallas_call x1, Pallas kernels: 30.7 us -> 26.2 us  [layers(): pl.pallas_call(lambda *refs: layers_kernel(*refs, hs=hs, nodes=nodes, slo...]
    pallas_call x2, Pallas kernels: 13.9 us -> 12.1 us  [mean_ends(): pl.pallas_call(mean_ends_kernel, grid=(count // block,), in_specs=[pl.Blo...]
where the time goes in v4:
time: 132 us; the launch traced here: 131 us
  Pallas kernels  56.1 us (42%)
  waiting for transfers between devices  30.8 us (23%)
  starting transfers between devices  25.4 us (19%)
  blocking collectives  11.1 us (8%)
  local copies, waits for them, and re-layouts  4.02 us (3%)
  other arithmetic  2.83 us (2%)
    pallas_call x1, Pallas kernels, layers(): pl.pallas_call(lambda *refs: layers_kernel(*refs, hs=hs, nodes=nodes, slo...  26.2 us
    ppermute x12, waiting for transfers between devices, trade(): return lax.ppermute(x, 'dom', [(i, i ^ offset) for i in range(size)])  26 us
    ppermute x12, starting transfers between devices, trade(): return lax.ppermute(x, 'dom', [(i, i ^ offset) for i in range(size)])  17.2 us
    pallas_call x2, Pallas kernels, mean_ends(): pl.pallas_call(mean_ends_kernel, grid=(count // block,), in_specs=[pl.Blo...  12.1 us
    all_to_all x1, blocking collectives, local(): parts = lax.all_to_all(parts, ('dom', 'rep'), 0, 0, tiled=True)  11.1 us
    all_to_all x2, starting transfers between devices, exchange(): return lax.all_to_all(sent, 'dom', 0, 0, tiled=True)  8.12 us
    pallas_call x1, Pallas kernels, select(): pl.pallas_call(select_kernel, out_shape=shapes, scratch_shapes=[pltpu.VME...  6.01 us
    pallas_call x1, Pallas kernels, mean_sent(): pl.pallas_call(mean_sent_kernel, grid=(1,), in_specs=[pl.BlockSpec((micro...  4.09 us
  transfers between devices with their start and end apart: 16, of which 11 were waited for; matrix products, arithmetic and copies ran while one was open for 1% of the time, Pallas kernels for 20%

profile of v4, /device:TPU:0, one launch (start us, length us, event | category | flops | bytes accessed | tf_op | source)
XLA Modules:
  0.0 131.2 jit_solution(17478399749048842636)
XLA Ops:
  0.6 0.0 copy-start.4
  0.7 0.0 copy-start.5
  0.7 0.8 copy.39
  1.5 0.7 copy.38
  2.3 0.8 select_maximum_fusion
  3.1 0.1 constant_dynamic-update-slice_fusion.6
  3.2 3.1 %collective-permute-start = (f32[1,96,128]{2,1,0:T(8,128)S(1)}, f32[1,96,128]{2,1,0:T(8,128)S(1)}, u32[]{:S(2)}, u32[]{:S(2)}) collective-permute-start(f32[1,96,128]{2,1,0:T(8,128)S(1)} %get-tuple-element.70), channel_id=1, source_target_pairs={{0,8},{2,10},{4,12},{6,14},{8,0},{10,2},{12,4},{14,6},{16,24},{18,... | collective-permute-start | bytes 147464 | tf_op jit(solution)/shard_map/ppermute | solution.py:404
  6.2 2.6 %collective-permute-start.1 = (f32[1,96,128]{2,1,0:T(8,128)S(1)}, f32[1,96,128]{2,1,0:T(8,128)S(1)}, u32[]{:S(2)}, u32[]{:S(2)}) collective-permute-start(f32[1,96,128]{2,1,0:T(8,128)S(1)} %get-tuple-element.70), channel_id=1, source_target_pairs={{0,16},{2,18},{4,20},{6,22},{8,24},{10,26},{12,28},{14,30},{16,0},... | collective-permute-start | bytes 147464 | tf_op jit(solution)/shard_map/ppermute | solution.py:404
  8.8 0.0 collective-permute-start.2
  8.8 0.0 collective-permute-done
  8.8 3.3 %collective-permute-done.1 = f32[1,96,128]{2,1,0:T(8,128)S(1)} collective-permute-done((f32[1,96,128]{2,1,0:T(8,128)S(1)}, f32[1,96,128]{2,1,0:T(8,128)S(1)}, u32[]{:S(2)}, u32[]{:S(2)}) %collective-permute-start.1) | collective-permute-done | bytes 49184 | tf_op jit(solution)/shard_map/ppermute | solution.py:404
  12.1 2.6 %collective-permute-done.2 = f32[1,96,128]{2,1,0:T(8,128)S(1)} collective-permute-done((f32[1,96,128]{2,1,0:T(8,128)S(1)}, f32[1,96,128]{2,1,0:T(8,128)S(1)}, u32[]{:S(2)}, u32[]{:S(2)}) %collective-permute-start.2) | collective-permute-done | bytes 49184 | tf_op jit(solution)/shard_map/ppermute | solution.py:404
  14.7 1.6 %collective-permute-start.3 = (f32[4,96,128]{2,1,0:T(8,128)S(1)}, f32[4,96,128]{2,1,0:T(8,128)S(1)}, u32[]{:S(2)}, u32[]{:S(2)}) collective-permute-start(f32[4,96,128]{2,1,0:T(8,128)S(1)} %pad_maximum_fusion), channel_id=1, source_target_pairs={{0,2},{2,0},{4,6},{6,4},{8,10},{10,8},{12,14},{14,12},{16,18},{18,... | collective-permute-start | bytes 589832 | tf_op jit(solution)/shard_map/ppermute | solution.py:404
  16.3 1.5 %collective-permute-start.4 = (f32[4,96,128]{2,1,0:T(8,128)S(1)}, f32[4,96,128]{2,1,0:T(8,128)S(1)}, u32[]{:S(2)}, u32[]{:S(2)}) collective-permute-start(f32[4,96,128]{2,1,0:T(8,128)S(1)} %pad_maximum_fusion), channel_id=1, source_target_pairs={{0,4},{2,6},{4,0},{6,2},{8,12},{10,14},{12,8},{14,10},{16,20},{18,... | collective-permute-start | bytes 589832 | tf_op jit(solution)/shard_map/ppermute | solution.py:404
  17.8 0.5 collective-permute-start.5
  18.3 3.9 %collective-permute-done.3 = f32[4,96,128]{2,1,0:T(8,128)S(1)} collective-permute-done((f32[4,96,128]{2,1,0:T(8,128)S(1)}, f32[4,96,128]{2,1,0:T(8,128)S(1)}, u32[]{:S(2)}, u32[]{:S(2)}) %collective-permute-start.3) | collective-permute-done | bytes 196640 | tf_op jit(solution)/shard_map/ppermute | solution.py:404
  22.2 3.3 %collective-permute-done.4 = f32[4,96,128]{2,1,0:T(8,128)S(1)} collective-permute-done((f32[4,96,128]{2,1,0:T(8,128)S(1)}, f32[4,96,128]{2,1,0:T(8,128)S(1)}, u32[]{:S(2)}, u32[]{:S(2)}) %collective-permute-start.4) | collective-permute-done | bytes 196640 | tf_op jit(solution)/shard_map/ppermute | solution.py:404
  25.6 0.0 collective-permute-done.5
  25.6 0.0 copy-start.1
  25.6 0.1 collective-permute-start.6
  25.7 0.0 copy-done.4
  25.7 0.0 copy-done.5
  25.7 0.1 copy.35
  25.8 0.7 reshape.52
  26.4 3.8 %front.1 = (bf16[2,256,2048]{2,1,0:T(8,128)(2,1)}, f32[16,2,8,128]{3,2,1,0:T(8,128)}) custom-call(f32[100,2,2048]{2,1,0:T(2,128)} %bitcast.37, s32[2,1,128]{2,1,0:T(1,128)} %bitcast.49), custom_call_target="tpu_custom_call" | custom-call | tf_op jit(solution)/shard_map/front/pallas_call | solution.py:70
  30.2 3.5 %all-to-all-start = ((f32[16,2,8,128]{3,2,1,0:T(8,128)}), f32[16,2,8,128]{3,2,1,0:T(8,128)S(1)}, u32[]{:S(2)}, u32[]{:S(2)}) async-start(f32[16,2,8,128]{3,2,1,0:T(8,128)} %get-tuple-element.45), calls=%async_computation | async-start | bytes 262144 | tf_op jit(solution)/shard_map/all_to_all | solution.py:605
  33.7 6.0 %select.7 = (s32[2,16,128]{2,1,0:T(8,128)}, f32[2,128,128]{2,1,0:T(8,128)}, s32[2,16,1024]{2,1,0:T(8,128)}, f32[2,128,1024]{2,1,0:T(8,128)}) custom-call(s32[2,16,2048]{2,1,0:T(8,128)} %bitcast.41, s32[2,16,2048]{2,1,0:T(8,128)} %bitcast.42, bf16[2,256,2048]{2,1,0:T(8,128)(2,1)} %get-tuple-element.42.table_ref, s32[2,1,128]{2,1,0:T(1,128)} %bitcast.50, ...), custom_call_target="tpu_custom_call" | custom-call | tf_op jit(solution)/shard_map/select/pallas_call | solution.py:122
  39.8 0.0 copy-done.1
  39.8 2.3 %all-to-all-done.arrived_ref = f32[16,2,8,128]{3,2,1,0:T(8,128)S(1)} async-done(((f32[16,2,8,128]{3,2,1,0:T(8,128)}), f32[16,2,8,128]{3,2,1,0:T(8,128)S(1)}, u32[]{:S(2)}, u32[]{:S(2)}) %all-to-all-start) | async-done | bytes 131104 | tf_op jit(solution)/shard_map/all_to_all | solution.py:605
  42.0 0.0 copy-start
  42.0 0.7 copy-done
  42.7 4.1 %mean_sent.1 = f32[16,2,8,128]{3,2,1,0:T(8,128)} custom-call(s32[2,16,128]{2,1,0:T(8,128)} %get-tuple-element.46.slot_ref, f32[2,128,128]{2,1,0:T(8,128)} %get-tuple-element.47.own_ref, bf16[2,256,2048]{2,1,0:T(8,128)(2,1)} %get-tuple-element.42.table_ref, f32[16,2,8,128]{3,2,1,0:T(8,128)} %copy-done), custom_call_target="tpu_custom_call" | custom-call | tf_op jit(solution)/shard_map/mean_sent/pallas_call | solution.py:195
  46.8 4.6 %all-to-all-start.1 = ((f32[16,2,8,128]{3,2,1,0:T(8,128)}), f32[16,2,8,128]{3,2,1,0:T(8,128)S(1)}, u32[]{:S(2)}, u32[]{:S(2)}) async-start(f32[16,2,8,128]{3,2,1,0:T(8,128)} %mean_sent.1), calls=%async_computation.1 | async-start | bytes 262144 | tf_op jit(solution)/shard_map/all_to_all | solution.py:605
  51.4 6.1 %mean_ends.2.refs_0_ = f32[128,1024]{1,0:T(8,128)} custom-call(s32[2,16,1024]{2,1,0:T(8,128)} %get-tuple-element.43.slot_ref, f32[2,128,1024]{2,1,0:T(8,128)} %get-tuple-element.44.own_ref, bf16[2,256,2048]{2,1,0:T(8,128)(2,1)} %get-tuple-element.42.table_ref, f32[16,2,8,128]{3,2,1,0:T(8,128)} %copy-done), custom_call_target="tpu_custom_call" | custom-call | tf_op jit(solution)/shard_map/mean_ends/pallas_call | solution.py:222
  57.5 6.0 %mean_ends.3.refs_1_ = f32[128,1024]{1,0:T(8,128)} custom-call(s32[2,16,1024]{2,1,0:T(8,128)} %get-tuple-element.43.slot_ref, f32[2,128,1024]{2,1,0:T(8,128)} %get-tuple-element.44.own_ref, bf16[2,256,2048]{2,1,0:T(8,128)(2,1)} %get-tuple-element.42.table_ref, f32[16,2,8,128]{3,2,1,0:T(8,128)} %copy-done), custom_call_target="tpu_custom_call" | custom-call | tf_op jit(solution)/shard_map/mean_ends/pallas_call | solution.py:222
  63.5 0.0 all-to-all-done.1.refs_4_
  63.5 0.0 copy-start.3
  63.5 0.0 collective-permute-done.6.refs_6_
  63.5 0.0 copy-start.2
  63.5 0.6 copy-done.3
  64.1 0.3 copy-done.2
  64.4 26.2 %layers.1 = (f32[16,96,128]{2,1,0:T(8,128)}, f32[16,96,128]{2,1,0:T(8,128)}, f32[8,128]{1,0:T(8,128)}) custom-call(f32[128,1024]{1,0:T(8,128)} %mean_ends.2.refs_0_, f32[128,1024]{1,0:T(8,128)} %mean_ends.3.refs_1_, s32[2,2,256]{2,1,0:T(2,128)} %bitcast.46, s32[2,2,256]{2,1,0:T(2,128)} %bitcast.48, f32[16,2,8,128]{3,2,1,0:T(8,128)} %copy-done.3, ...), custom_call_target="tpu_custom_call" | custom-call | tf_op jit(solution)/shard_map/layers/pallas_call | solution.py:377
  90.6 0.0 collective-permute-start.7
  90.6 2.5 %collective-permute-done.7 = f32[16,96,128]{2,1,0:T(8,128)S(1)} collective-permute-done((f32[16,96,128]{2,1,0:T(8,128)}, f32[16,96,128]{2,1,0:T(8,128)S(1)}, u32[]{:S(2)}, u32[]{:S(2)}) %collective-permute-start.7) | collective-permute-done | bytes 786464 | tf_op jit(solution)/shard_map/ppermute | solution.py:408
  93.1 1.2 add.25
  94.4 2.9 %collective-permute-start.10 = (f32[4,96,128]{2,1,0:T(8,128)S(1)}, f32[4,96,128]{2,1,0:T(8,128)S(1)}, u32[]{:S(2)}, u32[]{:S(2)}) collective-permute-start(f32[4,96,128]{2,1,0:T(8,128)S(1)} %get-tuple-element.72), channel_id=1, source_target_pairs={{0,6},{2,4},{4,2},{6,0},{8,14},{10,12},{12,10},{14,8},{16,22},{18,... | collective-permute-start | bytes 589832 | tf_op jit(solution)/shard_map/ppermute | solution.py:404
  97.3 0.6 collective-permute-start.9
  97.8 0.1 collective-permute-start.8
  97.9 5.2 %collective-permute-done.10 = f32[4,96,128]{2,1,0:T(8,128)S(1)} collective-permute-done((f32[4,96,128]{2,1,0:T(8,128)S(1)}, f32[4,96,128]{2,1,0:T(8,128)S(1)}, u32[]{:S(2)}, u32[]{:S(2)}) %collective-permute-start.10) | collective-permute-done | bytes 196640 | tf_op jit(solution)/shard_map/ppermute | solution.py:404
  103.2 3.5 %collective-permute-done.9 = f32[4,96,128]{2,1,0:T(8,128)S(1)} collective-permute-done((f32[4,96,128]{2,1,0:T(8,128)S(1)}, f32[4,96,128]{2,1,0:T(8,128)S(1)}, u32[]{:S(2)}, u32[]{:S(2)}) %collective-permute-start.9) | collective-permute-done | bytes 196640 | tf_op jit(solution)/shard_map/ppermute | solution.py:404
  106.7 0.3 collective-permute-done.8
  107.0 0.1 fusion.1
  107.1 3.3 %collective-permute-start.13 = (f32[1,96,128]{2,1,0:T(8,128)S(1)}, f32[1,96,128]{2,1,0:T(8,128)S(1)}, u32[]{:S(2)}, u32[]{:S(2)}) collective-permute-start(f32[1,96,128]{2,1,0:T(8,128)S(1)} %get-tuple-element.75), channel_id=1, source_target_pairs={{0,24},{2,26},{4,28},{6,30},{8,16},{10,18},{12,20},{14,22},{16,8},... | collective-permute-start | bytes 147464 | tf_op jit(solution)/shard_map/ppermute | solution.py:404
  110.4 0.0 collective-permute-start.12
  110.4 1.1 collective-permute-start.11
  111.5 1.8 %collective-permute-done.13 = f32[1,96,128]{2,1,0:T(8,128)S(1)} collective-permute-done((f32[1,96,128]{2,1,0:T(8,128)S(1)}, f32[1,96,128]{2,1,0:T(8,128)S(1)}, u32[]{:S(2)}, u32[]{:S(2)}) %collective-permute-start.13) | collective-permute-done | bytes 49184 | tf_op jit(solution)/shard_map/ppermute | solution.py:404
  113.4 2.0 %collective-permute-done.12 = f32[1,96,128]{2,1,0:T(8,128)S(1)} collective-permute-done((f32[1,96,128]{2,1,0:T(8,128)S(1)}, f32[1,96,128]{2,1,0:T(8,128)S(1)}, u32[]{:S(2)}, u32[]{:S(2)}) %collective-permute-start.12) | collective-permute-done | bytes 49184 | tf_op jit(solution)/shard_map/ppermute | solution.py:404
  115.4 0.0 collective-permute-done.11
  115.4 0.6 fusion.4.g_ref
  116.0 2.0 %stats.1 = (f32[64,100]{1,0:T(8,128)}, f32[47,64]{1,0:T(8,128)}, f32[1,64]{1,0:T(1,128)}, f32[1,64]{1,0:T(1,128)}, f32[1,64]{1,0:T(1,128)}, /*index=5*/f32[1,64]...) custom-call(f32[96,128]{1,0:T(8,128)} %fusion.4.g_ref, f32[8,128]{1,0:T(8,128)} %get-tuple-element.50.stats_ref, ...), custom_call_target="tpu_custom_call" | custom-call | tf_op jit(solution)/shard_map/stats/pallas_call | solution.py:636
  118.0 11.1 %all_to_all.15.refs_0_ = f32[32,4,128]{2,1,0:T(4,128)} all-to-all(f32[32,4,128]{2,1,0:T(4,128)} %get-tuple-element.51), channel_id=1, replica_groups=mesh['dom'=16,'rep'=2] {'dom','rep'}, dimensions={0} | all-to-all | bytes 131072 | tf_op jit(solution)/shard_map/all_to_all | solution.py:644
  129.0 2.0 %update.1 = (f32[1,1]{1,0:T(1,128)}, f32[64,100]{1,0:T(8,128)}, f32[1,100]{1,0:T(1,128)}, f32[47,64]{1,0:T(8,128)}, f32[1,47]{1,0:T(1,128)}, /*index=5*/f32[1,64...) custom-call(f32[32,4,128]{2,1,0:T(4,128)} %all_to_all.15.refs_0_, f32[64,128]{1,0:T(8,128)} %get-tuple-element.52.refs_1_, ...), custom_call_target="tpu_custom_call" | custom-call | tf_op jit(solution)/shard_map/update/pallas_call | solution.py:646
  (11 shorter events, 0.1 us)
Async XLA Ops:
  0.6 25.0 %copy-start.4 = (s32[2,16,8]{1,2,0:T(8,128)S(1)}, s32[2,16,8]{1,2,0:T(8,128)}, u32[]{:S(2)}) copy-start(s32[2,16,8]{1,2,0:T(8,128)} %param.20) | copy-start | bytes 3076
  0.7 25.0 %copy-start.5 = (s32[2,16]{1,0:T(2,128)S(1)}, s32[2,16]{1,0:T(2,128)}, u32[]{:S(2)}) copy-start(s32[2,16]{1,0:T(2,128)} %param.21) | copy-start | bytes 388
  3.2 5.7 %collective-permute-start = (f32[1,96,128]{2,1,0:T(8,128)S(1)}, f32[1,96,128]{2,1,0:T(8,128)S(1)}, u32[]{:S(2)}, u32[]{:S(2)}) collective-permute-start(f32[1,96,128]{2,1,0:T(8,128)S(1)} %get-tuple-element.70), channel_id=1, source_target_pairs={{0,8},{2,10},{4,12},{6,14},{8,0},{10,2},{12,4},{14,6},{16,24},{18,... | collective-permute-start | bytes 147464 | tf_op jit(solution)/shard_map/ppermute | solution.py:404
  6.2 5.9 %collective-permute-start.1 = (f32[1,96,128]{2,1,0:T(8,128)S(1)}, f32[1,96,128]{2,1,0:T(8,128)S(1)}, u32[]{:S(2)}, u32[]{:S(2)}) collective-permute-start(f32[1,96,128]{2,1,0:T(8,128)S(1)} %get-tuple-element.70), channel_id=1, source_target_pairs={{0,16},{2,18},{4,20},{6,22},{8,24},{10,26},{12,28},{14,30},{16,0},... | collective-permute-start | bytes 147464 | tf_op jit(solution)/shard_map/ppermute | solution.py:404
  8.8 5.9 %collective-permute-start.2 = (f32[1,96,128]{2,1,0:T(8,128)S(1)}, f32[1,96,128]{2,1,0:T(8,128)S(1)}, u32[]{:S(2)}, u32[]{:S(2)}) collective-permute-start(f32[1,96,128]{2,1,0:T(8,128)S(1)} %get-tuple-element.70), channel_id=1, source_target_pairs={{0,24},{2,26},{4,28},{6,30},{8,16},{10,18},{12,20},{14,22},{16,8},... | collective-permute-start | bytes 147464 | tf_op jit(solution)/shard_map/ppermute | solution.py:404
  14.7 7.5 %collective-permute-start.3 = (f32[4,96,128]{2,1,0:T(8,128)S(1)}, f32[4,96,128]{2,1,0:T(8,128)S(1)}, u32[]{:S(2)}, u32[]{:S(2)}) collective-permute-start(f32[4,96,128]{2,1,0:T(8,128)S(1)} %pad_maximum_fusion), channel_id=1, source_target_pairs={{0,2},{2,0},{4,6},{6,4},{8,10},{10,8},{12,14},{14,12},{16,18},{18,... | collective-permute-start | bytes 589832 | tf_op jit(solution)/shard_map/ppermute | solution.py:404
  16.3 9.3 %collective-permute-start.4 = (f32[4,96,128]{2,1,0:T(8,128)S(1)}, f32[4,96,128]{2,1,0:T(8,128)S(1)}, u32[]{:S(2)}, u32[]{:S(2)}) collective-permute-start(f32[4,96,128]{2,1,0:T(8,128)S(1)} %pad_maximum_fusion), channel_id=1, source_target_pairs={{0,4},{2,6},{4,0},{6,2},{8,12},{10,14},{12,8},{14,10},{16,20},{18,... | collective-permute-start | bytes 589832 | tf_op jit(solution)/shard_map/ppermute | solution.py:404
  17.8 7.8 %collective-permute-start.5 = (f32[4,96,128]{2,1,0:T(8,128)S(1)}, f32[4,96,128]{2,1,0:T(8,128)S(1)}, u32[]{:S(2)}, u32[]{:S(2)}) collective-permute-start(f32[4,96,128]{2,1,0:T(8,128)S(1)} %pad_maximum_fusion), channel_id=1, source_target_pairs={{0,6},{2,4},{4,2},{6,0},{8,14},{10,12},{12,10},{14,8},{16,22},{18,... | collective-permute-start | bytes 589832 | tf_op jit(solution)/shard_map/ppermute | solution.py:404
  25.6 14.2 %copy-start.1 = (f32[16,96,128]{2,1,0:T(8,128)}, f32[16,96,128]{2,1,0:T(8,128)S(1)}, u32[]{:S(2)}) copy-start(f32[16,96,128]{2,1,0:T(8,128)S(1)} %constant_dynamic-update-slice_fusion.refs_5_) | copy-start | bytes 2359300
  25.6 37.9 %collective-permute-start.6 = (f32[16,96,128]{2,1,0:T(8,128)S(1)}, f32[16,96,128]{2,1,0:T(8,128)S(1)}, u32[]{:S(2)}, u32[]{:S(2)}) collective-permute-start(f32[16,96,128]{2,1,0:T(8,128)S(1)} %constant_dynamic-update-slice_fusion.refs_5_), channel_id=1, source_target_pairs={{0,1},{1,0},{2,3},{3,2},{4,5},{5,4},{6,7},{7,6},{8,9},{9,8},{10,11... | collective-permute-start | bytes 2359304 | tf_op jit(solution)/shard_map/ppermute | solution.py:408
  30.2 11.8 %all-to-all-start = ((f32[16,2,8,128]{3,2,1,0:T(8,128)}), f32[16,2,8,128]{3,2,1,0:T(8,128)S(1)}, u32[]{:S(2)}, u32[]{:S(2)}) async-start(f32[16,2,8,128]{3,2,1,0:T(8,128)} %get-tuple-element.45), calls=%async_computation | async-start | bytes 262144 | tf_op jit(solution)/shard_map/all_to_all | solution.py:605
  42.0 0.7 copy-start
  46.8 16.7 %all-to-all-start.1 = ((f32[16,2,8,128]{3,2,1,0:T(8,128)}), f32[16,2,8,128]{3,2,1,0:T(8,128)S(1)}, u32[]{:S(2)}, u32[]{:S(2)}) async-start(f32[16,2,8,128]{3,2,1,0:T(8,128)} %mean_sent.1), calls=%async_computation.1 | async-start | bytes 262144 | tf_op jit(solution)/shard_map/all_to_all | solution.py:605
  63.5 0.6 copy-start.3
  63.5 0.9 copy-start.2
  90.6 2.5 %collective-permute-start.7 = (f32[16,96,128]{2,1,0:T(8,128)}, f32[16,96,128]{2,1,0:T(8,128)S(1)}, u32[]{:S(2)}, u32[]{:S(2)}) collective-permute-start(f32[16,96,128]{2,1,0:T(8,128)} %get-tuple-element.49), channel_id=1, source_target_pairs={{0,1},{1,0},{2,3},{3,2},{4,5},{5,4},{6,7},{7,6},{8,9},{9,8},{10,11... | collective-permute-start | bytes 2359304 | tf_op jit(solution)/shard_map/ppermute | solution.py:408
  94.4 8.8 %collective-permute-start.10 = (f32[4,96,128]{2,1,0:T(8,128)S(1)}, f32[4,96,128]{2,1,0:T(8,128)S(1)}, u32[]{:S(2)}, u32[]{:S(2)}) collective-permute-start(f32[4,96,128]{2,1,0:T(8,128)S(1)} %get-tuple-element.72), channel_id=1, source_target_pairs={{0,6},{2,4},{4,2},{6,0},{8,14},{10,12},{12,10},{14,8},{16,22},{18,... | collective-permute-start | bytes 589832 | tf_op jit(solution)/shard_map/ppermute | solution.py:404
  97.3 9.4 %collective-permute-start.9 = (f32[4,96,128]{2,1,0:T(8,128)S(1)}, f32[4,96,128]{2,1,0:T(8,128)S(1)}, u32[]{:S(2)}, u32[]{:S(2)}) collective-permute-start(f32[4,96,128]{2,1,0:T(8,128)S(1)} %get-tuple-element.73), channel_id=1, source_target_pairs={{0,4},{2,6},{4,0},{6,2},{8,12},{10,14},{12,8},{14,10},{16,20},{18,... | collective-permute-start | bytes 589832 | tf_op jit(solution)/shard_map/ppermute | solution.py:404
  97.8 9.2 %collective-permute-start.8 = (f32[4,96,128]{2,1,0:T(8,128)S(1)}, f32[4,96,128]{2,1,0:T(8,128)S(1)}, u32[]{:S(2)}, u32[]{:S(2)}) collective-permute-start(f32[4,96,128]{2,1,0:T(8,128)S(1)} %get-tuple-element.71), channel_id=1, source_target_pairs={{0,2},{2,0},{4,6},{6,4},{8,10},{10,8},{12,14},{14,12},{16,18},{18,... | collective-permute-start | bytes 589832 | tf_op jit(solution)/shard_map/ppermute | solution.py:404
  107.1 6.3 %collective-permute-start.13 = (f32[1,96,128]{2,1,0:T(8,128)S(1)}, f32[1,96,128]{2,1,0:T(8,128)S(1)}, u32[]{:S(2)}, u32[]{:S(2)}) collective-permute-start(f32[1,96,128]{2,1,0:T(8,128)S(1)} %get-tuple-element.75), channel_id=1, source_target_pairs={{0,24},{2,26},{4,28},{6,30},{8,16},{10,18},{12,20},{14,22},{16,8},... | collective-permute-start | bytes 147464 | tf_op jit(solution)/shard_map/ppermute | solution.py:404
  110.4 5.0 %collective-permute-start.12 = (f32[1,96,128]{2,1,0:T(8,128)S(1)}, f32[1,96,128]{2,1,0:T(8,128)S(1)}, u32[]{:S(2)}, u32[]{:S(2)}) collective-permute-start(f32[1,96,128]{2,1,0:T(8,128)S(1)} %get-tuple-element.76), channel_id=1, source_target_pairs={{0,16},{2,18},{4,20},{6,22},{8,24},{10,26},{12,28},{14,30},{16,0},... | collective-permute-start | bytes 147464 | tf_op jit(solution)/shard_map/ppermute | solution.py:404
  110.4 5.0 %collective-permute-start.11 = (f32[1,96,128]{2,1,0:T(8,128)S(1)}, f32[1,96,128]{2,1,0:T(8,128)S(1)}, u32[]{:S(2)}, u32[]{:S(2)}) collective-permute-start(f32[1,96,128]{2,1,0:T(8,128)S(1)} %get-tuple-element.74), channel_id=1, source_target_pairs={{0,8},{2,10},{4,12},{6,14},{8,0},{10,2},{12,4},{14,6},{16,24},{18,... | collective-permute-start | bytes 147464 | tf_op jit(solution)/shard_map/ppermute | solution.py:404
